TPU v7x, 32 devices: a whole 2x2x4 slice. The times are simulated.
32 devices in a mesh: chain: 16 (over z, y, x), grp: 2 (over core).
Axes of the slice: x: 2, y: 2, z: 4, core: 2. Of those that a mesh axis runs over, the one named last changes fastest.
Arguments:
- right_side: float32 [32, 64, 1024], P(('chain', 'grp')), may hold values from -6 to 6
- start: float32 [32, 64, 1024], P(('chain', 'grp')), may hold values from -3 to 3
- diag_tiles: float32 [32, 1024, 1024], P(('chain', 'grp')), may hold values from -0.12 to 2.92, as said below
- neighbour_tiles: float32 [32, 1024, 1024], P(('chain', 'grp')), may hold values from -0.0234375 to 0.0234375
- factors: float32 [32, 28, 96, 1024], P(('chain', 'grp')), may hold values from -0.078125 to 0.078125
- partner: int32 [32, 28], P(('chain', 'grp')), may hold values from -1 to 31, as said below
- ranks: int32 [32, 28], P(('chain', 'grp')), may hold values from 0 to 96, as said below
Outputs:
- solution: float32 [32, 64, 1024], P(('chain', 'grp'))
- residual: float32 [32, 64, 1024], P(('chain', 'grp'))
Inputs may be any that keep to these rules, and one draw needn't show every extreme that they name: If partner[i, s] = j >= 0 then j is not i, i - 1 or i + 1, partner[j, s] = i and ranks[j, s] = ranks[i, s]; no two slots of one cluster name the same partner; cluster 0 and cluster 32 - 1 are a far pair. ranks is 0 exactly at empty slots and from 32 to 96 elsewhere; every pair of cluster 0 has rank 96. `diag_tiles`: every tile is symmetric.
All inputs are finite; a program needn't handle non-finite values.
Results may differ from a plain program's by a relative error of at most 0.00017.
Values sent between devices are 32-bit elements; how exact they have to be, the bound alone decides.
No kernel may reach another device: no remote copies, remote signals or barrier semaphores. Data moves between devices by JAX's collectives and lax.ppermute only.
A program may use at most 128 MiB of HBM per device.

v0:
```python
import functools

import jax
import jax.numpy as jnp
from jax import lax
from jax.experimental import pallas as pl
from jax.experimental.pallas import tpu as pltpu
from jax.sharding import PartitionSpec as P


ITERS = 2

spectrum_low = 0.7
spectrum_high = 3.6

AXES = ("chain", "grp")
NT = (((1,), (1,)), ((), ()))
NN = (((1,), (0,)), ((), ()))
TN = (((0,), (0,)), ((), ()))
VMEM_LIMIT = 40 * 1024 * 1024
STEPS = 4


def from_behind(block, distance):
    devices = range(lax.axis_size(AXES))
    route = [(i - distance, i) for i in devices if i - distance in devices]
    return lax.ppermute(block, AXES, route)


def halves(value):
    high = value.astype(jnp.bfloat16)
    low = (value - high.astype(jnp.float32)).astype(jnp.bfloat16)
    return high, low


def product(left, right, form):
    return lax.dot_general(left, right, form, preferred_element_type=jnp.float32)


class Loader:
    def __init__(self, factors_ref, buffer, semaphore, high_ref=None, low_ref=None):
        self.factors_ref, self.buffer, self.semaphore = factors_ref, buffer, semaphore
        self.high_ref, self.low_ref = high_ref, low_ref
        self.width = factors_ref.shape[1]
        slots = factors_ref.shape[0]
        size = -(-slots // STEPS)
        self.groups = [(at, min(size, slots - at)) for at in range(0, slots, size)]

    def copy(self, index):
        at, size = self.groups[index]
        return pltpu.make_async_copy(
            self.factors_ref.at[at:at + size], self.buffer.at[at:at + size],
            self.semaphore.at[index],
        )

    def start(self):
        for index in range(len(self.groups)):
            self.copy(index).start()

    def rows(self, at, size):
        return slice(at * self.width, (at + size) * self.width)

    def parts(self):
        for index, (at, size) in enumerate(self.groups):
            self.copy(index).wait()
            rows = self.buffer[at:at + size].reshape(size * self.width, self.buffer.shape[2])
            high, low = halves(rows)
            if self.high_ref is not None:
                self.high_ref[self.rows(at, size), :] = high
                self.low_ref[self.rows(at, size), :] = low
            yield at, size, high, low

    def kept(self):
        for at, size in self.groups:
            rows = self.rows(at, size)
            yield at, size, self.high_ref[rows, :], self.low_ref[rows, :]


def project(parts, width, vectors, partner_ref, ranks_ref, outgoing_ref):
    high, low = halves(vectors)
    operand = jnp.concatenate([high, low], axis=0)
    lanes = operand.shape[0]
    half = width // 2
    left = lax.broadcasted_iota(jnp.int32, (half, lanes), 1) < lanes // 2
    rank_index = lax.broadcasted_iota(jnp.int32, (half, lanes), 0) + jnp.where(left, 0, half)
    for at, size, factor_high, factor_low in parts:
        rows = product(factor_high, operand, NT) + product(factor_low, operand, NT)
        rows = rows + pltpu.roll(rows, lanes // 2, 1)
        for inner in range(size):
            base = inner * width
            chunk = jnp.where(left, rows[base:base + half], rows[base + half:base + width])
            slot = at + inner
            chunk = jnp.where(rank_index < ranks_ref[slot], chunk, 0.0)
            place = partner_ref[slot]

            @pl.when(place >= 0)
            def _():
                outgoing_ref[place] = chunk


def unpack(width, slots, partner_ref, incoming_ref, received_ref):
    _, half, lanes = incoming_ref.shape
    n = lanes // 2
    left = lax.broadcasted_iota(jnp.int32, (half, lanes), 1) < n
    for slot in range(slots):
        place = partner_ref[slot]
        chunk = jnp.where(place >= 0, incoming_ref[jnp.maximum(place, 0)], 0.0)
        high = chunk.astype(jnp.bfloat16).astype(jnp.float32)
        low = chunk - high
        top = jnp.where(left, high, pltpu.roll(low, n, 1))
        bottom = jnp.where(left, pltpu.roll(high, n, 1), low)
        base = slot * width
        received_ref[base:base + half, :] = top.astype(jnp.bfloat16)
        received_ref[base + half:base + width, :] = bottom.astype(jnp.bfloat16)


def far(loader, received_ref):
    total = None
    for at, size, factor_high, factor_low in loader.parts():
        left = received_ref[loader.rows(at, size), :]
        term = product(left, factor_high, TN) + product(left, factor_low, TN)
        total = term if total is None else total + term
    n = total.shape[0] // 2
    return total[:n] + total[n:]


def project_kernel(partner_ref, ranks_ref, factors_ref, vectors_ref, outgoing_ref,
                   buffer, semaphore):
    loader = Loader(factors_ref, buffer, semaphore)
    loader.start()
    project(loader.parts(), loader.width, vectors_ref[...], partner_ref, ranks_ref, outgoing_ref)


def far_kernel(partner_ref, factors_ref, incoming_ref, base_ref, out_ref, buffer,
               semaphore, received_ref):
    loader = Loader(factors_ref, buffer, semaphore)
    loader.start()
    unpack(loader.width, factors_ref.shape[0], partner_ref, incoming_ref, received_ref)
    out_ref[...] = base_ref[...] - far(loader, received_ref)


def turn_kernel(weights, partner_ref, ranks_ref, factors_ref, incoming_ref,
                base_ref, previous_ref, residual_ref, direction_ref, outgoing_ref, buffer,
                semaphore, received_ref, high_ref, low_ref):
    loader = Loader(factors_ref, buffer, semaphore, high_ref, low_ref)
    loader.start()
    unpack(loader.width, factors_ref.shape[0], partner_ref, incoming_ref, received_ref)
    residual = base_ref[...] - far(loader, received_ref)
    residual_ref[...] = residual
    old, new = weights
    direction = new * residual if old is None else old * previous_ref[...] + new * residual
    direction_ref[...] = direction
    project(loader.kept(), loader.width, direction, partner_ref, ranks_ref, outgoing_ref)


SMEM_SPEC = pl.BlockSpec(memory_space=pltpu.SMEM)
VMEM_SPEC = pl.BlockSpec(memory_space=pltpu.VMEM)
ANY_SPEC = pl.BlockSpec(memory_space=pltpu.HBM)


def body(right_side, start, diag_tiles, neighbour_tiles, factors, partner, ranks):
    device_count = lax.axis_size(AXES)
    right_side, start = right_side[0], start[0]
    diag_block, neighbour_block, factor_block = diag_tiles[0], neighbour_tiles[0], factors[0]
    partner, ranks = partner[0], ranks[0]
    factor_block = pltpu.with_memory_space_constraint(factor_block, pltpu.HBM)
    slots, rank_width, points = factor_block.shape
    n = start.shape[0]
    rows = slots * rank_width
    block = jax.ShapeDtypeStruct((n, points), jnp.float32)
    chunks = jax.ShapeDtypeStruct((device_count, rank_width // 2, 2 * n), jnp.float32)
    loading = [
        pltpu.VMEM((slots, rank_width, points), jnp.float32),
        pltpu.SemaphoreType.DMA((STEPS,)),
    ]
    received = pltpu.VMEM((rows, 2 * n), jnp.bfloat16)
    split = [pltpu.VMEM((rows, points), jnp.bfloat16)] * 2
    params = pltpu.CompilerParams(vmem_limit_bytes=VMEM_LIMIT)

    def cost(times):
        return pl.CostEstimate(
            flops=times * 8 * rows * points * n, bytes_accessed=4 * rows * points,
            transcendentals=0,
        )

    def projected(vectors):
        return pl.pallas_call(
            project_kernel,
            out_shape=chunks,
            in_specs=[SMEM_SPEC, SMEM_SPEC, ANY_SPEC, VMEM_SPEC],
            out_specs=VMEM_SPEC,
            scratch_shapes=loading,
            compiler_params=params,
            cost_estimate=cost(1),
            name="project",
        )(partner, ranks, factor_block, vectors)

    def without_far(incoming, base):
        return pl.pallas_call(
            far_kernel,
            out_shape=block,
            in_specs=[SMEM_SPEC, ANY_SPEC, VMEM_SPEC, VMEM_SPEC],
            out_specs=VMEM_SPEC,
            scratch_shapes=loading + [received],
            compiler_params=params,
            cost_estimate=cost(1),
            name="far",
        )(partner, factor_block, incoming, base)

    def turn(weights, incoming, base, previous):
        return pl.pallas_call(
            functools.partial(turn_kernel, weights),
            out_shape=(block, block, chunks),
            in_specs=[SMEM_SPEC, SMEM_SPEC, ANY_SPEC] + [VMEM_SPEC] * 3,
            out_specs=(VMEM_SPEC,) * 3,
            scratch_shapes=loading + [received] + split,
            compiler_params=params,
            cost_estimate=cost(2),
            name="turn",
        )(partner, ranks, factor_block, incoming, base, previous)

    def finish(outgoing, vectors, before, weights):
        incoming = lax.all_to_all(outgoing, AXES, split_axis=0, concat_axis=0, tiled=True)
        exact = lax.Precision.HIGH
        following = from_behind(vectors, -1)
        carried = lax.dot_general(vectors, neighbour_block, NN, precision=exact)
        lower_term = from_behind(carried, 1)
        local_term = lax.dot_general(vectors, diag_block, NT, precision=exact)
        upper_term = lax.dot_general(following, neighbour_block, NT, precision=exact)
        base = before - (local_term + upper_term + lower_term)
        if weights is None:
            return without_far(incoming, base)
        return turn(weights, incoming, base, vectors)

    center = (spectrum_low + spectrum_high) / 2.0
    half_width = (spectrum_high - spectrum_low) / 2.0
    ratio = center / half_width
    rho_now = 1.0 / ratio
    solution = start
    outgoing = projected(start)
    residual, direction, outgoing = finish(outgoing, start, right_side, (None, 1.0 / center))
    for iteration in range(ITERS):
        solution = solution + direction
        if iteration + 1 < ITERS:
            rho_next = 1.0 / (2.0 * ratio - rho_now)
            weights = (rho_next * rho_now, 2.0 * rho_next / half_width)
            residual, direction, outgoing = finish(outgoing, direction, residual, weights)
            rho_now = rho_next
        else:
            residual = finish(outgoing, direction, residual, None)
    return (solution[None], residual[None])


def solution(mesh):
    return jax.shard_map(
        body,
        mesh=mesh,
        in_specs=(
            P(AXES, None, None),
            P(AXES, None, None),
            P(AXES, None, None),
            P(AXES, None, None),
            P(AXES, None, None, None),
            P(AXES, None),
            P(AXES, None),
        ),
        out_specs=(P(AXES, None, None), P(AXES, None, None)),
        check_vma=False,
    )
```

profile of v0, /device:TPU:15, one launch (start us, length us, event | category | flops | bytes accessed | tf_op | source)
XLA Modules:
  0.0 134.4 jit_solution(13610077486430923470)
XLA Ops:
  0.6 0.9 copy-done
  1.6 0.7 copy-done.2
  2.2 0.7 copy-done.4
  2.9 9.9 %project.1 = f32[32,48,128]{2,1,0:T(8,128)} custom-call(s32[28]{0:T(128)S(1)} %bitcast.54, s32[28]{0:T(128)S(1)} %bitcast.58, f32[28,96,1024]{2,1,0:T(8,128)} %bitcast.61, f32[64,1024]{1,0:T(8,128)S(1)} %bitcast.51), custom_call_target="tpu_custom_call" | custom-call | flops 1409286144 | bytes 11010048 | tf_op jit(solution)/shard_map/project/pallas_call | solution.py:187
  12.8 6.2 %all-to-all-start = ((f32[32,48,128]{2,1,0:T(8,128)}), f32[32,48,128]{2,1,0:T(8,128)S(1)}, u32[]{:S(2)}, u32[]{:S(2)}) async-start(f32[32,48,128]{2,1,0:T(8,128)} %project.1), calls=%async_computation | async-start | bytes 1572864 | tf_op jit(solution)/shard_map/all_to_all | solution.py:223
  19.1 0.0 copy-start.6
  19.1 2.6 %collective-permute-start = (f32[64,1024]{1,0:T(8,128)S(1)}, f32[64,1024]{1,0:T(8,128)S(1)}, u32[]{:S(2)}, u32[]{:S(2)}) collective-permute-start(f32[64,1024]{1,0:T(8,128)S(1)} %bitcast.52), channel_id=1, source_target_pairs={{1,0},{2,1},{3,2},{4,3},{5,4},{6,5},{7,6},{8,7},{9,8},{10,9},{11,1... | collective-permute-start | bytes 786440 | tf_op jit(solution)/shard_map/ppermute | solution.py:27
  21.7 3.6 %fusion.8 = f32[64,1024]{1,0:T(8,128)S(1)} fusion(f32[1,1024,1024]{2,1,0:T(8,128)} %param.10, f32[1,64,1024]{2,1,0:T(8,128)S(1)} %copy-done.1), kind=kOutput, calls=%fused_computation.8 | convolution fusion | flops 402653184 | bytes 4718592 | tf_op jit(solution)/shard_map/dot_general | solution.py:226
  25.3 5.2 %collective-permute-start.1 = (f32[64,1024]{1,0:T(8,128)S(1)}, f32[64,1024]{1,0:T(8,128)S(1)}, u32[]{:S(2)}, u32[]{:S(2)}) collective-permute-start(f32[64,1024]{1,0:T(8,128)S(1)} %fusion.8), channel_id=1, source_target_pairs={{0,1},{1,2},{2,3},{3,4},{4,5},{5,6},{6,7},{7,8},{8,9},{9,10},{10,1... | collective-permute-start | bytes 786440 | tf_op jit(solution)/shard_map/ppermute | solution.py:27
  30.6 4.2 %fusion.16 = f32[64,1024]{1,0:T(8,128)S(1)} fusion(f32[1,1024,1024]{2,1,0:T(8,128)} %param.9, f32[1,64,1024]{2,1,0:T(8,128)S(1)} %copy-done.1), kind=kOutput, calls=%fused_computation.16 | convolution fusion | flops 402653184 | bytes 4718592 | tf_op jit(solution)/shard_map/dot_general | solution.py:228
  34.8 4.6 %collective-permute-done.1 = f32[64,1024]{1,0:T(8,128)S(1)} collective-permute-done((f32[64,1024]{1,0:T(8,128)S(1)}, f32[64,1024]{1,0:T(8,128)S(1)}, u32[]{:S(2)}, u32[]{:S(2)}) %collective-permute-start.1) | collective-permute-done | bytes 262176 | tf_op jit(solution)/shard_map/ppermute | solution.py:27
  39.4 1.6 %collective-permute-done = f32[64,1024]{1,0:T(8,128)S(1)} collective-permute-done((f32[64,1024]{1,0:T(8,128)S(1)}, f32[64,1024]{1,0:T(8,128)S(1)}, u32[]{:S(2)}, u32[]{:S(2)}) %collective-permute-start) | collective-permute-done | bytes 262176 | tf_op jit(solution)/shard_map/ppermute | solution.py:27
  41.0 2.2 %fusion.30.base_ref = f32[64,1024]{1,0:T(8,128)S(1)} fusion(f32[64,1024]{1,0:T(8,128)S(1)} %collective-permute-done.1, f32[64,1024]{1,0:T(8,128)S(1)} %fusion.16, f32[64,1024]{1,0:T(8,128)S(1)} %collective-permute-done, f32[1,1024,1024]{2,1,0:T(8,128)S(1)} %copy-done.6, f32[1,64,1024]{2,1,0:T(8,128)S(1)} %copy-done.11), kind=kOutput, calls=%fused_computation.22 | convolution fusion | flops 402849792 | bytes 5505024 | tf_op jit(solution)/shard_map/dot_general | solution.py:229
  43.2 13.3 %turn.2 = (f32[64,1024]{1,0:T(8,128)S(1)}, f32[64,1024]{1,0:T(8,128)S(1)}, f32[32,48,128]{2,1,0:T(8,128)}) custom-call(s32[28]{0:T(128)S(1)} %bitcast.55, s32[28]{0:T(128)S(1)} %bitcast.59, f32[28,96,1024]{2,1,0:T(8,128)} %bitcast.62, f32[32,48,128]{2,1,0:T(8,128)S(1)} %all-to-all-done.incoming_ref, f32[64,1024]{1,0:T(8,128)S(1)} %fusion.30.base_ref, ...), custom_call_target="tpu_custom_call" | custom-call | flops 2818572288 | bytes 11010048 | tf_op jit(solution)/shard_map/turn/pallas_call | solution.py:211
  56.5 4.3 %all-to-all-start.1 = ((f32[32,48,128]{2,1,0:T(8,128)}), f32[32,48,128]{2,1,0:T(8,128)S(1)}, u32[]{:S(2)}, u32[]{:S(2)}) async-start(f32[32,48,128]{2,1,0:T(8,128)} %get-tuple-element.9), calls=%async_computation.1 | async-start | bytes 1572864 | tf_op jit(solution)/shard_map/all_to_all | solution.py:223
  60.8 2.7 %collective-permute-start.2 = (f32[64,1024]{1,0:T(8,128)S(1)}, f32[64,1024]{1,0:T(8,128)S(1)}, u32[]{:S(2)}, u32[]{:S(2)}) collective-permute-start(f32[64,1024]{1,0:T(8,128)S(1)} %get-tuple-element.8.previous_ref), channel_id=1, source_target_pairs={{1,0},{2,1},{3,2},{4,3},{5,4},{6,5},{7,6},{8,7},{9,8},{10,9},{11,1... | collective-permute-start | bytes 786440 | tf_op jit(solution)/shard_map/ppermute | solution.py:27
  63.5 3.6 %fusion.4 = f32[64,1024]{1,0:T(8,128)S(1)} fusion(f32[64,1024]{1,0:T(8,128)S(1)} %get-tuple-element.8.previous_ref, f32[1,1024,1024]{2,1,0:T(8,128)} %param.10), kind=kOutput, calls=%fused_computation.4 | convolution fusion | flops 402653184 | bytes 4718592 | tf_op jit(solution)/shard_map/dot_general | solution.py:226
  67.1 5.1 %collective-permute-start.3 = (f32[64,1024]{1,0:T(8,128)S(1)}, f32[64,1024]{1,0:T(8,128)S(1)}, u32[]{:S(2)}, u32[]{:S(2)}) collective-permute-start(f32[64,1024]{1,0:T(8,128)S(1)} %fusion.4), channel_id=1, source_target_pairs={{0,1},{1,2},{2,3},{3,4},{4,5},{5,6},{6,7},{7,8},{8,9},{9,10},{10,1... | collective-permute-start | bytes 786440 | tf_op jit(solution)/shard_map/ppermute | solution.py:27
  72.3 10.4 %collective-permute-done.2 = f32[64,1024]{1,0:T(8,128)S(1)} collective-permute-done((f32[64,1024]{1,0:T(8,128)S(1)}, f32[64,1024]{1,0:T(8,128)S(1)}, u32[]{:S(2)}, u32[]{:S(2)}) %collective-permute-start.2) | collective-permute-done | bytes 262176 | tf_op jit(solution)/shard_map/ppermute | solution.py:27
  82.7 2.0 %fusion.6 = f32[64,1024]{1,0:T(8,128)S(1)} fusion(f32[64,1024]{1,0:T(8,128)S(1)} %collective-permute-done.2, f32[1,1024,1024]{2,1,0:T(8,128)S(1)} %copy-done.7), kind=kOutput, calls=%fused_computation.6 | convolution fusion | flops 402653184 | bytes 4718592 | tf_op jit(solution)/shard_map/dot_general | solution.py:229
  84.7 2.1 %fusion.21 = f32[64,1024]{1,0:T(8,128)S(1)} fusion(f32[64,1024]{1,0:T(8,128)S(1)} %collective-permute-done.3, f32[64,1024]{1,0:T(8,128)S(1)} %fusion.6, f32[64,1024]{1,0:T(8,128)S(1)} %get-tuple-element.8.previous_ref, f32[1,1024,1024]{2,1,0:T(8,128)S(1)} %copy-done.9), kind=kOutput, calls=%fused_computation.19 | convolution fusion | flops 402784256 | bytes 5242880 | tf_op jit(solution)/shard_map/dot_general | solution.py:228
  86.8 13.3 %turn.3 = (f32[64,1024]{1,0:T(8,128)S(1)}, f32[64,1024]{1,0:T(8,128)S(1)}, f32[32,48,128]{2,1,0:T(8,128)}) custom-call(s32[28]{0:T(128)S(1)} %bitcast.56, s32[28]{0:T(128)S(1)} %bitcast.60, f32[28,96,1024]{2,1,0:T(8,128)} %bitcast.63, f32[32,48,128]{2,1,0:T(8,128)S(1)} %all-to-all-done.1.incoming_ref, f32[64,1024]{1,0:T(8,128)S(1)} %sub.10.base_ref, ...), custom_call_target="tpu_custom_call" | custom-call | flops 2818572288 | bytes 11010048 | tf_op jit(solution)/shard_map/turn/pallas_call | solution.py:211
  100.2 3.7 %all-to-all-start.2 = ((f32[32,48,128]{2,1,0:T(8,128)}), f32[32,48,128]{2,1,0:T(8,128)S(1)}, u32[]{:S(2)}, u32[]{:S(2)}) async-start(f32[32,48,128]{2,1,0:T(8,128)} %get-tuple-element.12), calls=%async_computation.2 | async-start | bytes 1572864 | tf_op jit(solution)/shard_map/all_to_all | solution.py:223
  103.8 2.7 %collective-permute-start.4 = (f32[64,1024]{1,0:T(8,128)S(1)}, f32[64,1024]{1,0:T(8,128)S(1)}, u32[]{:S(2)}, u32[]{:S(2)}) collective-permute-start(f32[64,1024]{1,0:T(8,128)S(1)} %get-tuple-element.11), channel_id=1, source_target_pairs={{1,0},{2,1},{3,2},{4,3},{5,4},{6,5},{7,6},{8,7},{9,8},{10,9},{11,1... | collective-permute-start | bytes 786440 | tf_op jit(solution)/shard_map/ppermute | solution.py:27
  106.6 3.6 %fusion = f32[64,1024]{1,0:T(8,128)S(1)} fusion(f32[64,1024]{1,0:T(8,128)S(1)} %get-tuple-element.11, f32[1,1024,1024]{2,1,0:T(8,128)} %param.10), kind=kOutput, calls=%fused_computation | convolution fusion | flops 402653184 | bytes 4718592 | tf_op jit(solution)/shard_map/dot_general | solution.py:226
  110.2 2.0 %fusion.12 = f32[64,1024]{1,0:T(8,128)S(1)} fusion(f32[64,1024]{1,0:T(8,128)S(1)} %get-tuple-element.11, f32[1,1024,1024]{2,1,0:T(8,128)S(1)} %copy-done.10), kind=kOutput, calls=%fused_computation.12 | convolution fusion | flops 402653184 | bytes 4718592 | tf_op jit(solution)/shard_map/dot_general | solution.py:228
  112.2 5.2 %collective-permute-start.5 = (f32[64,1024]{1,0:T(8,128)S(1)}, f32[64,1024]{1,0:T(8,128)S(1)}, u32[]{:S(2)}, u32[]{:S(2)}) collective-permute-start(f32[64,1024]{1,0:T(8,128)S(1)} %fusion), channel_id=1, source_target_pairs={{0,1},{1,2},{2,3},{3,4},{4,5},{5,6},{6,7},{7,8},{8,9},{9,10},{10,1... | collective-permute-start | bytes 786440 | tf_op jit(solution)/shard_map/ppermute | solution.py:27
  117.4 0.8 add_bitcast_fusion
  118.2 7.5 %collective-permute-done.4 = f32[64,1024]{1,0:T(8,128)S(1)} collective-permute-done((f32[64,1024]{1,0:T(8,128)S(1)}, f32[64,1024]{1,0:T(8,128)S(1)}, u32[]{:S(2)}, u32[]{:S(2)}) %collective-permute-start.4) | collective-permute-done | bytes 262176 | tf_op jit(solution)/shard_map/ppermute | solution.py:27
  125.7 2.0 %fusion.2 = f32[64,1024]{1,0:T(8,128)S(1)} fusion(f32[64,1024]{1,0:T(8,128)S(1)} %collective-permute-done.4, f32[1,1024,1024]{2,1,0:T(8,128)S(1)} %copy-done.8), kind=kOutput, calls=%fused_computation.2 | convolution fusion | flops 402653184 | bytes 4718592 | tf_op jit(solution)/shard_map/dot_general | solution.py:229
  127.8 0.1 add_subtract_fusion.base_ref
  127.8 6.4 %far.1 = f32[64,1024]{1,0:T(8,128)} custom-call(s32[28]{0:T(128)S(1)} %bitcast.57, f32[28,96,1024]{2,1,0:T(8,128)} %bitcast.64, f32[32,48,128]{2,1,0:T(8,128)S(1)} %all-to-all-done.2.incoming_ref, f32[64,1024]{1,0:T(8,128)S(1)} %add_subtract_fusion.base_ref), custom_call_target="tpu_custom_call" | custom-call | flops 1409286144 | bytes 11010048 | tf_op jit(solution)/shard_map/far/pallas_call | solution.py:199
  (26 shorter events, 0.1 us)
Async XLA Ops:
  0.6 1.0 copy-start
  1.6 0.7 copy-start.2
  2.2 0.7 copy-start.4
  2.9 16.2 %copy-start.1 = (f32[1,64,1024]{2,1,0:T(8,128)S(1)}, f32[1,64,1024]{2,1,0:T(8,128)}, u32[]{:S(2)}) copy-start(f32[1,64,1024]{2,1,0:T(8,128)} %param.8) | copy-start | bytes 786436
  12.8 30.3 %all-to-all-start = ((f32[32,48,128]{2,1,0:T(8,128)}), f32[32,48,128]{2,1,0:T(8,128)S(1)}, u32[]{:S(2)}, u32[]{:S(2)}) async-start(f32[32,48,128]{2,1,0:T(8,128)} %project.1), calls=%async_computation | async-start | bytes 1572864 | tf_op jit(solution)/shard_map/all_to_all | solution.py:223
  19.1 21.9 %copy-start.6 = (f32[1,1024,1024]{2,1,0:T(8,128)S(1)}, f32[1,1024,1024]{2,1,0:T(8,128)}, u32[]{:S(2)}) copy-start(f32[1,1024,1024]{2,1,0:T(8,128)} %param.10) | copy-start | bytes 12582916
  19.1 21.9 %copy-start.11 = (f32[1,64,1024]{2,1,0:T(8,128)S(1)}, f32[1,64,1024]{2,1,0:T(8,128)}, u32[]{:S(2)}) copy-start(f32[1,64,1024]{2,1,0:T(8,128)} %param.7) | copy-start | bytes 786436
  19.1 21.9 %collective-permute-start = (f32[64,1024]{1,0:T(8,128)S(1)}, f32[64,1024]{1,0:T(8,128)S(1)}, u32[]{:S(2)}, u32[]{:S(2)}) collective-permute-start(f32[64,1024]{1,0:T(8,128)S(1)} %bitcast.52), channel_id=1, source_target_pairs={{1,0},{2,1},{3,2},{4,3},{5,4},{6,5},{7,6},{8,7},{9,8},{10,9},{11,1... | collective-permute-start | bytes 786440 | tf_op jit(solution)/shard_map/ppermute | solution.py:27
  25.3 17.9 %copy-start.3 = (s32[1,28]{1,0:T(1,128)S(1)}, s32[1,28]{1,0:T(1,128)}, u32[]{:S(2)}) copy-start(s32[1,28]{1,0:T(1,128)} %param.12) | copy-start | bytes 340
  25.3 17.9 %copy-start.5 = (s32[1,28]{1,0:T(1,128)S(1)}, s32[1,28]{1,0:T(1,128)}, u32[]{:S(2)}) copy-start(s32[1,28]{1,0:T(1,128)} %param.13) | copy-start | bytes 340
  25.3 14.0 %collective-permute-start.1 = (f32[64,1024]{1,0:T(8,128)S(1)}, f32[64,1024]{1,0:T(8,128)S(1)}, u32[]{:S(2)}, u32[]{:S(2)}) collective-permute-start(f32[64,1024]{1,0:T(8,128)S(1)} %fusion.8), channel_id=1, source_target_pairs={{0,1},{1,2},{2,3},{3,4},{4,5},{5,6},{6,7},{7,8},{8,9},{9,10},{10,1... | collective-permute-start | bytes 786440 | tf_op jit(solution)/shard_map/ppermute | solution.py:27
  56.5 30.3 %all-to-all-start.1 = ((f32[32,48,128]{2,1,0:T(8,128)}), f32[32,48,128]{2,1,0:T(8,128)S(1)}, u32[]{:S(2)}, u32[]{:S(2)}) async-start(f32[32,48,128]{2,1,0:T(8,128)} %get-tuple-element.9), calls=%async_computation.1 | async-start | bytes 1572864 | tf_op jit(solution)/shard_map/all_to_all | solution.py:223
  60.8 21.9 %copy-start.7 = (f32[1,1024,1024]{2,1,0:T(8,128)S(1)}, f32[1,1024,1024]{2,1,0:T(8,128)}, u32[]{:S(2)}) copy-start(f32[1,1024,1024]{2,1,0:T(8,128)} %param.10) | copy-start | bytes 12582916
  60.8 23.9 %copy-start.9 = (f32[1,1024,1024]{2,1,0:T(8,128)S(1)}, f32[1,1024,1024]{2,1,0:T(8,128)}, u32[]{:S(2)}) copy-start(f32[1,1024,1024]{2,1,0:T(8,128)} %param.9) | copy-start | bytes 12582916
  60.8 21.9 %collective-permute-start.2 = (f32[64,1024]{1,0:T(8,128)S(1)}, f32[64,1024]{1,0:T(8,128)S(1)}, u32[]{:S(2)}, u32[]{:S(2)}) collective-permute-start(f32[64,1024]{1,0:T(8,128)S(1)} %get-tuple-element.8.previous_ref), channel_id=1, source_target_pairs={{1,0},{2,1},{3,2},{4,3},{5,4},{6,5},{7,6},{8,7},{9,8},{10,9},{11,1... | collective-permute-start | bytes 786440 | tf_op jit(solution)/shard_map/ppermute | solution.py:27
  67.1 17.6 %collective-permute-start.3 = (f32[64,1024]{1,0:T(8,128)S(1)}, f32[64,1024]{1,0:T(8,128)S(1)}, u32[]{:S(2)}, u32[]{:S(2)}) collective-permute-start(f32[64,1024]{1,0:T(8,128)S(1)} %fusion.4), channel_id=1, source_target_pairs={{0,1},{1,2},{2,3},{3,4},{4,5},{5,6},{6,7},{7,8},{8,9},{9,10},{10,1... | collective-permute-start | bytes 786440 | tf_op jit(solution)/shard_map/ppermute | solution.py:27
  100.2 27.7 %all-to-all-start.2 = ((f32[32,48,128]{2,1,0:T(8,128)}), f32[32,48,128]{2,1,0:T(8,128)S(1)}, u32[]{:S(2)}, u32[]{:S(2)}) async-start(f32[32,48,128]{2,1,0:T(8,128)} %get-tuple-element.12), calls=%async_computation.2 | async-start | bytes 1572864 | tf_op jit(solution)/shard_map/all_to_all | solution.py:223
  103.8 6.4 %copy-start.10 = (f32[1,1024,1024]{2,1,0:T(8,128)S(1)}, f32[1,1024,1024]{2,1,0:T(8,128)}, u32[]{:S(2)}) copy-start(f32[1,1024,1024]{2,1,0:T(8,128)} %param.9) | copy-start | bytes 12582916
  103.8 21.9 %copy-start.8 = (f32[1,1024,1024]{2,1,0:T(8,128)S(1)}, f32[1,1024,1024]{2,1,0:T(8,128)}, u32[]{:S(2)}) copy-start(f32[1,1024,1024]{2,1,0:T(8,128)} %param.10) | copy-start | bytes 12582916
  103.8 21.9 %collective-permute-start.4 = (f32[64,1024]{1,0:T(8,128)S(1)}, f32[64,1024]{1,0:T(8,128)S(1)}, u32[]{:S(2)}, u32[]{:S(2)}) collective-permute-start(f32[64,1024]{1,0:T(8,128)S(1)} %get-tuple-element.11), channel_id=1, source_target_pairs={{1,0},{2,1},{3,2},{4,3},{5,4},{6,5},{7,6},{8,7},{9,8},{10,9},{11,1... | collective-permute-start | bytes 786440 | tf_op jit(solution)/shard_map/ppermute | solution.py:27
  112.2 15.5 %collective-permute-start.5 = (f32[64,1024]{1,0:T(8,128)S(1)}, f32[64,1024]{1,0:T(8,128)S(1)}, u32[]{:S(2)}, u32[]{:S(2)}) collective-permute-start(f32[64,1024]{1,0:T(8,128)S(1)} %fusion), channel_id=1, source_target_pairs={{0,1},{1,2},{2,3},{3,4},{4,5},{5,6},{6,7},{7,8},{8,9},{9,10},{10,1... | collective-permute-start | bytes 786440 | tf_op jit(solution)/shard_map/ppermute | solution.py:27
where the time goes:
time: 135 us; the launch traced here: 134 us
  Pallas kernels  42.9 us (32%)
  starting transfers between devices  37.7 us (28%)
  matrix products  25.4 us (19%)
  waiting for transfers between devices  24.1 us (18%)
  local copies, waits for them, and re-layouts  2.31 us (2%)
    pallas_call x2, Pallas kernels, turn(): pl.pallas_call(functools.partial(turn_kernel, weights), out_shape=(block,...  26.6 us
    ppermute x6, waiting for transfers between devices, from_behind(): return lax.ppermute(block, AXES, route)  24.1 us
    ppermute x6, starting transfers between devices, from_behind(): return lax.ppermute(block, AXES, route)  23.5 us
    all_to_all x3, starting transfers between devices, finish(): lax.all_to_all(outgoing, AXES, split_axis=0, concat_axis=0, tiled=True)  14.2 us
    dot_general x3, matrix products, finish(): carried = lax.dot_general(vectors, neighbour_block, NN, precision=exact)  10.8 us
    pallas_call x1, Pallas kernels, projected(): pl.pallas_call(project_kernel, out_shape=chunks, in_specs=[SMEM_SPEC, SME...  9.93 us
    dot_general x3, matrix products, finish(): local_term = lax.dot_general(vectors, diag_block, NT, precision=exact)  8.32 us
    pallas_call x1, Pallas kernels, without_far(): pl.pallas_call(far_kernel, out_shape=block, in_specs=[SMEM_SPEC, ANY_SPEC...  6.36 us
  transfers between devices with their start and end apart: 9, of which 4 were waited for; matrix products, arithmetic and copies ran while one was open for 20% of the time, Pallas kernels for 0%

commit v1 on v0

v1 whole, which is shorter than its diff:
```python
import functools

import jax
import jax.numpy as jnp
from jax import lax
from jax.experimental import pallas as pl
from jax.experimental.pallas import tpu as pltpu
from jax.sharding import PartitionSpec as P


ITERS = 2

spectrum_low = 0.7
spectrum_high = 3.6

AXES = ("chain", "grp")
NT = (((1,), (1,)), ((), ()))
NN = (((1,), (0,)), ((), ()))
TN = (((0,), (0,)), ((), ()))
VMEM_LIMIT = 40 * 1024 * 1024


def from_behind(block, distance):
    devices = range(lax.axis_size(AXES))
    route = [(i - distance, i) for i in devices if i - distance in devices]
    return lax.ppermute(block, AXES, route)


def halves(value):
    high = value.astype(jnp.bfloat16)
    low = (value - high.astype(jnp.float32)).astype(jnp.bfloat16)
    return high, low


def product(left, right, form):
    return lax.dot_general(left, right, form, preferred_element_type=jnp.float32)


class Columns:
    def __init__(self, count, factors_ref, buffer, semaphore, high_ref, low_ref):
        self.count, self.factors_ref, self.buffer = count, factors_ref, buffer
        self.semaphore, self.high_ref, self.low_ref = semaphore, high_ref, low_ref
        self.slots, self.width, points = factors_ref.shape
        self.size = points // count

    def block(self, index):
        return pl.ds(pl.multiple_of(index * self.size, self.size), self.size)

    def copy(self, index):
        block = self.block(index)
        return pltpu.make_async_copy(
            self.factors_ref.at[:, :, block], self.buffer.at[:, :, block],
            self.semaphore.at[index],
        )

    def start(self):
        for index in range(self.count):
            self.copy(index).start()

    def load(self, index):
        self.copy(index).wait()
        block = self.block(index)
        values = self.buffer[:, :, block].reshape(self.slots * self.width, self.size)
        self.high_ref[:, block], self.low_ref[:, block] = halves(values)

    def far(self, index, turned_ref):
        block, received = self.block(index), turned_ref[...]
        total = (
            product(received, self.high_ref[:, block], NN)
            + product(received, self.low_ref[:, block], NN)
        )
        n = total.shape[0] // 2
        return total[:n] + total[n:]

    def project(self, index, vectors, sums_ref):
        block = self.block(index)
        operand = jnp.concatenate(halves(vectors), axis=0)
        sums_ref[...] += (
            product(self.high_ref[:, block], operand, NT)
            + product(self.low_ref[:, block], operand, NT)
        )


def each_slot(slots, visit):
    together = next(size for size in (7, 4, 2, 1) if slots % size == 0)

    @pl.loop(0, slots // together)
    def _(group):
        for inner in range(together):
            visit(group * together + inner)


def store_chunks(width, sums_ref, partner_ref, ranks_ref, outgoing_ref):
    rows, lanes = sums_ref.shape
    half = width // 2
    own = lax.axis_index(AXES)
    left = lax.broadcasted_iota(jnp.int32, (half, lanes), 1) < lanes // 2
    rank_index = lax.broadcasted_iota(jnp.int32, (half, lanes), 0) + jnp.where(left, 0, half)

    def visit(slot):
        base = pl.multiple_of(slot * width, 16)
        top = sums_ref[pl.ds(base, half), :]
        bottom = sums_ref[pl.ds(base + half, half), :]
        top = top + pltpu.roll(top, lanes // 2, 1)
        bottom = bottom + pltpu.roll(bottom, lanes // 2, 1)
        chunk = jnp.where(rank_index < ranks_ref[slot], jnp.where(left, top, bottom), 0.0)
        place = partner_ref[slot]
        outgoing_ref[jnp.where(place >= 0, place, own)] = chunk

    each_slot(rows // width, visit)


def unpack(width, slots, partner_ref, incoming_ref, received_ref):
    _, half, lanes = incoming_ref.shape
    n = lanes // 2
    left = lax.broadcasted_iota(jnp.int32, (half, lanes), 1) < n

    def visit(slot):
        place = partner_ref[slot]
        chunk = jnp.where(place >= 0, incoming_ref[jnp.maximum(place, 0)], 0.0)
        high = chunk.astype(jnp.bfloat16).astype(jnp.float32)
        low = chunk - high
        top = jnp.where(left, high, pltpu.roll(low, n, 1))
        bottom = jnp.where(left, pltpu.roll(high, n, 1), low)
        base = pl.multiple_of(slot * width, 16)
        received_ref[pl.ds(base, half), :] = top.astype(jnp.bfloat16)
        received_ref[pl.ds(base + half, half), :] = bottom.astype(jnp.bfloat16)

    each_slot(slots, visit)


def project_kernel(partner_hbm, ranks_hbm, vectors_hbm, factors_ref, outgoing_ref,
                   buffer, semaphore, high_ref, low_ref, sums_ref, partner_ref, ranks_ref,
                   vectors_ref, small_semaphore):
    small = [
        pltpu.make_async_copy(source, target, small_semaphore.at[index])
        for index, (source, target) in enumerate((
            (vectors_hbm, vectors_ref), (partner_hbm, partner_ref), (ranks_hbm, ranks_ref)
        ))
    ]
    for copy in small:
        copy.start()
    columns = Columns(4, factors_ref, buffer, semaphore, high_ref, low_ref)
    columns.start()
    sums_ref[...] = jnp.zeros_like(sums_ref)
    for copy in small:
        copy.wait()

    @pl.loop(0, columns.count)
    def _(index):
        columns.load(index)
        columns.project(index, vectors_ref[:, columns.block(index)], sums_ref)

    store_chunks(columns.width, sums_ref, partner_ref, ranks_ref, outgoing_ref)


def turn_kernel(weights, partner_ref, ranks_ref, factors_ref, incoming_ref, base_ref,
                previous_ref, *rest):
    if weights is None:
        residual_ref, *rest = rest
        buffer, semaphore, high_ref, low_ref, received_ref, turned_ref = rest
    else:
        residual_ref, direction_ref, outgoing_ref, *rest = rest
        buffer, semaphore, high_ref, low_ref, received_ref, turned_ref, sums_ref = rest
    count = 4 if weights is None else 2
    columns = Columns(count, factors_ref, buffer, semaphore, high_ref, low_ref)
    columns.start()
    unpack(columns.width, columns.slots, partner_ref, incoming_ref, received_ref)
    turned_ref[...] = received_ref[...].T
    if weights is not None:
        sums_ref[...] = jnp.zeros_like(sums_ref)

    @pl.loop(0, columns.count)
    def _(index):
        columns.load(index)
        block = columns.block(index)
        residual = base_ref[:, block] - columns.far(index, turned_ref)
        residual_ref[:, block] = residual
        if weights is not None:
            old, new = weights
            direction = new * residual
            if old is not None:
                direction = old * previous_ref[:, block] + direction
            direction_ref[:, block] = direction
            columns.project(index, direction, sums_ref)

    if weights is not None:
        store_chunks(columns.width, sums_ref, partner_ref, ranks_ref, outgoing_ref)


SMEM_SPEC = pl.BlockSpec(memory_space=pltpu.SMEM)
VMEM_SPEC = pl.BlockSpec(memory_space=pltpu.VMEM)
ANY_SPEC = pl.BlockSpec(memory_space=pltpu.HBM)


def body(right_side, start, diag_tiles, neighbour_tiles, factors, partner, ranks):
    device_count = lax.axis_size(AXES)
    right_side, start = right_side[0], start[0]
    diag_block, neighbour_block, factor_block = diag_tiles[0], neighbour_tiles[0], factors[0]
    partner, ranks = partner[0], ranks[0]
    factor_block = pltpu.with_memory_space_constraint(factor_block, pltpu.HBM)
    slots, rank_width, points = factor_block.shape
    n = start.shape[0]
    rows = slots * rank_width
    block = jax.ShapeDtypeStruct((n, points), jnp.float32)
    chunks = jax.ShapeDtypeStruct((device_count, rank_width // 2, 2 * n), jnp.float32)
    loading = [
        pltpu.VMEM((slots, rank_width, points), jnp.float32),
        pltpu.SemaphoreType.DMA((4,)),
        pltpu.VMEM((rows, points), jnp.bfloat16),
        pltpu.VMEM((rows, points), jnp.bfloat16),
    ]
    received = [
        pltpu.VMEM((rows, 2 * n), jnp.bfloat16),
        pltpu.VMEM((2 * n, rows), jnp.bfloat16),
    ]
    sums = pltpu.VMEM((rows, 2 * n), jnp.float32)
    params = pltpu.CompilerParams(vmem_limit_bytes=VMEM_LIMIT)

    def cost(times):
        return pl.CostEstimate(
            flops=times * 8 * rows * points * n, bytes_accessed=4 * rows * points,
            transcendentals=0,
        )

    def in_place(array):
        return pltpu.with_memory_space_constraint(array, pltpu.HBM)

    def projected(vectors):
        return pl.pallas_call(
            project_kernel,
            out_shape=chunks,
            in_specs=[ANY_SPEC] * 4,
            out_specs=VMEM_SPEC,
            scratch_shapes=loading + [
                sums,
                pltpu.SMEM((slots,), jnp.int32),
                pltpu.SMEM((slots,), jnp.int32),
                pltpu.VMEM((n, points), jnp.float32),
                pltpu.SemaphoreType.DMA((3,)),
            ],
            compiler_params=params,
            cost_estimate=cost(1),
            name="project",
        )(in_place(partner), in_place(ranks), in_place(vectors), factor_block)

    def turn(weights, incoming, base, previous):
        last = weights is None
        outs = (block,) if last else (block, block, chunks)
        return pl.pallas_call(
            functools.partial(turn_kernel, weights),
            out_shape=outs,
            in_specs=[SMEM_SPEC, SMEM_SPEC, ANY_SPEC] + [VMEM_SPEC] * 3,
            out_specs=(VMEM_SPEC,) * len(outs),
            scratch_shapes=loading + received + ([] if last else [sums]),
            compiler_params=params,
            cost_estimate=cost(1 if last else 2),
            name="far" if last else "turn",
        )(partner, ranks, factor_block, incoming, base, previous)

    def finish(outgoing, vectors, before, weights):
        incoming = lax.all_to_all(outgoing, AXES, split_axis=0, concat_axis=0, tiled=True)
        exact = lax.Precision.HIGH
        following = from_behind(vectors, -1)
        carried = lax.dot_general(vectors, neighbour_block, NN, precision=exact)
        lower_term = from_behind(carried, 1)
        local_term = lax.dot_general(vectors, diag_block, NT, precision=exact)
        upper_term = lax.dot_general(following, neighbour_block, NT, precision=exact)
        base = before - (local_term + upper_term + lower_term)
        return turn(weights, incoming, base, vectors)

    center = (spectrum_low + spectrum_high) / 2.0
    half_width = (spectrum_high - spectrum_low) / 2.0
    ratio = center / half_width
    rho_now = 1.0 / ratio
    solution = start
    outgoing = projected(start)
    residual, direction, outgoing = finish(outgoing, start, right_side, (None, 1.0 / center))
    for iteration in range(ITERS):
        solution = solution + direction
        if iteration + 1 < ITERS:
            rho_next = 1.0 / (2.0 * ratio - rho_now)
            weights = (rho_next * rho_now, 2.0 * rho_next / half_width)
            residual, direction, outgoing = finish(outgoing, direction, residual, weights)
            rho_now = rho_next
        else:
            (residual,) = finish(outgoing, direction, residual, None)
    return (solution[None], residual[None])


def solution(mesh):
    return jax.shard_map(
        body,
        mesh=mesh,
        in_specs=(
            P(AXES, None, None),
            P(AXES, None, None),
            P(AXES, None, None),
            P(AXES, None, None),
            P(AXES, None, None, None),
            P(AXES, None),
            P(AXES, None),
        ),
        out_specs=(P(AXES, None, None), P(AXES, None, None)),
        check_vma=False,
    )
```

time: 135 us -> 126 us (0.933)
  Pallas kernels: 42.9 us -> 35.9 us
  local copies, waits for them, and re-layouts: 2.31 us -> 0.05 us
    pallas_call x4, Pallas kernels: 42.9 us -> 35.9 us  [the longest x3 28 us: turn(): pl.pallas_call(functools.partial(turn_kernel, weights), out_shape=outs, i...]
    unnamed x24 -> x18, local copies, waits for them, and re-layouts: 2.31 us -> 0.05 us
  transfers between devices with their start and end apart: 9 -> 9, of which waited for: 4 -> 4; matrix products, arithmetic and copies ran while one was open for 20% -> 21% of each run, Pallas kernels for 0% -> 0%
where the time goes in v1:
time: 126 us; the launch traced here: 125 us
  starting transfers between devices  37.2 us (30%)
  Pallas kernels  35.9 us (28%)
  matrix products  25.7 us (20%)
  waiting for transfers between devices  24.5 us (19%)
    pallas_call x3, Pallas kernels, turn(): pl.pallas_call(functools.partial(turn_kernel, weights), out_shape=outs, i...  28 us
    ppermute x6, waiting for transfers between devices, from_behind(): return lax.ppermute(block, AXES, route)  24.5 us
    ppermute x6, starting transfers between devices, from_behind(): return lax.ppermute(block, AXES, route)  23.1 us
    all_to_all x3, starting transfers between devices, finish(): lax.all_to_all(outgoing, AXES, split_axis=0, concat_axis=0, tiled=True)  14.2 us
    dot_general x3, matrix products, finish(): carried = lax.dot_general(vectors, neighbour_block, NN, precision=exact)  10.8 us
    dot_general x3, matrix products, finish(): local_term = lax.dot_general(vectors, diag_block, NT, precision=exact)  8.53 us
    pallas_call x1, Pallas kernels, projected(): pl.pallas_call(project_kernel, out_shape=chunks, in_specs=[ANY_SPEC] * 4,...  7.85 us
    dot_general x3, matrix products, finish(): lax.dot_general(following, neighbour_block, NT, precision=exact)  6.35 us
  transfers between devices with their start and end apart: 9, of which 4 were waited for; matrix products, arithmetic and copies ran while one was open for 21% of the time, Pallas kernels for 0%

profile of v1, /device:TPU:15, one launch (start us, length us, event | category | flops | bytes accessed | tf_op | source)
XLA Modules:
  0.0 125.3 jit_solution(4483936778354050477)
XLA Ops:
  0.6 7.8 %project.1 = f32[32,48,128]{2,1,0:T(8,128)} custom-call(s32[28]{0:T(128)} %bitcast.54, s32[28]{0:T(128)} %bitcast.58, f32[64,1024]{1,0:T(8,128)} %bitcast.51, f32[28,96,1024]{2,1,0:T(8,128)} %bitcast.62), custom_call_target="tpu_custom_call" | custom-call | flops 1409286144 | bytes 11010048 | tf_op jit(solution)/shard_map/project/pallas_call | solution.py:230
  8.5 6.3 %all-to-all-start = ((f32[32,48,128]{2,1,0:T(8,128)}), f32[32,48,128]{2,1,0:T(8,128)S(1)}, u32[]{:S(2)}, u32[]{:S(2)}) async-start(f32[32,48,128]{2,1,0:T(8,128)} %project.1), calls=%async_computation | async-start | bytes 1572864 | tf_op jit(solution)/shard_map/all_to_all | solution.py:262
  14.8 0.0 copy-start.3
  14.8 0.0 copy-start.8
  14.8 2.6 %collective-permute-start = (f32[64,1024]{1,0:T(8,128)S(1)}, f32[64,1024]{1,0:T(8,128)S(1)}, u32[]{:S(2)}, u32[]{:S(2)}) collective-permute-start(f32[64,1024]{1,0:T(8,128)S(1)} %bitcast.52), channel_id=1, source_target_pairs={{1,0},{2,1},{3,2},{4,3},{5,4},{6,5},{7,6},{8,7},{9,8},{10,9},{11,1... | collective-permute-start | bytes 786440 | tf_op jit(solution)/shard_map/ppermute | solution.py:26
  17.4 3.6 %fusion.8 = f32[64,1024]{1,0:T(8,128)S(1)} fusion(f32[1,1024,1024]{2,1,0:T(8,128)} %param.10, f32[1,64,1024]{2,1,0:T(8,128)S(1)} %copy-done), kind=kOutput, calls=%fused_computation.8 | convolution fusion | flops 402653184 | bytes 4718592 | tf_op jit(solution)/shard_map/dot_general | solution.py:265
  21.0 0.0 copy-start.1
  21.0 5.1 %collective-permute-start.1 = (f32[64,1024]{1,0:T(8,128)S(1)}, f32[64,1024]{1,0:T(8,128)S(1)}, u32[]{:S(2)}, u32[]{:S(2)}) collective-permute-start(f32[64,1024]{1,0:T(8,128)S(1)} %fusion.8), channel_id=1, source_target_pairs={{0,1},{1,2},{2,3},{3,4},{4,5},{5,6},{6,7},{7,8},{8,9},{9,10},{10,1... | collective-permute-start | bytes 786440 | tf_op jit(solution)/shard_map/ppermute | solution.py:26
  26.1 4.2 %fusion.16 = f32[64,1024]{1,0:T(8,128)S(1)} fusion(f32[1,1024,1024]{2,1,0:T(8,128)} %param.9, f32[1,64,1024]{2,1,0:T(8,128)S(1)} %copy-done), kind=kOutput, calls=%fused_computation.16 | convolution fusion | flops 402653184 | bytes 4718592 | tf_op jit(solution)/shard_map/dot_general | solution.py:267
  30.3 4.8 %collective-permute-done.1 = f32[64,1024]{1,0:T(8,128)S(1)} collective-permute-done((f32[64,1024]{1,0:T(8,128)S(1)}, f32[64,1024]{1,0:T(8,128)S(1)}, u32[]{:S(2)}, u32[]{:S(2)}) %collective-permute-start.1) | collective-permute-done | bytes 262176 | tf_op jit(solution)/shard_map/ppermute | solution.py:26
  35.0 1.6 %collective-permute-done = f32[64,1024]{1,0:T(8,128)S(1)} collective-permute-done((f32[64,1024]{1,0:T(8,128)S(1)}, f32[64,1024]{1,0:T(8,128)S(1)}, u32[]{:S(2)}, u32[]{:S(2)}) %collective-permute-start) | collective-permute-done | bytes 262176 | tf_op jit(solution)/shard_map/ppermute | solution.py:26
  36.7 2.1 %fusion.30.base_ref = f32[64,1024]{1,0:T(8,128)S(1)} fusion(f32[64,1024]{1,0:T(8,128)S(1)} %collective-permute-done.1, f32[64,1024]{1,0:T(8,128)S(1)} %fusion.16, f32[64,1024]{1,0:T(8,128)S(1)} %collective-permute-done, f32[1,1024,1024]{2,1,0:T(8,128)S(1)} %copy-done.3, f32[1,64,1024]{2,1,0:T(8,128)S(1)} %copy-done.8), kind=kOutput, calls=%fused_computation.22 | convolution fusion | flops 402849792 | bytes 5505024 | tf_op jit(solution)/shard_map/dot_general | solution.py:268
  38.7 11.0 %turn.2 = (f32[64,1024]{1,0:T(8,128)S(1)}, f32[64,1024]{1,0:T(8,128)S(1)}, f32[32,48,128]{2,1,0:T(8,128)}) custom-call(s32[28]{0:T(128)S(1)} %bitcast.55, s32[28]{0:T(128)S(1)} %bitcast.59, f32[28,96,1024]{2,1,0:T(8,128)} %bitcast.63, f32[32,48,128]{2,1,0:T(8,128)S(1)} %all-to-all-done.incoming_ref, f32[64,1024]{1,0:T(8,128)S(1)} %fusion.30.base_ref, ...), custom_call_target="tpu_custom_call" | custom-call | flops 2818572288 | bytes 11010048 | tf_op jit(solution)/shard_map/turn/pallas_call | solution.py:250
  49.7 4.3 %all-to-all-start.1 = ((f32[32,48,128]{2,1,0:T(8,128)}), f32[32,48,128]{2,1,0:T(8,128)S(1)}, u32[]{:S(2)}, u32[]{:S(2)}) async-start(f32[32,48,128]{2,1,0:T(8,128)} %get-tuple-element.9), calls=%async_computation.1 | async-start | bytes 1572864 | tf_op jit(solution)/shard_map/all_to_all | solution.py:262
  54.0 2.7 %collective-permute-start.2 = (f32[64,1024]{1,0:T(8,128)S(1)}, f32[64,1024]{1,0:T(8,128)S(1)}, u32[]{:S(2)}, u32[]{:S(2)}) collective-permute-start(f32[64,1024]{1,0:T(8,128)S(1)} %get-tuple-element.8.previous_ref), channel_id=1, source_target_pairs={{1,0},{2,1},{3,2},{4,3},{5,4},{6,5},{7,6},{8,7},{9,8},{10,9},{11,1... | collective-permute-start | bytes 786440 | tf_op jit(solution)/shard_map/ppermute | solution.py:26
  56.7 3.6 %fusion.4 = f32[64,1024]{1,0:T(8,128)S(1)} fusion(f32[64,1024]{1,0:T(8,128)S(1)} %get-tuple-element.8.previous_ref, f32[1,1024,1024]{2,1,0:T(8,128)} %param.10), kind=kOutput, calls=%fused_computation.4 | convolution fusion | flops 402653184 | bytes 4718592 | tf_op jit(solution)/shard_map/dot_general | solution.py:265
  60.3 5.1 %collective-permute-start.3 = (f32[64,1024]{1,0:T(8,128)S(1)}, f32[64,1024]{1,0:T(8,128)S(1)}, u32[]{:S(2)}, u32[]{:S(2)}) collective-permute-start(f32[64,1024]{1,0:T(8,128)S(1)} %fusion.4), channel_id=1, source_target_pairs={{0,1},{1,2},{2,3},{3,4},{4,5},{5,6},{6,7},{7,8},{8,9},{9,10},{10,1... | collective-permute-start | bytes 786440 | tf_op jit(solution)/shard_map/ppermute | solution.py:26
  65.4 10.4 %collective-permute-done.2 = f32[64,1024]{1,0:T(8,128)S(1)} collective-permute-done((f32[64,1024]{1,0:T(8,128)S(1)}, f32[64,1024]{1,0:T(8,128)S(1)}, u32[]{:S(2)}, u32[]{:S(2)}) %collective-permute-start.2) | collective-permute-done | bytes 262176 | tf_op jit(solution)/shard_map/ppermute | solution.py:26
  75.9 2.1 %fusion.6 = f32[64,1024]{1,0:T(8,128)S(1)} fusion(f32[64,1024]{1,0:T(8,128)S(1)} %collective-permute-done.2, f32[1,1024,1024]{2,1,0:T(8,128)S(1)} %copy-done.4), kind=kOutput, calls=%fused_computation.6 | convolution fusion | flops 402653184 | bytes 4718592 | tf_op jit(solution)/shard_map/dot_general | solution.py:268
  78.0 2.2 %fusion.21 = f32[64,1024]{1,0:T(8,128)S(1)} fusion(f32[64,1024]{1,0:T(8,128)S(1)} %collective-permute-done.3, f32[64,1024]{1,0:T(8,128)S(1)} %fusion.6, f32[64,1024]{1,0:T(8,128)S(1)} %get-tuple-element.8.previous_ref, f32[1,1024,1024]{2,1,0:T(8,128)S(1)} %copy-done.6), kind=kOutput, calls=%fused_computation.19 | convolution fusion | flops 402784256 | bytes 5242880 | tf_op jit(solution)/shard_map/dot_general | solution.py:267
  80.3 11.0 %turn.3 = (f32[64,1024]{1,0:T(8,128)S(1)}, f32[64,1024]{1,0:T(8,128)S(1)}, f32[32,48,128]{2,1,0:T(8,128)}) custom-call(s32[28]{0:T(128)S(1)} %bitcast.56, s32[28]{0:T(128)S(1)} %bitcast.60, f32[28,96,1024]{2,1,0:T(8,128)} %bitcast.64, f32[32,48,128]{2,1,0:T(8,128)S(1)} %all-to-all-done.1.incoming_ref, f32[64,1024]{1,0:T(8,128)S(1)} %sub.10.base_ref, ...), custom_call_target="tpu_custom_call" | custom-call | flops 2818572288 | bytes 11010048 | tf_op jit(solution)/shard_map/turn/pallas_call | solution.py:250
  91.2 3.7 %all-to-all-start.2 = ((f32[32,48,128]{2,1,0:T(8,128)}), f32[32,48,128]{2,1,0:T(8,128)S(1)}, u32[]{:S(2)}, u32[]{:S(2)}) async-start(f32[32,48,128]{2,1,0:T(8,128)} %get-tuple-element.12), calls=%async_computation.2 | async-start | bytes 1572864 | tf_op jit(solution)/shard_map/all_to_all | solution.py:262
  94.9 0.0 copy-start.5
  94.9 2.7 %collective-permute-start.4 = (f32[64,1024]{1,0:T(8,128)S(1)}, f32[64,1024]{1,0:T(8,128)S(1)}, u32[]{:S(2)}, u32[]{:S(2)}) collective-permute-start(f32[64,1024]{1,0:T(8,128)S(1)} %get-tuple-element.11.previous_ref), channel_id=1, source_target_pairs={{1,0},{2,1},{3,2},{4,3},{5,4},{6,5},{7,6},{8,7},{9,8},{10,9},{11,1... | collective-permute-start | bytes 786440 | tf_op jit(solution)/shard_map/ppermute | solution.py:26
  97.6 3.6 %fusion = f32[64,1024]{1,0:T(8,128)S(1)} fusion(f32[64,1024]{1,0:T(8,128)S(1)} %get-tuple-element.11.previous_ref, f32[1,1024,1024]{2,1,0:T(8,128)} %param.10), kind=kOutput, calls=%fused_computation | convolution fusion | flops 402653184 | bytes 4718592 | tf_op jit(solution)/shard_map/dot_general | solution.py:265
  101.3 2.2 %fusion.12 = f32[64,1024]{1,0:T(8,128)S(1)} fusion(f32[64,1024]{1,0:T(8,128)S(1)} %get-tuple-element.11.previous_ref, f32[1,1024,1024]{2,1,0:T(8,128)S(1)} %copy-done.7), kind=kOutput, calls=%fused_computation.12 | convolution fusion | flops 402653184 | bytes 4718592 | tf_op jit(solution)/shard_map/dot_general | solution.py:267
  103.4 4.9 %collective-permute-start.5 = (f32[64,1024]{1,0:T(8,128)S(1)}, f32[64,1024]{1,0:T(8,128)S(1)}, u32[]{:S(2)}, u32[]{:S(2)}) collective-permute-start(f32[64,1024]{1,0:T(8,128)S(1)} %fusion), channel_id=1, source_target_pairs={{0,1},{1,2},{2,3},{3,4},{4,5},{5,6},{6,7},{7,8},{8,9},{9,10},{10,1... | collective-permute-start | bytes 786440 | tf_op jit(solution)/shard_map/ppermute | solution.py:26
  108.3 0.7 add_bitcast_fusion
  109.1 7.7 %collective-permute-done.4 = f32[64,1024]{1,0:T(8,128)S(1)} collective-permute-done((f32[64,1024]{1,0:T(8,128)S(1)}, f32[64,1024]{1,0:T(8,128)S(1)}, u32[]{:S(2)}, u32[]{:S(2)}) %collective-permute-start.4) | collective-permute-done | bytes 262176 | tf_op jit(solution)/shard_map/ppermute | solution.py:26
  116.8 2.1 %fusion.2 = f32[64,1024]{1,0:T(8,128)S(1)} fusion(f32[64,1024]{1,0:T(8,128)S(1)} %collective-permute-done.4, f32[1,1024,1024]{2,1,0:T(8,128)S(1)} %copy-done.5), kind=kOutput, calls=%fused_computation.2 | convolution fusion | flops 402653184 | bytes 4718592 | tf_op jit(solution)/shard_map/dot_general | solution.py:268
  118.9 0.1 add_subtract_fusion.base_ref
  119.0 6.1 %far.1 = f32[64,1024]{1,0:T(8,128)} custom-call(s32[28]{0:T(128)S(1)} %bitcast.57, s32[28]{0:T(128)S(1)} %bitcast.61, f32[28,96,1024]{2,1,0:T(8,128)} %bitcast.65, f32[32,48,128]{2,1,0:T(8,128)S(1)} %all-to-all-done.2.incoming_ref, f32[64,1024]{1,0:T(8,128)S(1)} %add_subtract_fusion.base_ref, f32[64,1024]{1,0:T(8,128)S(1)} %get-tuple-element.11.previous_ref), custom_call_target="tpu_custom_call" | custom-call | flops 1409286144 | bytes 11010048 | tf_op jit(solution)/shard_map/far/pallas_call | solution.py:250
  (20 shorter events, 0.1 us)
Async XLA Ops:
  0.6 14.1 %copy-start = (f32[1,64,1024]{2,1,0:T(8,128)S(1)}, f32[1,64,1024]{2,1,0:T(8,128)}, u32[]{:S(2)}) copy-start(f32[1,64,1024]{2,1,0:T(8,128)} %param.8) | copy-start | bytes 786436
  8.5 30.2 %all-to-all-start = ((f32[32,48,128]{2,1,0:T(8,128)}), f32[32,48,128]{2,1,0:T(8,128)S(1)}, u32[]{:S(2)}, u32[]{:S(2)}) async-start(f32[32,48,128]{2,1,0:T(8,128)} %project.1), calls=%async_computation | async-start | bytes 1572864 | tf_op jit(solution)/shard_map/all_to_all | solution.py:262
  14.8 21.9 %copy-start.3 = (f32[1,1024,1024]{2,1,0:T(8,128)S(1)}, f32[1,1024,1024]{2,1,0:T(8,128)}, u32[]{:S(2)}) copy-start(f32[1,1024,1024]{2,1,0:T(8,128)} %param.10) | copy-start | bytes 12582916
  14.8 21.9 %copy-start.8 = (f32[1,64,1024]{2,1,0:T(8,128)S(1)}, f32[1,64,1024]{2,1,0:T(8,128)}, u32[]{:S(2)}) copy-start(f32[1,64,1024]{2,1,0:T(8,128)} %param.7) | copy-start | bytes 786436
  14.8 21.9 %collective-permute-start = (f32[64,1024]{1,0:T(8,128)S(1)}, f32[64,1024]{1,0:T(8,128)S(1)}, u32[]{:S(2)}, u32[]{:S(2)}) collective-permute-start(f32[64,1024]{1,0:T(8,128)S(1)} %bitcast.52), channel_id=1, source_target_pairs={{1,0},{2,1},{3,2},{4,3},{5,4},{6,5},{7,6},{8,7},{9,8},{10,9},{11,1... | collective-permute-start | bytes 786440 | tf_op jit(solution)/shard_map/ppermute | solution.py:26
  21.0 17.7 %copy-start.1 = (s32[1,28]{1,0:T(1,128)S(1)}, s32[1,28]{1,0:T(1,128)}, u32[]{:S(2)}) copy-start(s32[1,28]{1,0:T(1,128)} %param.12) | copy-start | bytes 340
  21.0 17.7 %copy-start.2 = (s32[1,28]{1,0:T(1,128)S(1)}, s32[1,28]{1,0:T(1,128)}, u32[]{:S(2)}) copy-start(s32[1,28]{1,0:T(1,128)} %param.13) | copy-start | bytes 340
  21.0 14.0 %collective-permute-start.1 = (f32[64,1024]{1,0:T(8,128)S(1)}, f32[64,1024]{1,0:T(8,128)S(1)}, u32[]{:S(2)}, u32[]{:S(2)}) collective-permute-start(f32[64,1024]{1,0:T(8,128)S(1)} %fusion.8), channel_id=1, source_target_pairs={{0,1},{1,2},{2,3},{3,4},{4,5},{5,6},{6,7},{7,8},{8,9},{9,10},{10,1... | collective-permute-start | bytes 786440 | tf_op jit(solution)/shard_map/ppermute | solution.py:26
  49.7 30.5 %all-to-all-start.1 = ((f32[32,48,128]{2,1,0:T(8,128)}), f32[32,48,128]{2,1,0:T(8,128)S(1)}, u32[]{:S(2)}, u32[]{:S(2)}) async-start(f32[32,48,128]{2,1,0:T(8,128)} %get-tuple-element.9), calls=%async_computation.1 | async-start | bytes 1572864 | tf_op jit(solution)/shard_map/all_to_all | solution.py:262
  54.0 21.9 %copy-start.4 = (f32[1,1024,1024]{2,1,0:T(8,128)S(1)}, f32[1,1024,1024]{2,1,0:T(8,128)}, u32[]{:S(2)}) copy-start(f32[1,1024,1024]{2,1,0:T(8,128)} %param.10) | copy-start | bytes 12582916
  54.0 24.0 %copy-start.6 = (f32[1,1024,1024]{2,1,0:T(8,128)S(1)}, f32[1,1024,1024]{2,1,0:T(8,128)}, u32[]{:S(2)}) copy-start(f32[1,1024,1024]{2,1,0:T(8,128)} %param.9) | copy-start | bytes 12582916
  54.0 21.9 %collective-permute-start.2 = (f32[64,1024]{1,0:T(8,128)S(1)}, f32[64,1024]{1,0:T(8,128)S(1)}, u32[]{:S(2)}, u32[]{:S(2)}) collective-permute-start(f32[64,1024]{1,0:T(8,128)S(1)} %get-tuple-element.8.previous_ref), channel_id=1, source_target_pairs={{1,0},{2,1},{3,2},{4,3},{5,4},{6,5},{7,6},{8,7},{9,8},{10,9},{11,1... | collective-permute-start | bytes 786440 | tf_op jit(solution)/shard_map/ppermute | solution.py:26
  60.3 17.7 %collective-permute-start.3 = (f32[64,1024]{1,0:T(8,128)S(1)}, f32[64,1024]{1,0:T(8,128)S(1)}, u32[]{:S(2)}, u32[]{:S(2)}) collective-permute-start(f32[64,1024]{1,0:T(8,128)S(1)} %fusion.4), channel_id=1, source_target_pairs={{0,1},{1,2},{2,3},{3,4},{4,5},{5,6},{6,7},{7,8},{8,9},{9,10},{10,1... | collective-permute-start | bytes 786440 | tf_op jit(solution)/shard_map/ppermute | solution.py:26
  91.2 27.8 %all-to-all-start.2 = ((f32[32,48,128]{2,1,0:T(8,128)}), f32[32,48,128]{2,1,0:T(8,128)S(1)}, u32[]{:S(2)}, u32[]{:S(2)}) async-start(f32[32,48,128]{2,1,0:T(8,128)} %get-tuple-element.12), calls=%async_computation.2 | async-start | bytes 1572864 | tf_op jit(solution)/shard_map/all_to_all | solution.py:262
  94.9 6.3 %copy-start.7 = (f32[1,1024,1024]{2,1,0:T(8,128)S(1)}, f32[1,1024,1024]{2,1,0:T(8,128)}, u32[]{:S(2)}) copy-start(f32[1,1024,1024]{2,1,0:T(8,128)} %param.9) | copy-start | bytes 12582916
  94.9 21.9 %copy-start.5 = (f32[1,1024,1024]{2,1,0:T(8,128)S(1)}, f32[1,1024,1024]{2,1,0:T(8,128)}, u32[]{:S(2)}) copy-start(f32[1,1024,1024]{2,1,0:T(8,128)} %param.10) | copy-start | bytes 12582916
  94.9 21.9 %collective-permute-start.4 = (f32[64,1024]{1,0:T(8,128)S(1)}, f32[64,1024]{1,0:T(8,128)S(1)}, u32[]{:S(2)}, u32[]{:S(2)}) collective-permute-start(f32[64,1024]{1,0:T(8,128)S(1)} %get-tuple-element.11.previous_ref), channel_id=1, source_target_pairs={{1,0},{2,1},{3,2},{4,3},{5,4},{6,5},{7,6},{8,7},{9,8},{10,9},{11,1... | collective-permute-start | bytes 786440 | tf_op jit(solution)/shard_map/ppermute | solution.py:26
  103.4 15.5 %collective-permute-start.5 = (f32[64,1024]{1,0:T(8,128)S(1)}, f32[64,1024]{1,0:T(8,128)S(1)}, u32[]{:S(2)}, u32[]{:S(2)}) collective-permute-start(f32[64,1024]{1,0:T(8,128)S(1)} %fusion), channel_id=1, source_target_pairs={{0,1},{1,2},{2,3},{3,4},{4,5},{5,6},{6,7},{7,8},{8,9},{9,10},{10,1... | collective-permute-start | bytes 786440 | tf_op jit(solution)/shard_map/ppermute | solution.py:26

commit v2 on v1

--- a/solution.py
+++ b/solution.py
@@ -37,19 +37,17 @@
 
 
 class Columns:
-    def __init__(self, count, factors_ref, buffer, semaphore, high_ref, low_ref):
-        self.count, self.factors_ref, self.buffer = count, factors_ref, buffer
-        self.semaphore, self.high_ref, self.low_ref = semaphore, high_ref, low_ref
-        self.slots, self.width, points = factors_ref.shape
-        self.size = points // count
+    def __init__(self, factors_ref, buffer, semaphore, split_ref):
+        self.factors_ref, self.buffer = factors_ref, buffer
+        self.semaphore, self.split_ref = semaphore, split_ref
+        self.count, self.slots, self.width, self.size = buffer.shape
 
     def block(self, index):
         return pl.ds(pl.multiple_of(index * self.size, self.size), self.size)
 
     def copy(self, index):
-        block = self.block(index)
         return pltpu.make_async_copy(
-            self.factors_ref.at[:, :, block], self.buffer.at[:, :, block],
+            self.factors_ref.at[:, :, self.block(index)], self.buffer.at[index],
             self.semaphore.at[index],
         )
 
@@ -59,26 +57,19 @@
 
     def load(self, index):
         self.copy(index).wait()
-        block = self.block(index)
-        values = self.buffer[:, :, block].reshape(self.slots * self.width, self.size)
-        self.high_ref[:, block], self.low_ref[:, block] = halves(values)
-
-    def far(self, index, turned_ref):
-        block, received = self.block(index), turned_ref[...]
-        total = (
-            product(received, self.high_ref[:, block], NN)
-            + product(received, self.low_ref[:, block], NN)
-        )
+        values = self.buffer[index].reshape(self.slots * self.width, self.size)
+        self.split_ref[:, :self.size], self.split_ref[:, self.size:] = halves(values)
+
+    def far(self, turned_ref):
+        total = product(turned_ref[...], self.split_ref[...], NN)
         n = total.shape[0] // 2
-        return total[:n] + total[n:]
-
-    def project(self, index, vectors, sums_ref):
-        block = self.block(index)
+        total = total[:n] + total[n:]
+        return total[:, :self.size] + total[:, self.size:]
+
+    def project(self, vectors, sums_ref):
         operand = jnp.concatenate(halves(vectors), axis=0)
-        sums_ref[...] += (
-            product(self.high_ref[:, block], operand, NT)
-            + product(self.low_ref[:, block], operand, NT)
-        )
+        operand = jnp.concatenate([operand, operand], axis=1)
+        sums_ref[...] += product(self.split_ref[...], operand, NT)
 
 
 def each_slot(slots, visit):
@@ -130,7 +121,7 @@
 
 
 def project_kernel(partner_hbm, ranks_hbm, vectors_hbm, factors_ref, outgoing_ref,
-                   buffer, semaphore, high_ref, low_ref, sums_ref, partner_ref, ranks_ref,
+                   buffer, semaphore, split_ref, sums_ref, partner_ref, ranks_ref,
                    vectors_ref, small_semaphore):
     small = [
         pltpu.make_async_copy(source, target, small_semaphore.at[index])
@@ -140,7 +131,7 @@
     ]
     for copy in small:
         copy.start()
-    columns = Columns(4, factors_ref, buffer, semaphore, high_ref, low_ref)
+    columns = Columns(factors_ref, buffer, semaphore, split_ref)
     columns.start()
     sums_ref[...] = jnp.zeros_like(sums_ref)
     for copy in small:
@@ -149,7 +140,7 @@
     @pl.loop(0, columns.count)
     def _(index):
         columns.load(index)
-        columns.project(index, vectors_ref[:, columns.block(index)], sums_ref)
+        columns.project(vectors_ref[:, columns.block(index)], sums_ref)
 
     store_chunks(columns.width, sums_ref, partner_ref, ranks_ref, outgoing_ref)
 
@@ -158,12 +149,11 @@
                 previous_ref, *rest):
     if weights is None:
         residual_ref, *rest = rest
-        buffer, semaphore, high_ref, low_ref, received_ref, turned_ref = rest
+        buffer, semaphore, split_ref, received_ref, turned_ref = rest
     else:
         residual_ref, direction_ref, outgoing_ref, *rest = rest
-        buffer, semaphore, high_ref, low_ref, received_ref, turned_ref, sums_ref = rest
-    count = 4 if weights is None else 2
-    columns = Columns(count, factors_ref, buffer, semaphore, high_ref, low_ref)
+        buffer, semaphore, split_ref, received_ref, turned_ref, sums_ref = rest
+    columns = Columns(factors_ref, buffer, semaphore, split_ref)
     columns.start()
     unpack(columns.width, columns.slots, partner_ref, incoming_ref, received_ref)
     turned_ref[...] = received_ref[...].T
@@ -174,7 +164,7 @@
     def _(index):
         columns.load(index)
         block = columns.block(index)
-        residual = base_ref[:, block] - columns.far(index, turned_ref)
+        residual = base_ref[:, block] - columns.far(turned_ref)
         residual_ref[:, block] = residual
         if weights is not None:
             old, new = weights
@@ -182,7 +172,7 @@
             if old is not None:
                 direction = old * previous_ref[:, block] + direction
             direction_ref[:, block] = direction
-            columns.project(index, direction, sums_ref)
+            columns.project(direction, sums_ref)
 
     if weights is not None:
         store_chunks(columns.width, sums_ref, partner_ref, ranks_ref, outgoing_ref)
@@ -204,12 +194,13 @@
     rows = slots * rank_width
     block = jax.ShapeDtypeStruct((n, points), jnp.float32)
     chunks = jax.ShapeDtypeStruct((device_count, rank_width // 2, 2 * n), jnp.float32)
-    loading = [
-        pltpu.VMEM((slots, rank_width, points), jnp.float32),
-        pltpu.SemaphoreType.DMA((4,)),
-        pltpu.VMEM((rows, points), jnp.bfloat16),
-        pltpu.VMEM((rows, points), jnp.bfloat16),
-    ]
+    def loading(blocks):
+        return [
+            pltpu.VMEM((blocks, slots, rank_width, points // blocks), jnp.float32),
+            pltpu.SemaphoreType.DMA((blocks,)),
+            pltpu.VMEM((rows, 2 * points // blocks), jnp.bfloat16),
+        ]
+
     received = [
         pltpu.VMEM((rows, 2 * n), jnp.bfloat16),
         pltpu.VMEM((2 * n, rows), jnp.bfloat16),
@@ -232,7 +223,7 @@
             out_shape=chunks,
             in_specs=[ANY_SPEC] * 4,
             out_specs=VMEM_SPEC,
-            scratch_shapes=loading + [
+            scratch_shapes=loading(4) + [
                 sums,
                 pltpu.SMEM((slots,), jnp.int32),
                 pltpu.SMEM((slots,), jnp.int32),
@@ -252,7 +243,7 @@
             out_shape=outs,
             in_specs=[SMEM_SPEC, SMEM_SPEC, ANY_SPEC] + [VMEM_SPEC] * 3,
             out_specs=(VMEM_SPEC,) * len(outs),
-            scratch_shapes=loading + received + ([] if last else [sums]),
+            scratch_shapes=loading(4 if last else 2) + received + ([] if last else [sums]),
             compiler_params=params,
             cost_estimate=cost(1 if last else 2),
             name="far" if last else "turn",
@@ -264,9 +255,10 @@
         following = from_behind(vectors, -1)
         carried = lax.dot_general(vectors, neighbour_block, NN, precision=exact)
         lower_term = from_behind(carried, 1)
-        local_term = lax.dot_general(vectors, diag_block, NT, precision=exact)
+        partial = before - lax.dot_general(vectors, diag_block, NT, precision=exact)
+        partial = lax.optimization_barrier(partial)
         upper_term = lax.dot_general(following, neighbour_block, NT, precision=exact)
-        base = before - (local_term + upper_term + lower_term)
+        base = partial - (upper_term + lower_term)
         return turn(weights, incoming, base, vectors)
 
     center = (spectrum_low + spectrum_high) / 2.0

time: 126 us -> 124 us (0.984)
  waiting for transfers between devices: 24.5 us -> 22.2 us
    ppermute x6, waiting for transfers between devices: 24.5 us -> 22.2 us  [from_behind(): return lax.ppermute(block, AXES, route)]
  transfers between devices with their start and end apart: 9 -> 9, of which waited for: 4 -> 6; matrix products, arithmetic and copies ran while one was open for 21% -> 21% of each run, Pallas kernels for 0% -> 0%
where the time goes in v2:
time: 124 us; the launch traced here: 122 us
  starting transfers between devices  38.1 us (31%)
  Pallas kernels  34.7 us (28%)
  matrix products  25.3 us (20%)
  waiting for transfers between devices  22.2 us (18%)
    pallas_call x3, Pallas kernels, turn(): pl.pallas_call(functools.partial(turn_kernel, weights), out_shape=outs, i...  26.9 us
    ppermute x6, starting transfers between devices, from_behind(): return lax.ppermute(block, AXES, route)  23.3 us
    ppermute x6, waiting for transfers between devices, from_behind(): return lax.ppermute(block, AXES, route)  22.2 us
    all_to_all x3, starting transfers between devices, finish(): lax.all_to_all(outgoing, AXES, split_axis=0, concat_axis=0, tiled=True)  14.8 us
    dot_general x3, matrix products, finish(): carried = lax.dot_general(vectors, neighbour_block, NN, precision=exact)  10.8 us
    dot_general x3, matrix products, finish(): partial = before - lax.dot_general(vectors, diag_block, NT, precision=exact)  8.32 us
    pallas_call x1, Pallas kernels, projected(): pl.pallas_call(project_kernel, out_shape=chunks, in_specs=[ANY_SPEC] * 4,...  7.79 us
    dot_general x3, matrix products, finish(): lax.dot_general(following, neighbour_block, NT, precision=exact)  6.14 us
  transfers between devices with their start and end apart: 9, of which 6 were waited for; matrix products, arithmetic and copies ran while one was open for 21% of the time, Pallas kernels for 0%

profile of v2, /device:TPU:15, one launch (start us, length us, event | category | flops | bytes accessed | tf_op | source)
XLA Modules:
  0.0 122.2 jit_solution(1342455904360665116)
XLA Ops:
  0.6 7.8 %project.1 = f32[32,48,128]{2,1,0:T(8,128)} custom-call(s32[28]{0:T(128)} %bitcast.58, s32[28]{0:T(128)} %bitcast.62, f32[64,1024]{1,0:T(8,128)} %bitcast.55, f32[28,96,1024]{2,1,0:T(8,128)} %bitcast.66), custom_call_target="tpu_custom_call" | custom-call | flops 1409286144 | bytes 11010048 | tf_op jit(solution)/shard_map/project/pallas_call | solution.py:221
  8.4 0.0 copy-start.8
  8.4 6.2 %all-to-all-start = ((f32[32,48,128]{2,1,0:T(8,128)}), f32[32,48,128]{2,1,0:T(8,128)S(1)}, u32[]{:S(2)}, u32[]{:S(2)}) async-start(f32[32,48,128]{2,1,0:T(8,128)} %project.1), calls=%async_computation | async-start | bytes 1572864 | tf_op jit(solution)/shard_map/all_to_all | solution.py:253
  14.7 0.0 copy-start.3
  14.7 2.6 %collective-permute-start = (f32[64,1024]{1,0:T(8,128)S(1)}, f32[64,1024]{1,0:T(8,128)S(1)}, u32[]{:S(2)}, u32[]{:S(2)}) collective-permute-start(f32[64,1024]{1,0:T(8,128)S(1)} %bitcast.56), channel_id=1, source_target_pairs={{1,0},{2,1},{3,2},{4,3},{5,4},{6,5},{7,6},{8,7},{9,8},{10,9},{11,1... | collective-permute-start | bytes 786440 | tf_op jit(solution)/shard_map/ppermute | solution.py:26
  17.3 3.6 %fusion.8 = f32[64,1024]{1,0:T(8,128)S(1)} fusion(f32[1,1024,1024]{2,1,0:T(8,128)} %param.10, f32[1,64,1024]{2,1,0:T(8,128)S(1)} %copy-done), kind=kOutput, calls=%fused_computation.8 | convolution fusion | flops 402653184 | bytes 4718592 | tf_op jit(solution)/shard_map/dot_general | solution.py:256
  20.9 0.0 copy-start.1
  20.9 5.1 %collective-permute-start.1 = (f32[64,1024]{1,0:T(8,128)S(1)}, f32[64,1024]{1,0:T(8,128)S(1)}, u32[]{:S(2)}, u32[]{:S(2)}) collective-permute-start(f32[64,1024]{1,0:T(8,128)S(1)} %fusion.8), channel_id=1, source_target_pairs={{0,1},{1,2},{2,3},{3,4},{4,5},{5,6},{6,7},{7,8},{8,9},{9,10},{10,1... | collective-permute-start | bytes 786440 | tf_op jit(solution)/shard_map/ppermute | solution.py:26
  26.0 4.2 %fusion.18 = f32[64,1024]{1,0:T(8,128)S(1)} fusion(f32[1,1024,1024]{2,1,0:T(8,128)} %param.9, f32[1,64,1024]{2,1,0:T(8,128)S(1)} %copy-done.8, f32[1,64,1024]{2,1,0:T(8,128)S(1)} %copy-done), kind=kOutput, calls=%fused_computation.18 | convolution fusion | flops 402718720 | bytes 4980736 | tf_op jit(solution)/shard_map/dot_general | solution.py:258
  30.2 4.8 %collective-permute-done.1 = f32[64,1024]{1,0:T(8,128)S(1)} collective-permute-done((f32[64,1024]{1,0:T(8,128)S(1)}, f32[64,1024]{1,0:T(8,128)S(1)}, u32[]{:S(2)}, u32[]{:S(2)}) %collective-permute-start.1) | collective-permute-done | bytes 262176 | tf_op jit(solution)/shard_map/ppermute | solution.py:26
  35.0 1.6 %collective-permute-done = f32[64,1024]{1,0:T(8,128)S(1)} collective-permute-done((f32[64,1024]{1,0:T(8,128)S(1)}, f32[64,1024]{1,0:T(8,128)S(1)}, u32[]{:S(2)}, u32[]{:S(2)}) %collective-permute-start) | collective-permute-done | bytes 262176 | tf_op jit(solution)/shard_map/ppermute | solution.py:26
  36.6 2.0 %fusion.24.base_ref = f32[64,1024]{1,0:T(8,128)S(1)} fusion(f32[64,1024]{1,0:T(8,128)S(1)} %fusion.18, f32[64,1024]{1,0:T(8,128)S(1)} %collective-permute-done.1, f32[64,1024]{1,0:T(8,128)S(1)} %collective-permute-done, f32[1,1024,1024]{2,1,0:T(8,128)S(1)} %copy-done.3), kind=kOutput, calls=%fused_computation.20 | convolution fusion | flops 402784256 | bytes 5242880 | tf_op jit(solution)/shard_map/dot_general | solution.py:260
  38.7 10.4 %turn.2 = (f32[64,1024]{1,0:T(8,128)S(1)}, f32[64,1024]{1,0:T(8,128)S(1)}, f32[32,48,128]{2,1,0:T(8,128)}) custom-call(s32[28]{0:T(128)S(1)} %bitcast.59, s32[28]{0:T(128)S(1)} %bitcast.63, f32[28,96,1024]{2,1,0:T(8,128)} %bitcast.67, f32[32,48,128]{2,1,0:T(8,128)S(1)} %all-to-all-done.incoming_ref, f32[64,1024]{1,0:T(8,128)S(1)} %fusion.24.base_ref, ...), custom_call_target="tpu_custom_call" | custom-call | flops 2818572288 | bytes 11010048 | tf_op jit(solution)/shard_map/turn/pallas_call | solution.py:241
  49.1 4.3 %all-to-all-start.1 = ((f32[32,48,128]{2,1,0:T(8,128)}), f32[32,48,128]{2,1,0:T(8,128)S(1)}, u32[]{:S(2)}, u32[]{:S(2)}) async-start(f32[32,48,128]{2,1,0:T(8,128)} %get-tuple-element.9), calls=%async_computation.1 | async-start | bytes 1572864 | tf_op jit(solution)/shard_map/all_to_all | solution.py:253
  53.4 2.7 %collective-permute-start.2 = (f32[64,1024]{1,0:T(8,128)S(1)}, f32[64,1024]{1,0:T(8,128)S(1)}, u32[]{:S(2)}, u32[]{:S(2)}) collective-permute-start(f32[64,1024]{1,0:T(8,128)S(1)} %get-tuple-element.8.previous_ref), channel_id=1, source_target_pairs={{1,0},{2,1},{3,2},{4,3},{5,4},{6,5},{7,6},{8,7},{9,8},{10,9},{11,1... | collective-permute-start | bytes 786440 | tf_op jit(solution)/shard_map/ppermute | solution.py:26
  56.1 3.6 %fusion.4 = f32[64,1024]{1,0:T(8,128)S(1)} fusion(f32[64,1024]{1,0:T(8,128)S(1)} %get-tuple-element.8.previous_ref, f32[1,1024,1024]{2,1,0:T(8,128)} %param.10), kind=kOutput, calls=%fused_computation.4 | convolution fusion | flops 402653184 | bytes 4718592 | tf_op jit(solution)/shard_map/dot_general | solution.py:256
  59.7 5.1 %collective-permute-start.3 = (f32[64,1024]{1,0:T(8,128)S(1)}, f32[64,1024]{1,0:T(8,128)S(1)}, u32[]{:S(2)}, u32[]{:S(2)}) collective-permute-start(f32[64,1024]{1,0:T(8,128)S(1)} %fusion.4), channel_id=1, source_target_pairs={{0,1},{1,2},{2,3},{3,4},{4,5},{5,6},{6,7},{7,8},{8,9},{9,10},{10,1... | collective-permute-start | bytes 786440 | tf_op jit(solution)/shard_map/ppermute | solution.py:26
  64.8 2.0 %fusion.14 = f32[64,1024]{1,0:T(8,128)S(1)} fusion(f32[64,1024]{1,0:T(8,128)S(1)} %get-tuple-element.8.previous_ref, f32[1,1024,1024]{2,1,0:T(8,128)S(1)} %copy-done.6), kind=kOutput, calls=%fused_computation.14 | convolution fusion | flops 402653184 | bytes 4718592 | tf_op jit(solution)/shard_map/dot_general | solution.py:258
  66.9 6.7 %collective-permute-done.3 = f32[64,1024]{1,0:T(8,128)S(1)} collective-permute-done((f32[64,1024]{1,0:T(8,128)S(1)}, f32[64,1024]{1,0:T(8,128)S(1)}, u32[]{:S(2)}, u32[]{:S(2)}) %collective-permute-start.3) | collective-permute-done | bytes 262176 | tf_op jit(solution)/shard_map/ppermute | solution.py:26
  73.6 1.6 %collective-permute-done.2 = f32[64,1024]{1,0:T(8,128)S(1)} collective-permute-done((f32[64,1024]{1,0:T(8,128)S(1)}, f32[64,1024]{1,0:T(8,128)S(1)}, u32[]{:S(2)}, u32[]{:S(2)}) %collective-permute-start.2) | collective-permute-done | bytes 262176 | tf_op jit(solution)/shard_map/ppermute | solution.py:26
  75.2 2.0 %fusion.30.base_ref = f32[64,1024]{1,0:T(8,128)S(1)} fusion(f32[64,1024]{1,0:T(8,128)S(1)} %sub.20, f32[64,1024]{1,0:T(8,128)S(1)} %collective-permute-done.3, f32[64,1024]{1,0:T(8,128)S(1)} %collective-permute-done.2, f32[1,1024,1024]{2,1,0:T(8,128)S(1)} %copy-done.4), kind=kOutput, calls=%fused_computation.22 | convolution fusion | flops 402784256 | bytes 5242880 | tf_op jit(solution)/shard_map/dot_general | solution.py:260
  77.3 10.4 %turn.3 = (f32[64,1024]{1,0:T(8,128)S(1)}, f32[64,1024]{1,0:T(8,128)S(1)}, f32[32,48,128]{2,1,0:T(8,128)}) custom-call(s32[28]{0:T(128)S(1)} %bitcast.60, s32[28]{0:T(128)S(1)} %bitcast.64, f32[28,96,1024]{2,1,0:T(8,128)} %bitcast.68, f32[32,48,128]{2,1,0:T(8,128)S(1)} %all-to-all-done.1.incoming_ref, f32[64,1024]{1,0:T(8,128)S(1)} %fusion.30.base_ref, ...), custom_call_target="tpu_custom_call" | custom-call | flops 2818572288 | bytes 11010048 | tf_op jit(solution)/shard_map/turn/pallas_call | solution.py:241
  87.7 4.3 %all-to-all-start.2 = ((f32[32,48,128]{2,1,0:T(8,128)}), f32[32,48,128]{2,1,0:T(8,128)S(1)}, u32[]{:S(2)}, u32[]{:S(2)}) async-start(f32[32,48,128]{2,1,0:T(8,128)} %get-tuple-element.12), calls=%async_computation.2 | async-start | bytes 1572864 | tf_op jit(solution)/shard_map/all_to_all | solution.py:253
  92.0 2.6 %collective-permute-start.4 = (f32[64,1024]{1,0:T(8,128)S(1)}, f32[64,1024]{1,0:T(8,128)S(1)}, u32[]{:S(2)}, u32[]{:S(2)}) collective-permute-start(f32[64,1024]{1,0:T(8,128)S(1)} %get-tuple-element.11.previous_ref), channel_id=1, source_target_pairs={{1,0},{2,1},{3,2},{4,3},{5,4},{6,5},{7,6},{8,7},{9,8},{10,9},{11,1... | collective-permute-start | bytes 786440 | tf_op jit(solution)/shard_map/ppermute | solution.py:26
  94.5 3.6 %fusion = f32[64,1024]{1,0:T(8,128)S(1)} fusion(f32[64,1024]{1,0:T(8,128)S(1)} %get-tuple-element.11.previous_ref, f32[1,1024,1024]{2,1,0:T(8,128)} %param.10), kind=kOutput, calls=%fused_computation | convolution fusion | flops 402653184 | bytes 4718592 | tf_op jit(solution)/shard_map/dot_general | solution.py:256
  98.2 5.3 %collective-permute-start.5 = (f32[64,1024]{1,0:T(8,128)S(1)}, f32[64,1024]{1,0:T(8,128)S(1)}, u32[]{:S(2)}, u32[]{:S(2)}) collective-permute-start(f32[64,1024]{1,0:T(8,128)S(1)} %fusion), channel_id=1, source_target_pairs={{0,1},{1,2},{2,3},{3,4},{4,5},{5,6},{6,7},{7,8},{8,9},{9,10},{10,1... | collective-permute-start | bytes 786440 | tf_op jit(solution)/shard_map/ppermute | solution.py:26
  103.5 2.0 %fusion.12 = f32[64,1024]{1,0:T(8,128)S(1)} fusion(f32[64,1024]{1,0:T(8,128)S(1)} %get-tuple-element.11.previous_ref, f32[1,1024,1024]{2,1,0:T(8,128)S(1)} %copy-done.7), kind=kOutput, calls=%fused_computation.12 | convolution fusion | flops 402653184 | bytes 4718592 | tf_op jit(solution)/shard_map/dot_general | solution.py:258
  105.6 0.8 add_bitcast_fusion
  106.3 5.9 %collective-permute-done.5 = f32[64,1024]{1,0:T(8,128)S(1)} collective-permute-done((f32[64,1024]{1,0:T(8,128)S(1)}, f32[64,1024]{1,0:T(8,128)S(1)}, u32[]{:S(2)}, u32[]{:S(2)}) %collective-permute-start.5) | collective-permute-done | bytes 262176 | tf_op jit(solution)/shard_map/ppermute | solution.py:26
  112.2 1.6 %collective-permute-done.4 = f32[64,1024]{1,0:T(8,128)S(1)} collective-permute-done((f32[64,1024]{1,0:T(8,128)S(1)}, f32[64,1024]{1,0:T(8,128)S(1)}, u32[]{:S(2)}, u32[]{:S(2)}) %collective-permute-start.4) | collective-permute-done | bytes 262176 | tf_op jit(solution)/shard_map/ppermute | solution.py:26
  113.8 2.0 %fusion.36.base_ref = f32[64,1024]{1,0:T(8,128)S(1)} fusion(f32[64,1024]{1,0:T(8,128)S(1)} %sub.22, f32[64,1024]{1,0:T(8,128)S(1)} %collective-permute-done.5, f32[64,1024]{1,0:T(8,128)S(1)} %collective-permute-done.4, f32[1,1024,1024]{2,1,0:T(8,128)S(1)} %copy-done.5), kind=kOutput, calls=%fused_computation.24 | convolution fusion | flops 402784256 | bytes 5242880 | tf_op jit(solution)/shard_map/dot_general | solution.py:260
  115.9 6.1 %far.1 = f32[64,1024]{1,0:T(8,128)} custom-call(s32[28]{0:T(128)S(1)} %bitcast.61, s32[28]{0:T(128)S(1)} %bitcast.65, f32[28,96,1024]{2,1,0:T(8,128)} %bitcast.69, f32[32,48,128]{2,1,0:T(8,128)S(1)} %all-to-all-done.2.incoming_ref, f32[64,1024]{1,0:T(8,128)S(1)} %fusion.36.base_ref, f32[64,1024]{1,0:T(8,128)S(1)} %get-tuple-element.11.previous_ref), custom_call_target="tpu_custom_call" | custom-call | flops 1409286144 | bytes 11010048 | tf_op jit(solution)/shard_map/far/pallas_call | solution.py:241
  (20 shorter events, 0.1 us)
Async XLA Ops:
  0.6 14.1 %copy-start = (f32[1,64,1024]{2,1,0:T(8,128)S(1)}, f32[1,64,1024]{2,1,0:T(8,128)}, u32[]{:S(2)}) copy-start(f32[1,64,1024]{2,1,0:T(8,128)} %param.8) | copy-start | bytes 786436
  8.4 17.6 %copy-start.8 = (f32[1,64,1024]{2,1,0:T(8,128)S(1)}, f32[1,64,1024]{2,1,0:T(8,128)}, u32[]{:S(2)}) copy-start(f32[1,64,1024]{2,1,0:T(8,128)} %param.7) | copy-start | bytes 786436
  8.4 30.2 %all-to-all-start = ((f32[32,48,128]{2,1,0:T(8,128)}), f32[32,48,128]{2,1,0:T(8,128)S(1)}, u32[]{:S(2)}, u32[]{:S(2)}) async-start(f32[32,48,128]{2,1,0:T(8,128)} %project.1), calls=%async_computation | async-start | bytes 1572864 | tf_op jit(solution)/shard_map/all_to_all | solution.py:253
  14.7 21.9 %copy-start.3 = (f32[1,1024,1024]{2,1,0:T(8,128)S(1)}, f32[1,1024,1024]{2,1,0:T(8,128)}, u32[]{:S(2)}) copy-start(f32[1,1024,1024]{2,1,0:T(8,128)} %param.10) | copy-start | bytes 12582916
  14.7 21.9 %collective-permute-start = (f32[64,1024]{1,0:T(8,128)S(1)}, f32[64,1024]{1,0:T(8,128)S(1)}, u32[]{:S(2)}, u32[]{:S(2)}) collective-permute-start(f32[64,1024]{1,0:T(8,128)S(1)} %bitcast.56), channel_id=1, source_target_pairs={{1,0},{2,1},{3,2},{4,3},{5,4},{6,5},{7,6},{8,7},{9,8},{10,9},{11,1... | collective-permute-start | bytes 786440 | tf_op jit(solution)/shard_map/ppermute | solution.py:26
  20.9 17.7 %copy-start.1 = (s32[1,28]{1,0:T(1,128)S(1)}, s32[1,28]{1,0:T(1,128)}, u32[]{:S(2)}) copy-start(s32[1,28]{1,0:T(1,128)} %param.12) | copy-start | bytes 340
  20.9 17.7 %copy-start.2 = (s32[1,28]{1,0:T(1,128)S(1)}, s32[1,28]{1,0:T(1,128)}, u32[]{:S(2)}) copy-start(s32[1,28]{1,0:T(1,128)} %param.13) | copy-start | bytes 340
  20.9 14.1 %collective-permute-start.1 = (f32[64,1024]{1,0:T(8,128)S(1)}, f32[64,1024]{1,0:T(8,128)S(1)}, u32[]{:S(2)}, u32[]{:S(2)}) collective-permute-start(f32[64,1024]{1,0:T(8,128)S(1)} %fusion.8), channel_id=1, source_target_pairs={{0,1},{1,2},{2,3},{3,4},{4,5},{5,6},{6,7},{7,8},{8,9},{9,10},{10,1... | collective-permute-start | bytes 786440 | tf_op jit(solution)/shard_map/ppermute | solution.py:26
  49.1 28.2 %all-to-all-start.1 = ((f32[32,48,128]{2,1,0:T(8,128)}), f32[32,48,128]{2,1,0:T(8,128)S(1)}, u32[]{:S(2)}, u32[]{:S(2)}) async-start(f32[32,48,128]{2,1,0:T(8,128)} %get-tuple-element.9), calls=%async_computation.1 | async-start | bytes 1572864 | tf_op jit(solution)/shard_map/all_to_all | solution.py:253
  53.3 11.5 %copy-start.6 = (f32[1,1024,1024]{2,1,0:T(8,128)S(1)}, f32[1,1024,1024]{2,1,0:T(8,128)}, u32[]{:S(2)}) copy-start(f32[1,1024,1024]{2,1,0:T(8,128)} %param.9) | copy-start | bytes 12582916
  53.3 21.9 %copy-start.4 = (f32[1,1024,1024]{2,1,0:T(8,128)S(1)}, f32[1,1024,1024]{2,1,0:T(8,128)}, u32[]{:S(2)}) copy-start(f32[1,1024,1024]{2,1,0:T(8,128)} %param.10) | copy-start | bytes 12582916
  53.4 21.9 %collective-permute-start.2 = (f32[64,1024]{1,0:T(8,128)S(1)}, f32[64,1024]{1,0:T(8,128)S(1)}, u32[]{:S(2)}, u32[]{:S(2)}) collective-permute-start(f32[64,1024]{1,0:T(8,128)S(1)} %get-tuple-element.8.previous_ref), channel_id=1, source_target_pairs={{1,0},{2,1},{3,2},{4,3},{5,4},{6,5},{7,6},{8,7},{9,8},{10,9},{11,1... | collective-permute-start | bytes 786440 | tf_op jit(solution)/shard_map/ppermute | solution.py:26
  59.7 13.9 %collective-permute-start.3 = (f32[64,1024]{1,0:T(8,128)S(1)}, f32[64,1024]{1,0:T(8,128)S(1)}, u32[]{:S(2)}, u32[]{:S(2)}) collective-permute-start(f32[64,1024]{1,0:T(8,128)S(1)} %fusion.4), channel_id=1, source_target_pairs={{0,1},{1,2},{2,3},{3,4},{4,5},{5,6},{6,7},{7,8},{8,9},{9,10},{10,1... | collective-permute-start | bytes 786440 | tf_op jit(solution)/shard_map/ppermute | solution.py:26
  87.7 28.2 %all-to-all-start.2 = ((f32[32,48,128]{2,1,0:T(8,128)}), f32[32,48,128]{2,1,0:T(8,128)S(1)}, u32[]{:S(2)}, u32[]{:S(2)}) async-start(f32[32,48,128]{2,1,0:T(8,128)} %get-tuple-element.12), calls=%async_computation.2 | async-start | bytes 1572864 | tf_op jit(solution)/shard_map/all_to_all | solution.py:253
  91.9 11.5 %copy-start.7 = (f32[1,1024,1024]{2,1,0:T(8,128)S(1)}, f32[1,1024,1024]{2,1,0:T(8,128)}, u32[]{:S(2)}) copy-start(f32[1,1024,1024]{2,1,0:T(8,128)} %param.9) | copy-start | bytes 12582916
  92.0 21.9 %collective-permute-start.4 = (f32[64,1024]{1,0:T(8,128)S(1)}, f32[64,1024]{1,0:T(8,128)S(1)}, u32[]{:S(2)}, u32[]{:S(2)}) collective-permute-start(f32[64,1024]{1,0:T(8,128)S(1)} %get-tuple-element.11.previous_ref), channel_id=1, source_target_pairs={{1,0},{2,1},{3,2},{4,3},{5,4},{6,5},{7,6},{8,7},{9,8},{10,9},{11,1... | collective-permute-start | bytes 786440 | tf_op jit(solution)/shard_map/ppermute | solution.py:26
  98.1 15.7 %copy-start.5 = (f32[1,1024,1024]{2,1,0:T(8,128)S(1)}, f32[1,1024,1024]{2,1,0:T(8,128)}, u32[]{:S(2)}) copy-start(f32[1,1024,1024]{2,1,0:T(8,128)} %param.10) | copy-start | bytes 12582916
  98.2 14.1 %collective-permute-start.5 = (f32[64,1024]{1,0:T(8,128)S(1)}, f32[64,1024]{1,0:T(8,128)S(1)}, u32[]{:S(2)}, u32[]{:S(2)}) collective-permute-start(f32[64,1024]{1,0:T(8,128)S(1)} %fusion), channel_id=1, source_target_pairs={{0,1},{1,2},{2,3},{3,4},{4,5},{5,6},{6,7},{7,8},{8,9},{9,10},{10,1... | collective-permute-start | bytes 786440 | tf_op jit(solution)/shard_map/ppermute | solution.py:26

commit v3 on v2

--- a/solution.py
+++ b/solution.py
@@ -36,69 +36,86 @@
     return lax.dot_general(left, right, form, preferred_element_type=jnp.float32)
 
 
-class Columns:
-    def __init__(self, factors_ref, buffer, semaphore, split_ref):
-        self.factors_ref, self.buffer = factors_ref, buffer
+def cuts(rows, parts):
+    edges = [rows * part // parts // 256 * 256 for part in range(parts)] + [rows]
+    return [(first, last) for first, last in zip(edges, edges[1:]) if last > first]
+
+
+class Pieces:
+    def __init__(self, rectangles, factors_ref, buffer, semaphore, split_ref):
+        self.rectangles, self.factors_ref, self.buffer = rectangles, factors_ref, buffer
         self.semaphore, self.split_ref = semaphore, split_ref
-        self.count, self.slots, self.width, self.size = buffer.shape
-
-    def block(self, index):
-        return pl.ds(pl.multiple_of(index * self.size, self.size), self.size)
 
     def copy(self, index):
+        rows, columns = (slice(*edges) for edges in self.rectangles[index])
         return pltpu.make_async_copy(
-            self.factors_ref.at[:, :, self.block(index)], self.buffer.at[index],
+            self.factors_ref.at[rows, columns], self.buffer.at[rows, columns],
             self.semaphore.at[index],
         )
 
     def start(self):
-        for index in range(self.count):
+        for index in range(len(self.rectangles)):
             self.copy(index).start()
 
     def load(self, index):
         self.copy(index).wait()
-        values = self.buffer[index].reshape(self.slots * self.width, self.size)
-        self.split_ref[:, :self.size], self.split_ref[:, self.size:] = halves(values)
-
-    def far(self, turned_ref):
-        total = product(turned_ref[...], self.split_ref[...], NN)
+        rows, columns = (slice(*edges) for edges in self.rectangles[index])
+        high, low = halves(self.buffer[rows, columns])
+        width = high.shape[1]
+        self.split_ref[rows, :width], self.split_ref[rows, width:2 * width] = high, low
+
+    def far(self, index, turned_ref):
+        (first, last), (left, right) = self.rectangles[index]
+        width = right - left
+        total = product(turned_ref[:, first:last], self.split_ref[first:last, :2 * width], NN)
         n = total.shape[0] // 2
         total = total[:n] + total[n:]
-        return total[:, :self.size] + total[:, self.size:]
-
-    def project(self, vectors, sums_ref):
-        operand = jnp.concatenate(halves(vectors), axis=0)
-        operand = jnp.concatenate([operand, operand], axis=1)
-        sums_ref[...] += product(self.split_ref[...], operand, NT)
-
-
-def each_slot(slots, visit):
-    together = next(size for size in (7, 4, 2, 1) if slots % size == 0)
-
-    @pl.loop(0, slots // together)
-    def _(group):
-        for inner in range(together):
-            visit(group * together + inner)
-
-
-def store_chunks(width, sums_ref, partner_ref, ranks_ref, outgoing_ref):
+        return total[:, :width] + total[:, width:]
+
+
+def operand_of(vectors):
+    operand = jnp.concatenate(halves(vectors), axis=0).T
+    return jnp.concatenate([operand, operand], axis=0)
+
+
+def project(split_ref, vectors, sums_ref, first):
+    total = product(split_ref[:, :2 * vectors.shape[1]], operand_of(vectors), NN)
+    sums_ref[...] = total if first else sums_ref[...] + total
+
+
+def project_last(split_ref, vectors, sums_ref, width, partner_ref, ranks_ref, outgoing_ref):
+    operand = operand_of(vectors)
     rows, lanes = sums_ref.shape
     half = width // 2
     own = lax.axis_index(AXES)
     left = lax.broadcasted_iota(jnp.int32, (half, lanes), 1) < lanes // 2
     rank_index = lax.broadcasted_iota(jnp.int32, (half, lanes), 0) + jnp.where(left, 0, half)
-
-    def visit(slot):
-        base = pl.multiple_of(slot * width, 16)
-        top = sums_ref[pl.ds(base, half), :]
-        bottom = sums_ref[pl.ds(base + half, half), :]
-        top = top + pltpu.roll(top, lanes // 2, 1)
-        bottom = bottom + pltpu.roll(bottom, lanes // 2, 1)
-        chunk = jnp.where(rank_index < ranks_ref[slot], jnp.where(left, top, bottom), 0.0)
-        place = partner_ref[slot]
-        outgoing_ref[jnp.where(place >= 0, place, own)] = chunk
-
-    each_slot(rows // width, visit)
+    slots = rows // width
+    together = -(-slots // 4)
+    for at in range(0, slots, together):
+        end = min(at + together, slots)
+        some = slice(at * width, end * width)
+        total = sums_ref[some, :] + product(split_ref[some, :operand.shape[0]], operand, NN)
+        total = total + pltpu.roll(total, lanes // 2, 1)
+        for slot in range(at, end):
+            base = (slot - at) * width
+            chunk = jnp.where(left, total[base:base + half], total[base + half:base + width])
+            chunk = jnp.where(rank_index < ranks_ref[slot], chunk, 0.0)
+            place = partner_ref[slot]
+            outgoing_ref[jnp.where(place >= 0, place, own)] = chunk
+
+
+def apart(partner_ref):
+    return pl.when(partner_ref[0] >= -1)
+
+
+def each_slot(slots, visit):
+    together = next(size for size in (7, 4, 2, 1) if slots % size == 0)
+
+    @pl.loop(0, slots // together)
+    def _(group):
+        for inner in range(together):
+            visit(group * together + inner)
 
 
 def unpack(width, slots, partner_ref, incoming_ref, received_ref):
@@ -120,8 +137,8 @@
     each_slot(slots, visit)
 
 
-def project_kernel(partner_hbm, ranks_hbm, vectors_hbm, factors_ref, outgoing_ref,
-                   buffer, semaphore, split_ref, sums_ref, partner_ref, ranks_ref,
+def project_kernel(rectangles, width, partner_hbm, ranks_hbm, vectors_hbm, factors_ref,
+                   outgoing_ref, buffer, semaphore, split_ref, sums_ref, partner_ref, ranks_ref,
                    vectors_ref, small_semaphore):
     small = [
         pltpu.make_async_copy(source, target, small_semaphore.at[index])
@@ -131,51 +148,57 @@
     ]
     for copy in small:
         copy.start()
-    columns = Columns(factors_ref, buffer, semaphore, split_ref)
-    columns.start()
-    sums_ref[...] = jnp.zeros_like(sums_ref)
+    pieces = Pieces(rectangles, factors_ref, buffer, semaphore, split_ref)
+    pieces.start()
     for copy in small:
         copy.wait()
-
-    @pl.loop(0, columns.count)
-    def _(index):
-        columns.load(index)
-        columns.project(vectors_ref[:, columns.block(index)], sums_ref)
-
-    store_chunks(columns.width, sums_ref, partner_ref, ranks_ref, outgoing_ref)
-
-
-def turn_kernel(weights, partner_ref, ranks_ref, factors_ref, incoming_ref, base_ref,
-                previous_ref, *rest):
+    for index, (_, columns) in enumerate(rectangles):
+        @apart(partner_ref)
+        def _():
+            pieces.load(index)
+            vectors = vectors_ref[:, slice(*columns)]
+            if index + 1 < len(rectangles):
+                project(split_ref, vectors, sums_ref, index == 0)
+            else:
+                project_last(
+                    split_ref, vectors, sums_ref, width, partner_ref, ranks_ref, outgoing_ref
+                )
+
+
+def turn_kernel(weights, rectangles, width, partner_ref, ranks_ref, factors_ref, incoming_ref,
+                base_ref, previous_ref, *rest):
     if weights is None:
         residual_ref, *rest = rest
         buffer, semaphore, split_ref, received_ref, turned_ref = rest
     else:
         residual_ref, direction_ref, outgoing_ref, *rest = rest
         buffer, semaphore, split_ref, received_ref, turned_ref, sums_ref = rest
-    columns = Columns(factors_ref, buffer, semaphore, split_ref)
-    columns.start()
-    unpack(columns.width, columns.slots, partner_ref, incoming_ref, received_ref)
+    pieces = Pieces(rectangles, factors_ref, buffer, semaphore, split_ref)
+    pieces.start()
+    unpack(width, factors_ref.shape[0] // width, partner_ref, incoming_ref, received_ref)
     turned_ref[...] = received_ref[...].T
-    if weights is not None:
-        sums_ref[...] = jnp.zeros_like(sums_ref)
-
-    @pl.loop(0, columns.count)
-    def _(index):
-        columns.load(index)
-        block = columns.block(index)
-        residual = base_ref[:, block] - columns.far(turned_ref)
-        residual_ref[:, block] = residual
-        if weights is not None:
+    rows = factors_ref.shape[0]
+    for index, ((first, last), columns) in enumerate(rectangles):
+        @apart(partner_ref)
+        def _():
+            block = slice(*columns)
+            pieces.load(index)
+            before = base_ref if first == 0 else residual_ref
+            residual = before[:, block] - pieces.far(index, turned_ref)
+            residual_ref[:, block] = residual
+            if weights is None or last < rows:
+                return
             old, new = weights
             direction = new * residual
             if old is not None:
                 direction = old * previous_ref[:, block] + direction
             direction_ref[:, block] = direction
-            columns.project(direction, sums_ref)
-
-    if weights is not None:
-        store_chunks(columns.width, sums_ref, partner_ref, ranks_ref, outgoing_ref)
+            if index + 1 < len(rectangles):
+                project(split_ref, direction, sums_ref, columns[0] == 0)
+            else:
+                project_last(
+                    split_ref, direction, sums_ref, width, partner_ref, ranks_ref, outgoing_ref
+                )
 
 
 SMEM_SPEC = pl.BlockSpec(memory_space=pltpu.SMEM)
@@ -188,17 +211,23 @@
     right_side, start = right_side[0], start[0]
     diag_block, neighbour_block, factor_block = diag_tiles[0], neighbour_tiles[0], factors[0]
     partner, ranks = partner[0], ranks[0]
-    factor_block = pltpu.with_memory_space_constraint(factor_block, pltpu.HBM)
     slots, rank_width, points = factor_block.shape
     n = start.shape[0]
     rows = slots * rank_width
     block = jax.ShapeDtypeStruct((n, points), jnp.float32)
     chunks = jax.ShapeDtypeStruct((device_count, rank_width // 2, 2 * n), jnp.float32)
-    def loading(blocks):
+    factor_block = factor_block.reshape(rows, points)
+    factor_block = pltpu.with_memory_space_constraint(factor_block, pltpu.HBM)
+    middle, quarter = points // 2, points // 4
+    by_columns = [((0, rows), (at, at + quarter)) for at in range(0, points, quarter)]
+    by_halves = [(part, (0, middle)) for part in cuts(rows, 2)] + [((0, rows), (middle, points))]
+
+    def loading(rectangles):
+        width = max(right - left for _, (left, right) in rectangles)
         return [
-            pltpu.VMEM((blocks, slots, rank_width, points // blocks), jnp.float32),
-            pltpu.SemaphoreType.DMA((blocks,)),
-            pltpu.VMEM((rows, 2 * points // blocks), jnp.bfloat16),
+            pltpu.VMEM((rows, points), jnp.float32),
+            pltpu.SemaphoreType.DMA((len(rectangles),)),
+            pltpu.VMEM((rows, 2 * width), jnp.bfloat16),
         ]
 
     received = [
@@ -219,11 +248,11 @@
 
     def projected(vectors):
         return pl.pallas_call(
-            project_kernel,
+            functools.partial(project_kernel, by_columns, rank_width),
             out_shape=chunks,
             in_specs=[ANY_SPEC] * 4,
             out_specs=VMEM_SPEC,
-            scratch_shapes=loading(4) + [
+            scratch_shapes=loading(by_columns) + [
                 sums,
                 pltpu.SMEM((slots,), jnp.int32),
                 pltpu.SMEM((slots,), jnp.int32),
@@ -237,13 +266,14 @@
 
     def turn(weights, incoming, base, previous):
         last = weights is None
+        rectangles = by_columns if last else by_halves
         outs = (block,) if last else (block, block, chunks)
         return pl.pallas_call(
-            functools.partial(turn_kernel, weights),
+            functools.partial(turn_kernel, weights, rectangles, rank_width),
             out_shape=outs,
             in_specs=[SMEM_SPEC, SMEM_SPEC, ANY_SPEC] + [VMEM_SPEC] * 3,
             out_specs=(VMEM_SPEC,) * len(outs),
-            scratch_shapes=loading(4 if last else 2) + received + ([] if last else [sums]),
+            scratch_shapes=loading(rectangles) + received + ([] if last else [sums]),
             compiler_params=params,
             cost_estimate=cost(1 if last else 2),
             name="far" if last else "turn",

time: 124 us -> 122 us (0.984)
  Pallas kernels: 34.7 us -> 33 us
    pallas_call x4, Pallas kernels: 34.7 us -> 33 us  [the longest x3 25.6 us: turn(): pl.pallas_call(functools.partial(turn_kernel, weights, rectangles, rank_w...]
  transfers between devices with their start and end apart: 9 -> 9, of which waited for: 6 -> 6; matrix products, arithmetic and copies ran while one was open for 21% -> 22% of each run, Pallas kernels for 0% -> 0%
where the time goes in v3:
time: 122 us; the launch traced here: 121 us
  starting transfers between devices  37.9 us (31%)
  Pallas kernels  33 us (27%)
  matrix products  25.3 us (21%)
  waiting for transfers between devices  22.4 us (18%)
    pallas_call x3, Pallas kernels, turn(): pl.pallas_call(functools.partial(turn_kernel, weights, rectangles, rank_w...  25.6 us
    ppermute x6, starting transfers between devices, from_behind(): return lax.ppermute(block, AXES, route)  23.1 us
    ppermute x6, waiting for transfers between devices, from_behind(): return lax.ppermute(block, AXES, route)  22.4 us
    all_to_all x3, starting transfers between devices, finish(): lax.all_to_all(outgoing, AXES, split_axis=0, concat_axis=0, tiled=True)  14.8 us
    dot_general x3, matrix products, finish(): carried = lax.dot_general(vectors, neighbour_block, NN, precision=exact)  10.8 us
    dot_general x3, matrix products, finish(): partial = before - lax.dot_general(vectors, diag_block, NT, precision=exact)  8.32 us
    pallas_call x1, Pallas kernels, projected(): pl.pallas_call(functools.partial(project_kernel, by_columns, rank_width),...  7.42 us
    dot_general x3, matrix products, finish(): lax.dot_general(following, neighbour_block, NT, precision=exact)  6.14 us
  transfers between devices with their start and end apart: 9, of which 6 were waited for; matrix products, arithmetic and copies ran while one was open for 22% of the time, Pallas kernels for 0%

profile of v3, /device:TPU:15, one launch (start us, length us, event | category | flops | bytes accessed | tf_op | source)
XLA Modules:
  0.0 120.5 jit_solution(11150577207392778378)
XLA Ops:
  0.6 7.4 %project.1 = f32[32,48,128]{2,1,0:T(8,128)} custom-call(s32[28]{0:T(128)} %bitcast.58, s32[28]{0:T(128)} %bitcast.62, f32[64,1024]{1,0:T(8,128)} %bitcast.55, f32[2688,1024]{1,0:T(8,128)} %bitcast.66), custom_call_target="tpu_custom_call" | custom-call | flops 1409286144 | bytes 11010048 | tf_op jit(solution)/shard_map/project/pallas_call | solution.py:250
  8.1 6.2 %all-to-all-start = ((f32[32,48,128]{2,1,0:T(8,128)}), f32[32,48,128]{2,1,0:T(8,128)S(1)}, u32[]{:S(2)}, u32[]{:S(2)}) async-start(f32[32,48,128]{2,1,0:T(8,128)} %project.1), calls=%async_computation | async-start | bytes 1572864 | tf_op jit(solution)/shard_map/all_to_all | solution.py:283
  14.3 0.0 copy-start.3
  14.4 2.6 %collective-permute-start = (f32[64,1024]{1,0:T(8,128)S(1)}, f32[64,1024]{1,0:T(8,128)S(1)}, u32[]{:S(2)}, u32[]{:S(2)}) collective-permute-start(f32[64,1024]{1,0:T(8,128)S(1)} %bitcast.56), channel_id=1, source_target_pairs={{1,0},{2,1},{3,2},{4,3},{5,4},{6,5},{7,6},{8,7},{9,8},{10,9},{11,1... | collective-permute-start | bytes 786440 | tf_op jit(solution)/shard_map/ppermute | solution.py:26
  16.9 3.6 %fusion.8 = f32[64,1024]{1,0:T(8,128)S(1)} fusion(f32[1,1024,1024]{2,1,0:T(8,128)} %param.10, f32[1,64,1024]{2,1,0:T(8,128)S(1)} %copy-done), kind=kOutput, calls=%fused_computation.8 | convolution fusion | flops 402653184 | bytes 4718592 | tf_op jit(solution)/shard_map/dot_general | solution.py:286
  20.6 0.0 copy-start.2
  20.6 5.1 %collective-permute-start.1 = (f32[64,1024]{1,0:T(8,128)S(1)}, f32[64,1024]{1,0:T(8,128)S(1)}, u32[]{:S(2)}, u32[]{:S(2)}) collective-permute-start(f32[64,1024]{1,0:T(8,128)S(1)} %fusion.8), channel_id=1, source_target_pairs={{0,1},{1,2},{2,3},{3,4},{4,5},{5,6},{6,7},{7,8},{8,9},{9,10},{10,1... | collective-permute-start | bytes 786440 | tf_op jit(solution)/shard_map/ppermute | solution.py:26
  25.7 4.2 %fusion.18 = f32[64,1024]{1,0:T(8,128)S(1)} fusion(f32[1,1024,1024]{2,1,0:T(8,128)} %param.9, f32[1,64,1024]{2,1,0:T(8,128)S(1)} %copy-done.8, f32[1,64,1024]{2,1,0:T(8,128)S(1)} %copy-done), kind=kOutput, calls=%fused_computation.18 | convolution fusion | flops 402718720 | bytes 4980736 | tf_op jit(solution)/shard_map/dot_general | solution.py:288
  29.9 4.8 %collective-permute-done.1 = f32[64,1024]{1,0:T(8,128)S(1)} collective-permute-done((f32[64,1024]{1,0:T(8,128)S(1)}, f32[64,1024]{1,0:T(8,128)S(1)}, u32[]{:S(2)}, u32[]{:S(2)}) %collective-permute-start.1) | collective-permute-done | bytes 262176 | tf_op jit(solution)/shard_map/ppermute | solution.py:26
  34.6 1.6 %collective-permute-done = f32[64,1024]{1,0:T(8,128)S(1)} collective-permute-done((f32[64,1024]{1,0:T(8,128)S(1)}, f32[64,1024]{1,0:T(8,128)S(1)}, u32[]{:S(2)}, u32[]{:S(2)}) %collective-permute-start) | collective-permute-done | bytes 262176 | tf_op jit(solution)/shard_map/ppermute | solution.py:26
  36.2 2.0 %fusion.24.base_ref = f32[64,1024]{1,0:T(8,128)S(1)} fusion(f32[64,1024]{1,0:T(8,128)S(1)} %fusion.18, f32[64,1024]{1,0:T(8,128)S(1)} %collective-permute-done.1, f32[64,1024]{1,0:T(8,128)S(1)} %collective-permute-done, f32[1,1024,1024]{2,1,0:T(8,128)S(1)} %copy-done.3), kind=kOutput, calls=%fused_computation.20 | convolution fusion | flops 402784256 | bytes 5242880 | tf_op jit(solution)/shard_map/dot_general | solution.py:290
  38.3 9.7 %turn.2 = (f32[64,1024]{1,0:T(8,128)S(1)}, f32[64,1024]{1,0:T(8,128)S(1)}, f32[32,48,128]{2,1,0:T(8,128)}) custom-call(s32[28]{0:T(128)S(1)} %bitcast.59, s32[28]{0:T(128)S(1)} %bitcast.63, f32[2688,1024]{1,0:T(8,128)} %bitcast.67, f32[32,48,128]{2,1,0:T(8,128)S(1)} %all-to-all-done.incoming_ref, f32[64,1024]{1,0:T(8,128)S(1)} %fusion.24.base_ref, ...), custom_call_target="tpu_custom_call" | custom-call | flops 2818572288 | bytes 11010048 | tf_op jit(solution)/shard_map/turn/pallas_call | solution.py:271
  48.0 4.3 %all-to-all-start.1 = ((f32[32,48,128]{2,1,0:T(8,128)}), f32[32,48,128]{2,1,0:T(8,128)S(1)}, u32[]{:S(2)}, u32[]{:S(2)}) async-start(f32[32,48,128]{2,1,0:T(8,128)} %get-tuple-element.9), calls=%async_computation.1 | async-start | bytes 1572864 | tf_op jit(solution)/shard_map/all_to_all | solution.py:283
  52.3 0.0 copy-start.4
  52.3 2.7 %collective-permute-start.2 = (f32[64,1024]{1,0:T(8,128)S(1)}, f32[64,1024]{1,0:T(8,128)S(1)}, u32[]{:S(2)}, u32[]{:S(2)}) collective-permute-start(f32[64,1024]{1,0:T(8,128)S(1)} %get-tuple-element.8.previous_ref), channel_id=1, source_target_pairs={{1,0},{2,1},{3,2},{4,3},{5,4},{6,5},{7,6},{8,7},{9,8},{10,9},{11,1... | collective-permute-start | bytes 786440 | tf_op jit(solution)/shard_map/ppermute | solution.py:26
  55.0 3.6 %fusion.4 = f32[64,1024]{1,0:T(8,128)S(1)} fusion(f32[64,1024]{1,0:T(8,128)S(1)} %get-tuple-element.8.previous_ref, f32[1,1024,1024]{2,1,0:T(8,128)} %param.10), kind=kOutput, calls=%fused_computation.4 | convolution fusion | flops 402653184 | bytes 4718592 | tf_op jit(solution)/shard_map/dot_general | solution.py:286
  58.7 4.9 %collective-permute-start.3 = (f32[64,1024]{1,0:T(8,128)S(1)}, f32[64,1024]{1,0:T(8,128)S(1)}, u32[]{:S(2)}, u32[]{:S(2)}) collective-permute-start(f32[64,1024]{1,0:T(8,128)S(1)} %fusion.4), channel_id=1, source_target_pairs={{0,1},{1,2},{2,3},{3,4},{4,5},{5,6},{6,7},{7,8},{8,9},{9,10},{10,1... | collective-permute-start | bytes 786440 | tf_op jit(solution)/shard_map/ppermute | solution.py:26
  63.6 2.0 %fusion.14 = f32[64,1024]{1,0:T(8,128)S(1)} fusion(f32[64,1024]{1,0:T(8,128)S(1)} %get-tuple-element.8.previous_ref, f32[1,1024,1024]{2,1,0:T(8,128)S(1)} %copy-done.6), kind=kOutput, calls=%fused_computation.14 | convolution fusion | flops 402653184 | bytes 4718592 | tf_op jit(solution)/shard_map/dot_general | solution.py:288
  65.7 6.9 %collective-permute-done.3 = f32[64,1024]{1,0:T(8,128)S(1)} collective-permute-done((f32[64,1024]{1,0:T(8,128)S(1)}, f32[64,1024]{1,0:T(8,128)S(1)}, u32[]{:S(2)}, u32[]{:S(2)}) %collective-permute-start.3) | collective-permute-done | bytes 262176 | tf_op jit(solution)/shard_map/ppermute | solution.py:26
  72.6 1.6 %collective-permute-done.2 = f32[64,1024]{1,0:T(8,128)S(1)} collective-permute-done((f32[64,1024]{1,0:T(8,128)S(1)}, f32[64,1024]{1,0:T(8,128)S(1)}, u32[]{:S(2)}, u32[]{:S(2)}) %collective-permute-start.2) | collective-permute-done | bytes 262176 | tf_op jit(solution)/shard_map/ppermute | solution.py:26
  74.2 2.0 %fusion.30.base_ref = f32[64,1024]{1,0:T(8,128)S(1)} fusion(f32[64,1024]{1,0:T(8,128)S(1)} %sub.20, f32[64,1024]{1,0:T(8,128)S(1)} %collective-permute-done.3, f32[64,1024]{1,0:T(8,128)S(1)} %collective-permute-done.2, f32[1,1024,1024]{2,1,0:T(8,128)S(1)} %copy-done.4), kind=kOutput, calls=%fused_computation.22 | convolution fusion | flops 402784256 | bytes 5242880 | tf_op jit(solution)/shard_map/dot_general | solution.py:290
  76.3 9.7 %turn.3 = (f32[64,1024]{1,0:T(8,128)S(1)}, f32[64,1024]{1,0:T(8,128)S(1)}, f32[32,48,128]{2,1,0:T(8,128)}) custom-call(s32[28]{0:T(128)S(1)} %bitcast.60, s32[28]{0:T(128)S(1)} %bitcast.64, f32[2688,1024]{1,0:T(8,128)} %bitcast.68, f32[32,48,128]{2,1,0:T(8,128)S(1)} %all-to-all-done.1.incoming_ref, f32[64,1024]{1,0:T(8,128)S(1)} %fusion.30.base_ref, ...), custom_call_target="tpu_custom_call" | custom-call | flops 2818572288 | bytes 11010048 | tf_op jit(solution)/shard_map/turn/pallas_call | solution.py:271
  86.0 4.3 %all-to-all-start.2 = ((f32[32,48,128]{2,1,0:T(8,128)}), f32[32,48,128]{2,1,0:T(8,128)S(1)}, u32[]{:S(2)}, u32[]{:S(2)}) async-start(f32[32,48,128]{2,1,0:T(8,128)} %get-tuple-element.12), calls=%async_computation.2 | async-start | bytes 1572864 | tf_op jit(solution)/shard_map/all_to_all | solution.py:283
  90.3 2.6 %collective-permute-start.4 = (f32[64,1024]{1,0:T(8,128)S(1)}, f32[64,1024]{1,0:T(8,128)S(1)}, u32[]{:S(2)}, u32[]{:S(2)}) collective-permute-start(f32[64,1024]{1,0:T(8,128)S(1)} %get-tuple-element.11.previous_ref), channel_id=1, source_target_pairs={{1,0},{2,1},{3,2},{4,3},{5,4},{6,5},{7,6},{8,7},{9,8},{10,9},{11,1... | collective-permute-start | bytes 786440 | tf_op jit(solution)/shard_map/ppermute | solution.py:26
  92.9 3.6 %fusion = f32[64,1024]{1,0:T(8,128)S(1)} fusion(f32[64,1024]{1,0:T(8,128)S(1)} %get-tuple-element.11.previous_ref, f32[1,1024,1024]{2,1,0:T(8,128)} %param.10), kind=kOutput, calls=%fused_computation | convolution fusion | flops 402653184 | bytes 4718592 | tf_op jit(solution)/shard_map/dot_general | solution.py:286
  96.5 5.3 %collective-permute-start.5 = (f32[64,1024]{1,0:T(8,128)S(1)}, f32[64,1024]{1,0:T(8,128)S(1)}, u32[]{:S(2)}, u32[]{:S(2)}) collective-permute-start(f32[64,1024]{1,0:T(8,128)S(1)} %fusion), channel_id=1, source_target_pairs={{0,1},{1,2},{2,3},{3,4},{4,5},{5,6},{6,7},{7,8},{8,9},{9,10},{10,1... | collective-permute-start | bytes 786440 | tf_op jit(solution)/shard_map/ppermute | solution.py:26
  101.8 2.0 %fusion.12 = f32[64,1024]{1,0:T(8,128)S(1)} fusion(f32[64,1024]{1,0:T(8,128)S(1)} %get-tuple-element.11.previous_ref, f32[1,1024,1024]{2,1,0:T(8,128)S(1)} %copy-done.7), kind=kOutput, calls=%fused_computation.12 | convolution fusion | flops 402653184 | bytes 4718592 | tf_op jit(solution)/shard_map/dot_general | solution.py:288
  103.9 0.8 add_bitcast_fusion
  104.7 5.9 %collective-permute-done.5 = f32[64,1024]{1,0:T(8,128)S(1)} collective-permute-done((f32[64,1024]{1,0:T(8,128)S(1)}, f32[64,1024]{1,0:T(8,128)S(1)}, u32[]{:S(2)}, u32[]{:S(2)}) %collective-permute-start.5) | collective-permute-done | bytes 262176 | tf_op jit(solution)/shard_map/ppermute | solution.py:26
  110.6 1.6 %collective-permute-done.4 = f32[64,1024]{1,0:T(8,128)S(1)} collective-permute-done((f32[64,1024]{1,0:T(8,128)S(1)}, f32[64,1024]{1,0:T(8,128)S(1)}, u32[]{:S(2)}, u32[]{:S(2)}) %collective-permute-start.4) | collective-permute-done | bytes 262176 | tf_op jit(solution)/shard_map/ppermute | solution.py:26
  112.2 2.0 %fusion.36.base_ref = f32[64,1024]{1,0:T(8,128)S(1)} fusion(f32[64,1024]{1,0:T(8,128)S(1)} %sub.22, f32[64,1024]{1,0:T(8,128)S(1)} %collective-permute-done.5, f32[64,1024]{1,0:T(8,128)S(1)} %collective-permute-done.4, f32[1,1024,1024]{2,1,0:T(8,128)S(1)} %copy-done.5), kind=kOutput, calls=%fused_computation.24 | convolution fusion | flops 402784256 | bytes 5242880 | tf_op jit(solution)/shard_map/dot_general | solution.py:290
  114.2 6.1 %far.1 = f32[64,1024]{1,0:T(8,128)} custom-call(s32[28]{0:T(128)S(1)} %bitcast.61, s32[28]{0:T(128)S(1)} %bitcast.65, f32[2688,1024]{1,0:T(8,128)} %bitcast.69, f32[32,48,128]{2,1,0:T(8,128)S(1)} %all-to-all-done.2.incoming_ref, f32[64,1024]{1,0:T(8,128)S(1)} %fusion.36.base_ref, f32[64,1024]{1,0:T(8,128)S(1)} %get-tuple-element.11.previous_ref), custom_call_target="tpu_custom_call" | custom-call | flops 1409286144 | bytes 11010048 | tf_op jit(solution)/shard_map/far/pallas_call | solution.py:271
  (20 shorter events, 0.1 us)
Async XLA Ops:
  0.6 13.7 %copy-start = (f32[1,64,1024]{2,1,0:T(8,128)S(1)}, f32[1,64,1024]{2,1,0:T(8,128)}, u32[]{:S(2)}) copy-start(f32[1,64,1024]{2,1,0:T(8,128)} %param.8) | copy-start | bytes 786436
  8.1 17.6 %copy-start.8 = (f32[1,64,1024]{2,1,0:T(8,128)S(1)}, f32[1,64,1024]{2,1,0:T(8,128)}, u32[]{:S(2)}) copy-start(f32[1,64,1024]{2,1,0:T(8,128)} %param.7) | copy-start | bytes 786436
  8.1 30.2 %all-to-all-start = ((f32[32,48,128]{2,1,0:T(8,128)}), f32[32,48,128]{2,1,0:T(8,128)S(1)}, u32[]{:S(2)}, u32[]{:S(2)}) async-start(f32[32,48,128]{2,1,0:T(8,128)} %project.1), calls=%async_computation | async-start | bytes 1572864 | tf_op jit(solution)/shard_map/all_to_all | solution.py:283
  14.3 21.9 %copy-start.3 = (f32[1,1024,1024]{2,1,0:T(8,128)S(1)}, f32[1,1024,1024]{2,1,0:T(8,128)}, u32[]{:S(2)}) copy-start(f32[1,1024,1024]{2,1,0:T(8,128)} %param.10) | copy-start | bytes 12582916
  14.4 21.9 %collective-permute-start = (f32[64,1024]{1,0:T(8,128)S(1)}, f32[64,1024]{1,0:T(8,128)S(1)}, u32[]{:S(2)}, u32[]{:S(2)}) collective-permute-start(f32[64,1024]{1,0:T(8,128)S(1)} %bitcast.56), channel_id=1, source_target_pairs={{1,0},{2,1},{3,2},{4,3},{5,4},{6,5},{7,6},{8,7},{9,8},{10,9},{11,1... | collective-permute-start | bytes 786440 | tf_op jit(solution)/shard_map/ppermute | solution.py:26
  20.6 17.7 %copy-start.1 = (s32[1,28]{1,0:T(1,128)S(1)}, s32[1,28]{1,0:T(1,128)}, u32[]{:S(2)}) copy-start(s32[1,28]{1,0:T(1,128)} %param.12) | copy-start | bytes 340
  20.6 17.7 %copy-start.2 = (s32[1,28]{1,0:T(1,128)S(1)}, s32[1,28]{1,0:T(1,128)}, u32[]{:S(2)}) copy-start(s32[1,28]{1,0:T(1,128)} %param.13) | copy-start | bytes 340
  20.6 14.1 %collective-permute-start.1 = (f32[64,1024]{1,0:T(8,128)S(1)}, f32[64,1024]{1,0:T(8,128)S(1)}, u32[]{:S(2)}, u32[]{:S(2)}) collective-permute-start(f32[64,1024]{1,0:T(8,128)S(1)} %fusion.8), channel_id=1, source_target_pairs={{0,1},{1,2},{2,3},{3,4},{4,5},{5,6},{6,7},{7,8},{8,9},{9,10},{10,1... | collective-permute-start | bytes 786440 | tf_op jit(solution)/shard_map/ppermute | solution.py:26
  48.0 28.2 %all-to-all-start.1 = ((f32[32,48,128]{2,1,0:T(8,128)}), f32[32,48,128]{2,1,0:T(8,128)S(1)}, u32[]{:S(2)}, u32[]{:S(2)}) async-start(f32[32,48,128]{2,1,0:T(8,128)} %get-tuple-element.9), calls=%async_computation.1 | async-start | bytes 1572864 | tf_op jit(solution)/shard_map/all_to_all | solution.py:283
  52.3 11.3 %copy-start.6 = (f32[1,1024,1024]{2,1,0:T(8,128)S(1)}, f32[1,1024,1024]{2,1,0:T(8,128)}, u32[]{:S(2)}) copy-start(f32[1,1024,1024]{2,1,0:T(8,128)} %param.9) | copy-start | bytes 12582916
  52.3 21.9 %copy-start.4 = (f32[1,1024,1024]{2,1,0:T(8,128)S(1)}, f32[1,1024,1024]{2,1,0:T(8,128)}, u32[]{:S(2)}) copy-start(f32[1,1024,1024]{2,1,0:T(8,128)} %param.10) | copy-start | bytes 12582916
  52.3 21.9 %collective-permute-start.2 = (f32[64,1024]{1,0:T(8,128)S(1)}, f32[64,1024]{1,0:T(8,128)S(1)}, u32[]{:S(2)}, u32[]{:S(2)}) collective-permute-start(f32[64,1024]{1,0:T(8,128)S(1)} %get-tuple-element.8.previous_ref), channel_id=1, source_target_pairs={{1,0},{2,1},{3,2},{4,3},{5,4},{6,5},{7,6},{8,7},{9,8},{10,9},{11,1... | collective-permute-start | bytes 786440 | tf_op jit(solution)/shard_map/ppermute | solution.py:26
  58.7 13.9 %collective-permute-start.3 = (f32[64,1024]{1,0:T(8,128)S(1)}, f32[64,1024]{1,0:T(8,128)S(1)}, u32[]{:S(2)}, u32[]{:S(2)}) collective-permute-start(f32[64,1024]{1,0:T(8,128)S(1)} %fusion.4), channel_id=1, source_target_pairs={{0,1},{1,2},{2,3},{3,4},{4,5},{5,6},{6,7},{7,8},{8,9},{9,10},{10,1... | collective-permute-start | bytes 786440 | tf_op jit(solution)/shard_map/ppermute | solution.py:26
  86.0 28.2 %all-to-all-start.2 = ((f32[32,48,128]{2,1,0:T(8,128)}), f32[32,48,128]{2,1,0:T(8,128)S(1)}, u32[]{:S(2)}, u32[]{:S(2)}) async-start(f32[32,48,128]{2,1,0:T(8,128)} %get-tuple-element.12), calls=%async_computation.2 | async-start | bytes 1572864 | tf_op jit(solution)/shard_map/all_to_all | solution.py:283
  90.3 11.5 %copy-start.7 = (f32[1,1024,1024]{2,1,0:T(8,128)S(1)}, f32[1,1024,1024]{2,1,0:T(8,128)}, u32[]{:S(2)}) copy-start(f32[1,1024,1024]{2,1,0:T(8,128)} %param.9) | copy-start | bytes 12582916
  90.3 21.9 %collective-permute-start.4 = (f32[64,1024]{1,0:T(8,128)S(1)}, f32[64,1024]{1,0:T(8,128)S(1)}, u32[]{:S(2)}, u32[]{:S(2)}) collective-permute-start(f32[64,1024]{1,0:T(8,128)S(1)} %get-tuple-element.11.previous_ref), channel_id=1, source_target_pairs={{1,0},{2,1},{3,2},{4,3},{5,4},{6,5},{7,6},{8,7},{9,8},{10,9},{11,1... | collective-permute-start | bytes 786440 | tf_op jit(solution)/shard_map/ppermute | solution.py:26
  96.5 15.7 %copy-start.5 = (f32[1,1024,1024]{2,1,0:T(8,128)S(1)}, f32[1,1024,1024]{2,1,0:T(8,128)}, u32[]{:S(2)}) copy-start(f32[1,1024,1024]{2,1,0:T(8,128)} %param.10) | copy-start | bytes 12582916
  96.5 14.1 %collective-permute-start.5 = (f32[64,1024]{1,0:T(8,128)S(1)}, f32[64,1024]{1,0:T(8,128)S(1)}, u32[]{:S(2)}, u32[]{:S(2)}) collective-permute-start(f32[64,1024]{1,0:T(8,128)S(1)} %fusion), channel_id=1, source_target_pairs={{0,1},{1,2},{2,3},{3,4},{4,5},{5,6},{6,7},{7,8},{8,9},{9,10},{10,1... | collective-permute-start | bytes 786440 | tf_op jit(solution)/shard_map/ppermute | solution.py:26

commit v4 on v3

--- a/solution.py
+++ b/solution.py
@@ -16,7 +16,6 @@
 AXES = ("chain", "grp")
 NT = (((1,), (1,)), ((), ()))
 NN = (((1,), (0,)), ((), ()))
-TN = (((0,), (0,)), ((), ()))
 VMEM_LIMIT = 40 * 1024 * 1024
 
 
@@ -166,7 +165,7 @@
 
 
 def turn_kernel(weights, rectangles, width, partner_ref, ranks_ref, factors_ref, incoming_ref,
-                base_ref, previous_ref, *rest):
+                base_ref, lower_ref, previous_ref, *rest):
     if weights is None:
         residual_ref, *rest = rest
         buffer, semaphore, split_ref, received_ref, turned_ref = rest
@@ -183,8 +182,11 @@
         def _():
             block = slice(*columns)
             pieces.load(index)
-            before = base_ref if first == 0 else residual_ref
-            residual = before[:, block] - pieces.far(index, turned_ref)
+            if first == 0:
+                before = base_ref[:, block] - lower_ref[:, block]
+            else:
+                before = residual_ref[:, block]
+            residual = before - pieces.far(index, turned_ref)
             residual_ref[:, block] = residual
             if weights is None or last < rows:
                 return
@@ -264,32 +266,38 @@
             name="project",
         )(in_place(partner), in_place(ranks), in_place(vectors), factor_block)
 
-    def turn(weights, incoming, base, previous):
+    def turn(weights, incoming, base, lower, previous):
         last = weights is None
         rectangles = by_columns if last else by_halves
         outs = (block,) if last else (block, block, chunks)
         return pl.pallas_call(
             functools.partial(turn_kernel, weights, rectangles, rank_width),
             out_shape=outs,
-            in_specs=[SMEM_SPEC, SMEM_SPEC, ANY_SPEC] + [VMEM_SPEC] * 3,
+            in_specs=[SMEM_SPEC, SMEM_SPEC, ANY_SPEC] + [VMEM_SPEC] * 4,
             out_specs=(VMEM_SPEC,) * len(outs),
             scratch_shapes=loading(rectangles) + received + ([] if last else [sums]),
             compiler_params=params,
             cost_estimate=cost(1 if last else 2),
             name="far" if last else "turn",
-        )(partner, ranks, factor_block, incoming, base, previous)
+        )(partner, ranks, factor_block, incoming, base, lower, previous)
 
     def finish(outgoing, vectors, before, weights):
-        incoming = lax.all_to_all(outgoing, AXES, split_axis=0, concat_axis=0, tiled=True)
         exact = lax.Precision.HIGH
-        following = from_behind(vectors, -1)
+        incoming = lax.all_to_all(
+            outgoing, AXES, split_axis=0, concat_axis=0, tiled=True
+        )
+        following = []
+        for part in jnp.split(vectors, 2, axis=1):
+            following.append(from_behind(part, -1))
         carried = lax.dot_general(vectors, neighbour_block, NN, precision=exact)
         lower_term = from_behind(carried, 1)
         partial = before - lax.dot_general(vectors, diag_block, NT, precision=exact)
         partial = lax.optimization_barrier(partial)
-        upper_term = lax.dot_general(following, neighbour_block, NT, precision=exact)
-        base = partial - (upper_term + lower_term)
-        return turn(weights, incoming, base, vectors)
+        for part, tile in zip(following, jnp.split(neighbour_block, 2, axis=1)):
+            partial = lax.optimization_barrier(
+                partial - lax.dot_general(part, tile, NT, precision=exact)
+            )
+        return turn(weights, incoming, partial, lower_term, vectors)
 
     center = (spectrum_low + spectrum_high) / 2.0
     half_width = (spectrum_high - spectrum_low) / 2.0

time: 122 us -> 120 us (0.984)
  waiting for transfers between devices: 22.4 us -> 16 us
  starting transfers between devices: 37.9 us -> 43.5 us
    ppermute x6 -> x9, starting transfers between devices: 23.1 us -> 29.9 us  [from_behind(): return lax.ppermute(block, AXES, route)]
    ppermute x6 -> x9, waiting for transfers between devices: 22.4 us -> 16 us  [from_behind(): return lax.ppermute(block, AXES, route)]
    dot_general x3, matrix products: 10.8 us -> 8.81 us  [finish(): carried = lax.dot_general(vectors, neighbour_block, NN, precision=exact)]
    dot_general x3 -> x6, matrix products: 6.14 us -> 6.79 us  [finish(): lax.dot_general(part, tile, NT, precision=exact)]
  transfers between devices with their start and end apart: 9 -> 12, of which waited for: 6 -> 4; matrix products, arithmetic and copies ran while one was open for 22% -> 21% of each run, Pallas kernels for 0% -> 0%
where the time goes in v4:
time: 120 us; the launch traced here: 119 us
  starting transfers between devices  43.5 us (36%)
  Pallas kernels  33 us (28%)
  matrix products  24.3 us (20%)
  waiting for transfers between devices  16 us (13%)
  between operations  1.21 us (1%)
    ppermute x9, starting transfers between devices, from_behind(): return lax.ppermute(block, AXES, route)  29.9 us
    pallas_call x3, Pallas kernels, turn(): pl.pallas_call(functools.partial(turn_kernel, weights, rectangles, rank_w...  25.6 us
    ppermute x9, waiting for transfers between devices, from_behind(): return lax.ppermute(block, AXES, route)  16 us
    all_to_all x3, starting transfers between devices, finish(): lax.all_to_all(outgoing, AXES, split_axis=0, concat_axis=0, tiled=True)  13.6 us
    dot_general x3, matrix products, finish(): carried = lax.dot_general(vectors, neighbour_block, NN, precision=exact)  8.81 us
    dot_general x3, matrix products, finish(): partial = before - lax.dot_general(vectors, diag_block, NT, precision=exact)  8.68 us
    pallas_call x1, Pallas kernels, projected(): pl.pallas_call(functools.partial(project_kernel, by_columns, rank_width),...  7.43 us
    dot_general x6, matrix products, finish(): lax.dot_general(part, tile, NT, precision=exact)  6.79 us
  transfers between devices with their start and end apart: 12, of which 4 were waited for; matrix products, arithmetic and copies ran while one was open for 21% of the time, Pallas kernels for 0%

profile of v4, /device:TPU:15, one launch (start us, length us, event | category | flops | bytes accessed | tf_op | source)
XLA Modules:
  0.0 119.1 jit_solution(9889771530720985804)
XLA Ops:
  0.6 7.4 %project.1 = f32[32,48,128]{2,1,0:T(8,128)} custom-call(s32[28]{0:T(128)} %bitcast.43, s32[28]{0:T(128)} %bitcast.47, f32[64,1024]{1,0:T(8,128)} %bitcast.40, f32[2688,1024]{1,0:T(8,128)} %bitcast.51), custom_call_target="tpu_custom_call" | custom-call | flops 1409286144 | bytes 11010048 | tf_op jit(solution)/shard_map/project/pallas_call | solution.py:252
  8.1 6.2 %all-to-all-start = ((f32[32,48,128]{2,1,0:T(8,128)}), f32[32,48,128]{2,1,0:T(8,128)S(1)}, u32[]{:S(2)}, u32[]{:S(2)}) async-start(f32[32,48,128]{2,1,0:T(8,128)} %project.1), calls=%async_computation | async-start | bytes 1572864 | tf_op jit(solution)/shard_map/all_to_all | solution.py:286
  14.4 2.6 %collective-permute-start.1 = (f32[64,512]{1,0:T(8,128)S(1)}, f32[64,512]{1,0:T(8,128)S(1)}, u32[]{:S(2)}, u32[]{:S(2)}) collective-permute-start(f32[64,512]{1,0:T(8,128)S(1)} %get-tuple-element.18), channel_id=1, source_target_pairs={{1,0},{2,1},{3,2},{4,3},{5,4},{6,5},{7,6},{8,7},{9,8},{10,9},{11,1... | collective-permute-start | bytes 393224 | tf_op jit(solution)/shard_map/ppermute | solution.py:25
  17.0 2.5 %collective-permute-start = (f32[64,512]{1,0:T(8,128)S(1)}, f32[64,512]{1,0:T(8,128)S(1)}, u32[]{:S(2)}, u32[]{:S(2)}) collective-permute-start(f32[64,512]{1,0:T(8,128)S(1)} %get-tuple-element.19), channel_id=1, source_target_pairs={{1,0},{2,1},{3,2},{4,3},{5,4},{6,5},{7,6},{8,7},{9,8},{10,9},{11,1... | collective-permute-start | bytes 393224 | tf_op jit(solution)/shard_map/ppermute | solution.py:25
  19.4 3.6 %fusion.28 = f32[64,1024]{1,0:T(8,128)S(1)} fusion(f32[1,1024,1024]{2,1,0:T(8,128)} %param.10, f32[1,64,1024]{2,1,0:T(8,128)S(1)} %copy-done), kind=kOutput, calls=%fused_computation.25 | convolution fusion | flops 402653184 | bytes 4718592 | tf_op jit(solution)/shard_map/dot_general | solution.py:292
  23.1 5.2 %collective-permute-start.2 = (f32[64,1024]{1,0:T(8,128)S(1)}, f32[64,1024]{1,0:T(8,128)S(1)}, u32[]{:S(2)}, u32[]{:S(2)}) collective-permute-start(f32[64,1024]{1,0:T(8,128)S(1)} %fusion.28), channel_id=1, source_target_pairs={{0,1},{1,2},{2,3},{3,4},{4,5},{5,6},{6,7},{7,8},{8,9},{9,10},{10,1... | collective-permute-start | bytes 786440 | tf_op jit(solution)/shard_map/ppermute | solution.py:25
  28.3 2.2 %fusion.21 = f32[64,1024]{1,0:T(8,128)S(1)} fusion(f32[1,1024,1024]{2,1,0:T(8,128)S(1)} %copy-done.6, f32[1,64,1024]{2,1,0:T(8,128)S(1)} %copy-done.8, f32[1,64,1024]{2,1,0:T(8,128)S(1)} %copy-done), kind=kOutput, calls=%fused_computation.19 | convolution fusion | flops 402718720 | bytes 4980736 | tf_op jit(solution)/shard_map/dot_general | solution.py:294
  30.4 5.8 %collective-permute-done = f32[64,512]{1,0:T(8,128)S(1)} collective-permute-done((f32[64,512]{1,0:T(8,128)S(1)}, f32[64,512]{1,0:T(8,128)S(1)}, u32[]{:S(2)}, u32[]{:S(2)}) %collective-permute-start) | collective-permute-done | bytes 131104 | tf_op jit(solution)/shard_map/ppermute | solution.py:25
  36.2 1.1 fusion.18
  37.4 1.1 fusion.10
  38.6 9.7 %turn.2 = (f32[64,1024]{1,0:T(8,128)S(1)}, f32[64,1024]{1,0:T(8,128)S(1)}, f32[32,48,128]{2,1,0:T(8,128)}) custom-call(s32[28]{0:T(128)S(1)} %bitcast.44, s32[28]{0:T(128)S(1)} %bitcast.48, f32[2688,1024]{1,0:T(8,128)} %bitcast.52, f32[32,48,128]{2,1,0:T(8,128)S(1)} %all-to-all-done.incoming_ref, f32[64,1024]{1,0:T(8,128)S(1)} %sub.29.base_ref, ...), custom_call_target="tpu_custom_call" | custom-call | flops 2818572288 | bytes 11010048 | tf_op jit(solution)/shard_map/turn/pallas_call | solution.py:273
  48.3 3.7 %all-to-all-start.1 = ((f32[32,48,128]{2,1,0:T(8,128)}), f32[32,48,128]{2,1,0:T(8,128)S(1)}, u32[]{:S(2)}, u32[]{:S(2)}) async-start(f32[32,48,128]{2,1,0:T(8,128)} %get-tuple-element.9), calls=%async_computation.1 | async-start | bytes 1572864 | tf_op jit(solution)/shard_map/all_to_all | solution.py:286
  52.0 2.7 %collective-permute-start.3 = (f32[64,512]{1,0:T(8,128)S(1)}, f32[64,512]{1,0:T(8,128)S(1)}, u32[]{:S(2)}, u32[]{:S(2)}) collective-permute-start(f32[64,512]{1,0:T(8,128)S(1)} %get-tuple-element.17), channel_id=1, source_target_pairs={{1,0},{2,1},{3,2},{4,3},{5,4},{6,5},{7,6},{8,7},{9,8},{10,9},{11,1... | collective-permute-start | bytes 393224 | tf_op jit(solution)/shard_map/ppermute | solution.py:25
  54.7 3.6 %fusion.26 = f32[64,1024]{1,0:T(8,128)S(1)} fusion(f32[64,1024]{1,0:T(8,128)S(1)} %get-tuple-element.8.previous_ref, f32[1,1024,1024]{2,1,0:T(8,128)} %param.10), kind=kOutput, calls=%fused_computation.23 | convolution fusion | flops 402653184 | bytes 4718592 | tf_op jit(solution)/shard_map/dot_general | solution.py:292
  58.4 2.2 %fusion.2 = f32[64,1024]{1,0:T(8,128)S(1)} fusion(f32[64,1024]{1,0:T(8,128)S(1)} %get-tuple-element.8.previous_ref, f32[1,1024,1024]{2,1,0:T(8,128)S(1)} %copy-done.7), kind=kOutput, calls=%fused_computation.2 | convolution fusion | flops 402653184 | bytes 4718592 | tf_op jit(solution)/shard_map/dot_general | solution.py:294
  60.6 2.2 %collective-permute-start.4 = (f32[64,512]{1,0:T(8,128)S(1)}, f32[64,512]{1,0:T(8,128)S(1)}, u32[]{:S(2)}, u32[]{:S(2)}) collective-permute-start(f32[64,512]{1,0:T(8,128)S(1)} %get-tuple-element.16), channel_id=1, source_target_pairs={{1,0},{2,1},{3,2},{4,3},{5,4},{6,5},{7,6},{8,7},{9,8},{10,9},{11,1... | collective-permute-start | bytes 393224 | tf_op jit(solution)/shard_map/ppermute | solution.py:25
  62.8 5.2 %collective-permute-start.5 = (f32[64,1024]{1,0:T(8,128)S(1)}, f32[64,1024]{1,0:T(8,128)S(1)}, u32[]{:S(2)}, u32[]{:S(2)}) collective-permute-start(f32[64,1024]{1,0:T(8,128)S(1)} %fusion.26), channel_id=1, source_target_pairs={{0,1},{1,2},{2,3},{3,4},{4,5},{5,6},{6,7},{7,8},{8,9},{9,10},{10,1... | collective-permute-start | bytes 786440 | tf_op jit(solution)/shard_map/ppermute | solution.py:25
  67.9 4.5 %collective-permute-done.3 = f32[64,512]{1,0:T(8,128)S(1)} collective-permute-done((f32[64,512]{1,0:T(8,128)S(1)}, f32[64,512]{1,0:T(8,128)S(1)}, u32[]{:S(2)}, u32[]{:S(2)}) %collective-permute-start.3) | collective-permute-done | bytes 131104 | tf_op jit(solution)/shard_map/ppermute | solution.py:25
  72.5 1.1 fusion.14
  73.9 1.1 fusion.8
  75.1 9.8 %turn.3 = (f32[64,1024]{1,0:T(8,128)S(1)}, f32[64,1024]{1,0:T(8,128)S(1)}, f32[32,48,128]{2,1,0:T(8,128)}) custom-call(s32[28]{0:T(128)S(1)} %bitcast.45, s32[28]{0:T(128)S(1)} %bitcast.49, f32[2688,1024]{1,0:T(8,128)} %bitcast.53, f32[32,48,128]{2,1,0:T(8,128)S(1)} %all-to-all-done.1.incoming_ref, f32[64,1024]{1,0:T(8,128)S(1)} %sub.32.base_ref, ...), custom_call_target="tpu_custom_call" | custom-call | flops 2818572288 | bytes 11010048 | tf_op jit(solution)/shard_map/turn/pallas_call | solution.py:273
  84.8 3.7 %all-to-all-start.2 = ((f32[32,48,128]{2,1,0:T(8,128)}), f32[32,48,128]{2,1,0:T(8,128)S(1)}, u32[]{:S(2)}, u32[]{:S(2)}) async-start(f32[32,48,128]{2,1,0:T(8,128)} %get-tuple-element.12), calls=%async_computation.2 | async-start | bytes 1572864 | tf_op jit(solution)/shard_map/all_to_all | solution.py:286
  88.5 4.4 %fusion = f32[64,1024]{1,0:T(8,128)S(1)} fusion(f32[64,1024]{1,0:T(8,128)S(1)} %get-tuple-element.11.previous_ref, f32[1,1024,1024]{2,1,0:T(8,128)} %param.9), kind=kOutput, calls=%fused_computation | convolution fusion | flops 402653184 | bytes 4718592 | tf_op jit(solution)/shard_map/dot_general | solution.py:294
  93.0 2.3 %collective-permute-start.7 = (f32[64,512]{1,0:T(8,128)S(1)}, f32[64,512]{1,0:T(8,128)S(1)}, u32[]{:S(2)}, u32[]{:S(2)}) collective-permute-start(f32[64,512]{1,0:T(8,128)S(1)} %get-tuple-element.14), channel_id=1, source_target_pairs={{1,0},{2,1},{3,2},{4,3},{5,4},{6,5},{7,6},{8,7},{9,8},{10,9},{11,1... | collective-permute-start | bytes 393224 | tf_op jit(solution)/shard_map/ppermute | solution.py:25
  95.3 2.2 %collective-permute-start.6 = (f32[64,512]{1,0:T(8,128)S(1)}, f32[64,512]{1,0:T(8,128)S(1)}, u32[]{:S(2)}, u32[]{:S(2)}) collective-permute-start(f32[64,512]{1,0:T(8,128)S(1)} %get-tuple-element.15), channel_id=1, source_target_pairs={{1,0},{2,1},{3,2},{4,3},{5,4},{6,5},{7,6},{8,7},{9,8},{10,9},{11,1... | collective-permute-start | bytes 393224 | tf_op jit(solution)/shard_map/ppermute | solution.py:25
  97.5 1.6 %fusion.24 = f32[64,1024]{1,0:T(8,128)S(1)} fusion(f32[64,1024]{1,0:T(8,128)S(1)} %get-tuple-element.11.previous_ref, f32[1,1024,1024]{2,1,0:T(8,128)S(1)} %copy-done.5), kind=kOutput, calls=%fused_computation.21 | convolution fusion | flops 402653184 | bytes 4718592 | tf_op jit(solution)/shard_map/dot_general | solution.py:292
  99.1 5.2 %collective-permute-start.8 = (f32[64,1024]{1,0:T(8,128)S(1)}, f32[64,1024]{1,0:T(8,128)S(1)}, u32[]{:S(2)}, u32[]{:S(2)}) collective-permute-start(f32[64,1024]{1,0:T(8,128)S(1)} %fusion.24), channel_id=1, source_target_pairs={{0,1},{1,2},{2,3},{3,4},{4,5},{5,6},{6,7},{7,8},{8,9},{9,10},{10,1... | collective-permute-start | bytes 786440 | tf_op jit(solution)/shard_map/ppermute | solution.py:25
  104.3 0.8 add_bitcast_fusion
  105.0 5.4 %collective-permute-done.6 = f32[64,512]{1,0:T(8,128)S(1)} collective-permute-done((f32[64,512]{1,0:T(8,128)S(1)}, f32[64,512]{1,0:T(8,128)S(1)}, u32[]{:S(2)}, u32[]{:S(2)}) %collective-permute-start.6) | collective-permute-done | bytes 131104 | tf_op jit(solution)/shard_map/ppermute | solution.py:25
  110.4 1.1 fusion.12
  111.6 1.1 fusion.6
  112.8 6.1 %far.1 = f32[64,1024]{1,0:T(8,128)} custom-call(s32[28]{0:T(128)S(1)} %bitcast.46, s32[28]{0:T(128)S(1)} %bitcast.50, f32[2688,1024]{1,0:T(8,128)} %bitcast.54, f32[32,48,128]{2,1,0:T(8,128)S(1)} %all-to-all-done.2.incoming_ref, f32[64,1024]{1,0:T(8,128)S(1)} %sub.35.base_ref, f32[64,1024]{1,0:T(8,128)S(1)} %collective-permute-done.8.lower_ref, ...), custom_call_target="tpu_custom_call" | custom-call | flops 1409286144 | bytes 11010048 | tf_op jit(solution)/shard_map/far/pallas_call | solution.py:273
  (37 shorter events, 0.6 us)
Async XLA Ops:
  0.6 13.7 %copy-start = (f32[1,64,1024]{2,1,0:T(8,128)S(1)}, f32[1,64,1024]{2,1,0:T(8,128)}, u32[]{:S(2)}) copy-start(f32[1,64,1024]{2,1,0:T(8,128)} %param.8) | copy-start | bytes 786436
  8.1 20.2 %copy-start.8 = (f32[1,64,1024]{2,1,0:T(8,128)S(1)}, f32[1,64,1024]{2,1,0:T(8,128)}, u32[]{:S(2)}) copy-start(f32[1,64,1024]{2,1,0:T(8,128)} %param.7) | copy-start | bytes 786436
  8.1 30.5 %all-to-all-start = ((f32[32,48,128]{2,1,0:T(8,128)}), f32[32,48,128]{2,1,0:T(8,128)S(1)}, u32[]{:S(2)}, u32[]{:S(2)}) async-start(f32[32,48,128]{2,1,0:T(8,128)} %project.1), calls=%async_computation | async-start | bytes 1572864 | tf_op jit(solution)/shard_map/all_to_all | solution.py:286
  14.4 13.9 %copy-start.6 = (f32[1,1024,1024]{2,1,0:T(8,128)S(1)}, f32[1,1024,1024]{2,1,0:T(8,128)}, u32[]{:S(2)}) copy-start(f32[1,1024,1024]{2,1,0:T(8,128)} %param.9) | copy-start | bytes 12582916
  14.4 23.0 %collective-permute-start.1 = (f32[64,512]{1,0:T(8,128)S(1)}, f32[64,512]{1,0:T(8,128)S(1)}, u32[]{:S(2)}, u32[]{:S(2)}) collective-permute-start(f32[64,512]{1,0:T(8,128)S(1)} %get-tuple-element.18), channel_id=1, source_target_pairs={{1,0},{2,1},{3,2},{4,3},{5,4},{6,5},{7,6},{8,7},{9,8},{10,9},{11,1... | collective-permute-start | bytes 393224 | tf_op jit(solution)/shard_map/ppermute | solution.py:25
  17.0 19.3 %copy-start.3 = (f32[1,1024,1024]{2,1,0:T(8,128)S(1)}, f32[1,1024,1024]{2,1,0:T(8,128)}, u32[]{:S(2)}) copy-start(f32[1,1024,1024]{2,1,0:T(8,128)} %param.10) | copy-start | bytes 12582916
  17.0 19.3 %collective-permute-start = (f32[64,512]{1,0:T(8,128)S(1)}, f32[64,512]{1,0:T(8,128)S(1)}, u32[]{:S(2)}, u32[]{:S(2)}) collective-permute-start(f32[64,512]{1,0:T(8,128)S(1)} %get-tuple-element.19), channel_id=1, source_target_pairs={{1,0},{2,1},{3,2},{4,3},{5,4},{6,5},{7,6},{8,7},{9,8},{10,9},{11,1... | collective-permute-start | bytes 393224 | tf_op jit(solution)/shard_map/ppermute | solution.py:25
  23.1 15.5 %collective-permute-start.2 = (f32[64,1024]{1,0:T(8,128)S(1)}, f32[64,1024]{1,0:T(8,128)S(1)}, u32[]{:S(2)}, u32[]{:S(2)}) collective-permute-start(f32[64,1024]{1,0:T(8,128)S(1)} %fusion.28), channel_id=1, source_target_pairs={{0,1},{1,2},{2,3},{3,4},{4,5},{5,6},{6,7},{7,8},{8,9},{9,10},{10,1... | collective-permute-start | bytes 786440 | tf_op jit(solution)/shard_map/ppermute | solution.py:25
  30.4 8.2 %copy-start.1 = (s32[1,28]{1,0:T(1,128)S(1)}, s32[1,28]{1,0:T(1,128)}, u32[]{:S(2)}) copy-start(s32[1,28]{1,0:T(1,128)} %param.12) | copy-start | bytes 340
  30.4 8.2 %copy-start.2 = (s32[1,28]{1,0:T(1,128)S(1)}, s32[1,28]{1,0:T(1,128)}, u32[]{:S(2)}) copy-start(s32[1,28]{1,0:T(1,128)} %param.13) | copy-start | bytes 340
  48.3 26.7 %all-to-all-start.1 = ((f32[32,48,128]{2,1,0:T(8,128)}), f32[32,48,128]{2,1,0:T(8,128)S(1)}, u32[]{:S(2)}, u32[]{:S(2)}) async-start(f32[32,48,128]{2,1,0:T(8,128)} %get-tuple-element.9), calls=%async_computation.1 | async-start | bytes 1572864 | tf_op jit(solution)/shard_map/all_to_all | solution.py:286
  52.0 6.4 %copy-start.7 = (f32[1,1024,1024]{2,1,0:T(8,128)S(1)}, f32[1,1024,1024]{2,1,0:T(8,128)}, u32[]{:S(2)}) copy-start(f32[1,1024,1024]{2,1,0:T(8,128)} %param.9) | copy-start | bytes 12582916
  52.0 20.5 %copy-start.4 = (f32[1,1024,1024]{2,1,0:T(8,128)S(1)}, f32[1,1024,1024]{2,1,0:T(8,128)}, u32[]{:S(2)}) copy-start(f32[1,1024,1024]{2,1,0:T(8,128)} %param.10) | copy-start | bytes 12582916
  52.0 20.4 %collective-permute-start.3 = (f32[64,512]{1,0:T(8,128)S(1)}, f32[64,512]{1,0:T(8,128)S(1)}, u32[]{:S(2)}, u32[]{:S(2)}) collective-permute-start(f32[64,512]{1,0:T(8,128)S(1)} %get-tuple-element.17), channel_id=1, source_target_pairs={{1,0},{2,1},{3,2},{4,3},{5,4},{6,5},{7,6},{8,7},{9,8},{10,9},{11,1... | collective-permute-start | bytes 393224 | tf_op jit(solution)/shard_map/ppermute | solution.py:25
  60.6 13.3 %collective-permute-start.4 = (f32[64,512]{1,0:T(8,128)S(1)}, f32[64,512]{1,0:T(8,128)S(1)}, u32[]{:S(2)}, u32[]{:S(2)}) collective-permute-start(f32[64,512]{1,0:T(8,128)S(1)} %get-tuple-element.16), channel_id=1, source_target_pairs={{1,0},{2,1},{3,2},{4,3},{5,4},{6,5},{7,6},{8,7},{9,8},{10,9},{11,1... | collective-permute-start | bytes 393224 | tf_op jit(solution)/shard_map/ppermute | solution.py:25
  62.8 12.3 %collective-permute-start.5 = (f32[64,1024]{1,0:T(8,128)S(1)}, f32[64,1024]{1,0:T(8,128)S(1)}, u32[]{:S(2)}, u32[]{:S(2)}) collective-permute-start(f32[64,1024]{1,0:T(8,128)S(1)} %fusion.26), channel_id=1, source_target_pairs={{0,1},{1,2},{2,3},{3,4},{4,5},{5,6},{6,7},{7,8},{8,9},{9,10},{10,1... | collective-permute-start | bytes 786440 | tf_op jit(solution)/shard_map/ppermute | solution.py:25
  84.8 27.9 %all-to-all-start.2 = ((f32[32,48,128]{2,1,0:T(8,128)}), f32[32,48,128]{2,1,0:T(8,128)S(1)}, u32[]{:S(2)}, u32[]{:S(2)}) async-start(f32[32,48,128]{2,1,0:T(8,128)} %get-tuple-element.12), calls=%async_computation.2 | async-start | bytes 1572864 | tf_op jit(solution)/shard_map/all_to_all | solution.py:286
  88.5 9.0 %copy-start.5 = (f32[1,1024,1024]{2,1,0:T(8,128)S(1)}, f32[1,1024,1024]{2,1,0:T(8,128)}, u32[]{:S(2)}) copy-start(f32[1,1024,1024]{2,1,0:T(8,128)} %param.10) | copy-start | bytes 12582916
  93.0 18.6 %collective-permute-start.7 = (f32[64,512]{1,0:T(8,128)S(1)}, f32[64,512]{1,0:T(8,128)S(1)}, u32[]{:S(2)}, u32[]{:S(2)}) collective-permute-start(f32[64,512]{1,0:T(8,128)S(1)} %get-tuple-element.14), channel_id=1, source_target_pairs={{1,0},{2,1},{3,2},{4,3},{5,4},{6,5},{7,6},{8,7},{9,8},{10,9},{11,1... | collective-permute-start | bytes 393224 | tf_op jit(solution)/shard_map/ppermute | solution.py:25
  95.3 15.1 %collective-permute-start.6 = (f32[64,512]{1,0:T(8,128)S(1)}, f32[64,512]{1,0:T(8,128)S(1)}, u32[]{:S(2)}, u32[]{:S(2)}) collective-permute-start(f32[64,512]{1,0:T(8,128)S(1)} %get-tuple-element.15), channel_id=1, source_target_pairs={{1,0},{2,1},{3,2},{4,3},{5,4},{6,5},{7,6},{8,7},{9,8},{10,9},{11,1... | collective-permute-start | bytes 393224 | tf_op jit(solution)/shard_map/ppermute | solution.py:25
  99.1 13.7 %collective-permute-start.8 = (f32[64,1024]{1,0:T(8,128)S(1)}, f32[64,1024]{1,0:T(8,128)S(1)}, u32[]{:S(2)}, u32[]{:S(2)}) collective-permute-start(f32[64,1024]{1,0:T(8,128)S(1)} %fusion.24), channel_id=1, source_target_pairs={{0,1},{1,2},{2,3},{3,4},{4,5},{5,6},{6,7},{7,8},{8,9},{9,10},{10,1... | collective-permute-start | bytes 786440 | tf_op jit(solution)/shard_map/ppermute | solution.py:25

commit v5 on v4

--- a/solution.py
+++ b/solution.py
@@ -41,9 +41,12 @@
 
 
 class Pieces:
-    def __init__(self, rectangles, factors_ref, buffer, semaphore, split_ref):
+    def __init__(self, rectangles, factors_ref, buffer, semaphore, split_ref, held_ref=None):
         self.rectangles, self.factors_ref, self.buffer = rectangles, factors_ref, buffer
-        self.semaphore, self.split_ref = semaphore, split_ref
+        self.semaphore, self.split_ref, self.held_ref = semaphore, split_ref, held_ref
+
+    def held(self, index):
+        return index == 0 and self.held_ref is not None
 
     def copy(self, index):
         rows, columns = (slice(*edges) for edges in self.rectangles[index])
@@ -54,12 +57,17 @@
 
     def start(self):
         for index in range(len(self.rectangles)):
-            self.copy(index).start()
+            if not self.held(index):
+                self.copy(index).start()
 
     def load(self, index):
-        self.copy(index).wait()
         rows, columns = (slice(*edges) for edges in self.rectangles[index])
-        high, low = halves(self.buffer[rows, columns])
+        if self.held(index):
+            values = self.held_ref[...]
+        else:
+            self.copy(index).wait()
+            values = self.buffer[rows, columns]
+        high, low = halves(values)
         width = high.shape[1]
         self.split_ref[rows, :width], self.split_ref[rows, width:2 * width] = high, low
 
@@ -164,15 +172,15 @@
                 )
 
 
-def turn_kernel(weights, rectangles, width, partner_ref, ranks_ref, factors_ref, incoming_ref,
-                base_ref, lower_ref, previous_ref, *rest):
+def turn_kernel(weights, rectangles, width, partner_ref, ranks_ref, factors_ref, held_ref,
+                incoming_ref, base_ref, lower_ref, previous_ref, *rest):
     if weights is None:
         residual_ref, *rest = rest
         buffer, semaphore, split_ref, received_ref, turned_ref = rest
     else:
         residual_ref, direction_ref, outgoing_ref, *rest = rest
         buffer, semaphore, split_ref, received_ref, turned_ref, sums_ref = rest
-    pieces = Pieces(rectangles, factors_ref, buffer, semaphore, split_ref)
+    pieces = Pieces(rectangles, factors_ref, buffer, semaphore, split_ref, held_ref)
     pieces.start()
     unpack(width, factors_ref.shape[0] // width, partner_ref, incoming_ref, received_ref)
     turned_ref[...] = received_ref[...].T
@@ -219,10 +227,19 @@
     block = jax.ShapeDtypeStruct((n, points), jnp.float32)
     chunks = jax.ShapeDtypeStruct((device_count, rank_width // 2, 2 * n), jnp.float32)
     factor_block = factor_block.reshape(rows, points)
-    factor_block = pltpu.with_memory_space_constraint(factor_block, pltpu.HBM)
     middle, quarter = points // 2, points // 4
     by_columns = [((0, rows), (at, at + quarter)) for at in range(0, points, quarter)]
-    by_halves = [(part, (0, middle)) for part in cuts(rows, 2)] + [((0, rows), (middle, points))]
+    held_rows = 512
+    held = factor_block[:held_rows, :middle]
+    factor_block = pltpu.with_memory_space_constraint(factor_block, pltpu.HBM)
+    left = [(0, held_rows)] + [
+        (held_rows + first, held_rows + last) for first, last in cuts(rows - held_rows, 3)
+    ]
+    left = [(part, (0, middle)) for part in left]
+    by_halves = left + [((0, rows), (middle, points))]
+    for_last = left + [((0, rows), (middle, middle + quarter))] + [
+        (part, (middle + quarter, points)) for part in cuts(rows, 2)
+    ]
 
     def loading(rectangles):
         width = max(right - left for _, (left, right) in rectangles)
@@ -268,18 +285,18 @@
 
     def turn(weights, incoming, base, lower, previous):
         last = weights is None
-        rectangles = by_columns if last else by_halves
+        rectangles = for_last if last else by_halves
         outs = (block,) if last else (block, block, chunks)
         return pl.pallas_call(
             functools.partial(turn_kernel, weights, rectangles, rank_width),
             out_shape=outs,
-            in_specs=[SMEM_SPEC, SMEM_SPEC, ANY_SPEC] + [VMEM_SPEC] * 4,
+            in_specs=[SMEM_SPEC, SMEM_SPEC, ANY_SPEC] + [VMEM_SPEC] * 5,
             out_specs=(VMEM_SPEC,) * len(outs),
             scratch_shapes=loading(rectangles) + received + ([] if last else [sums]),
             compiler_params=params,
             cost_estimate=cost(1 if last else 2),
             name="far" if last else "turn",
-        )(partner, ranks, factor_block, incoming, base, lower, previous)
+        )(partner, ranks, factor_block, held, incoming, base, lower, previous)
 
     def finish(outgoing, vectors, before, weights):
         exact = lax.Precision.HIGH

time: 120 us -> 118 us (0.983)
  Pallas kernels: 33 us -> 30.8 us
  local copies, waits for them, and re-layouts: 0.11 us -> 2.3 us
  waiting for transfers between devices: 16 us -> 14.7 us
    pallas_call x3, Pallas kernels: 25.6 us -> 23.3 us  [turn(): pl.pallas_call(functools.partial(turn_kernel, weights, rectangles, rank_w...]
    ppermute x9, waiting for transfers between devices: 16 us -> 14.7 us  [from_behind(): return lax.ppermute(block, AXES, route)]
    slice x0 -> x1, local copies, waits for them, and re-layouts: none -> 1.31 us  [body(): held = factor_block[:held_rows, :middle]]
  transfers between devices with their start and end apart: 12 -> 12, of which waited for: 4 -> 4; matrix products, arithmetic and copies ran while one was open for 21% -> 23% of each run, Pallas kernels for 0% -> 0%
where the time goes in v5:
time: 118 us
  starting transfers between devices  43.5 us (37%)
  Pallas kernels  30.8 us (26%)
  matrix products  24.3 us (21%)
  waiting for transfers between devices  14.7 us (12%)
  local copies, waits for them, and re-layouts  2.3 us (2%)
  between operations  1.23 us (1%)
    ppermute x9, starting transfers between devices, from_behind(): return lax.ppermute(block, AXES, route)  29.9 us
    pallas_call x3, Pallas kernels, turn(): pl.pallas_call(functools.partial(turn_kernel, weights, rectangles, rank_w...  23.3 us
    ppermute x9, waiting for transfers between devices, from_behind(): return lax.ppermute(block, AXES, route)  14.7 us
    all_to_all x3, starting transfers between devices, finish(): lax.all_to_all(outgoing, AXES, split_axis=0, concat_axis=0, tiled=True)  13.6 us
    dot_general x3, matrix products, finish(): carried = lax.dot_general(vectors, neighbour_block, NN, precision=exact)  8.81 us
    dot_general x3, matrix products, finish(): partial = before - lax.dot_general(vectors, diag_block, NT, precision=exact)  8.68 us
    pallas_call x1, Pallas kernels, projected(): pl.pallas_call(functools.partial(project_kernel, by_columns, rank_width),...  7.42 us
    dot_general x6, matrix products, finish(): lax.dot_general(part, tile, NT, precision=exact)  6.79 us
  transfers between devices with their start and end apart: 12, of which 4 were waited for; matrix products, arithmetic and copies ran while one was open for 23% of the time, Pallas kernels for 0%

profile of v5, /device:TPU:15, one launch (start us, length us, event | category | flops | bytes accessed | tf_op | source)
XLA Modules:
  0.0 117.7 jit_solution(9410732811719966836)
XLA Ops:
  0.6 7.4 %project.1 = f32[32,48,128]{2,1,0:T(8,128)} custom-call(s32[28]{0:T(128)} %bitcast.43, s32[28]{0:T(128)} %bitcast.47, f32[64,1024]{1,0:T(8,128)} %bitcast.40, f32[2688,1024]{1,0:T(8,128)} %bitcast.51), custom_call_target="tpu_custom_call" | custom-call | flops 1409286144 | bytes 11010048 | tf_op jit(solution)/shard_map/project/pallas_call | solution.py:269
  8.1 6.2 %all-to-all-start = ((f32[32,48,128]{2,1,0:T(8,128)}), f32[32,48,128]{2,1,0:T(8,128)S(1)}, u32[]{:S(2)}, u32[]{:S(2)}) async-start(f32[32,48,128]{2,1,0:T(8,128)} %project.1), calls=%async_computation | async-start | bytes 1572864 | tf_op jit(solution)/shard_map/all_to_all | solution.py:303
  14.4 2.6 %collective-permute-start.1 = (f32[64,512]{1,0:T(8,128)S(1)}, f32[64,512]{1,0:T(8,128)S(1)}, u32[]{:S(2)}, u32[]{:S(2)}) collective-permute-start(f32[64,512]{1,0:T(8,128)S(1)} %get-tuple-element.18), channel_id=1, source_target_pairs={{1,0},{2,1},{3,2},{4,3},{5,4},{6,5},{7,6},{8,7},{9,8},{10,9},{11,1... | collective-permute-start | bytes 393224 | tf_op jit(solution)/shard_map/ppermute | solution.py:25
  17.0 2.2 %collective-permute-start = (f32[64,512]{1,0:T(8,128)S(1)}, f32[64,512]{1,0:T(8,128)S(1)}, u32[]{:S(2)}, u32[]{:S(2)}) collective-permute-start(f32[64,512]{1,0:T(8,128)S(1)} %get-tuple-element.19), channel_id=1, source_target_pairs={{1,0},{2,1},{3,2},{4,3},{5,4},{6,5},{7,6},{8,7},{9,8},{10,9},{11,1... | collective-permute-start | bytes 393224 | tf_op jit(solution)/shard_map/ppermute | solution.py:25
  19.2 3.6 %fusion.28 = f32[64,1024]{1,0:T(8,128)S(1)} fusion(f32[1,1024,1024]{2,1,0:T(8,128)} %param.10, f32[1,64,1024]{2,1,0:T(8,128)S(1)} %copy-done), kind=kOutput, calls=%fused_computation.25 | convolution fusion | flops 402653184 | bytes 4718592 | tf_op jit(solution)/shard_map/dot_general | solution.py:309
  22.8 5.4 %collective-permute-start.2 = (f32[64,1024]{1,0:T(8,128)S(1)}, f32[64,1024]{1,0:T(8,128)S(1)}, u32[]{:S(2)}, u32[]{:S(2)}) collective-permute-start(f32[64,1024]{1,0:T(8,128)S(1)} %fusion.28), channel_id=1, source_target_pairs={{0,1},{1,2},{2,3},{3,4},{4,5},{5,6},{6,7},{7,8},{8,9},{9,10},{10,1... | collective-permute-start | bytes 786440 | tf_op jit(solution)/shard_map/ppermute | solution.py:25
  28.3 2.2 %fusion.21 = f32[64,1024]{1,0:T(8,128)S(1)} fusion(f32[1,1024,1024]{2,1,0:T(8,128)S(1)} %copy-done.7, f32[1,64,1024]{2,1,0:T(8,128)S(1)} %copy-done.9, f32[1,64,1024]{2,1,0:T(8,128)S(1)} %copy-done), kind=kOutput, calls=%fused_computation.19 | convolution fusion | flops 402718720 | bytes 4980736 | tf_op jit(solution)/shard_map/dot_general | solution.py:311
  30.4 1.3 %slice.4.held_ref = f32[512,512]{1,0:T(8,128)S(1)} slice(f32[2688,1024]{1,0:T(8,128)} %bitcast.52), slice={[0:512], [0:512]} | slice | bytes 2097152 | tf_op jit(solution)/shard_map/slice | solution.py:233
  31.7 4.5 %collective-permute-done = f32[64,512]{1,0:T(8,128)S(1)} collective-permute-done((f32[64,512]{1,0:T(8,128)S(1)}, f32[64,512]{1,0:T(8,128)S(1)}, u32[]{:S(2)}, u32[]{:S(2)}) %collective-permute-start) | collective-permute-done | bytes 131104 | tf_op jit(solution)/shard_map/ppermute | solution.py:25
  36.2 1.1 fusion.18
  37.4 1.1 fusion.10
  38.6 9.2 %turn.2 = (f32[64,1024]{1,0:T(8,128)S(1)}, f32[64,1024]{1,0:T(8,128)S(1)}, f32[32,48,128]{2,1,0:T(8,128)}) custom-call(s32[28]{0:T(128)S(1)} %bitcast.44, s32[28]{0:T(128)S(1)} %bitcast.48, f32[2688,1024]{1,0:T(8,128)} %bitcast.53, f32[512,512]{1,0:T(8,128)S(1)} %slice.4.held_ref, f32[32,48,128]{2,1,0:T(8,128)S(1)} %all-to-all-done.incoming_ref, ...), custom_call_target="tpu_custom_call" | custom-call | flops 2818572288 | bytes 11010048 | tf_op jit(solution)/shard_map/turn/pallas_call | solution.py:290
  47.8 3.7 %all-to-all-start.1 = ((f32[32,48,128]{2,1,0:T(8,128)}), f32[32,48,128]{2,1,0:T(8,128)S(1)}, u32[]{:S(2)}, u32[]{:S(2)}) async-start(f32[32,48,128]{2,1,0:T(8,128)} %get-tuple-element.9), calls=%async_computation.1 | async-start | bytes 1572864 | tf_op jit(solution)/shard_map/all_to_all | solution.py:303
  51.5 2.7 %collective-permute-start.3 = (f32[64,512]{1,0:T(8,128)S(1)}, f32[64,512]{1,0:T(8,128)S(1)}, u32[]{:S(2)}, u32[]{:S(2)}) collective-permute-start(f32[64,512]{1,0:T(8,128)S(1)} %get-tuple-element.17), channel_id=1, source_target_pairs={{1,0},{2,1},{3,2},{4,3},{5,4},{6,5},{7,6},{8,7},{9,8},{10,9},{11,1... | collective-permute-start | bytes 393224 | tf_op jit(solution)/shard_map/ppermute | solution.py:25
  54.2 3.6 %fusion.26 = f32[64,1024]{1,0:T(8,128)S(1)} fusion(f32[64,1024]{1,0:T(8,128)S(1)} %get-tuple-element.8.previous_ref, f32[1,1024,1024]{2,1,0:T(8,128)} %param.10), kind=kOutput, calls=%fused_computation.23 | convolution fusion | flops 402653184 | bytes 4718592 | tf_op jit(solution)/shard_map/dot_general | solution.py:309
  57.9 2.2 %fusion.2 = f32[64,1024]{1,0:T(8,128)S(1)} fusion(f32[64,1024]{1,0:T(8,128)S(1)} %get-tuple-element.8.previous_ref, f32[1,1024,1024]{2,1,0:T(8,128)S(1)} %copy-done.8), kind=kOutput, calls=%fused_computation.2 | convolution fusion | flops 402653184 | bytes 4718592 | tf_op jit(solution)/shard_map/dot_general | solution.py:311
  60.1 2.2 %collective-permute-start.4 = (f32[64,512]{1,0:T(8,128)S(1)}, f32[64,512]{1,0:T(8,128)S(1)}, u32[]{:S(2)}, u32[]{:S(2)}) collective-permute-start(f32[64,512]{1,0:T(8,128)S(1)} %get-tuple-element.16), channel_id=1, source_target_pairs={{1,0},{2,1},{3,2},{4,3},{5,4},{6,5},{7,6},{8,7},{9,8},{10,9},{11,1... | collective-permute-start | bytes 393224 | tf_op jit(solution)/shard_map/ppermute | solution.py:25
  62.3 5.2 %collective-permute-start.5 = (f32[64,1024]{1,0:T(8,128)S(1)}, f32[64,1024]{1,0:T(8,128)S(1)}, u32[]{:S(2)}, u32[]{:S(2)}) collective-permute-start(f32[64,1024]{1,0:T(8,128)S(1)} %fusion.26), channel_id=1, source_target_pairs={{0,1},{1,2},{2,3},{3,4},{4,5},{5,6},{6,7},{7,8},{8,9},{9,10},{10,1... | collective-permute-start | bytes 786440 | tf_op jit(solution)/shard_map/ppermute | solution.py:25
  67.4 4.5 %collective-permute-done.3 = f32[64,512]{1,0:T(8,128)S(1)} collective-permute-done((f32[64,512]{1,0:T(8,128)S(1)}, f32[64,512]{1,0:T(8,128)S(1)}, u32[]{:S(2)}, u32[]{:S(2)}) %collective-permute-start.3) | collective-permute-done | bytes 131104 | tf_op jit(solution)/shard_map/ppermute | solution.py:25
  72.0 1.1 fusion.14
  73.4 1.1 fusion.8
  74.6 8.4 %turn.3 = (f32[64,1024]{1,0:T(8,128)S(1)}, f32[64,1024]{1,0:T(8,128)S(1)}, f32[32,48,128]{2,1,0:T(8,128)S(1)}) custom-call(s32[28]{0:T(128)S(1)} %bitcast.45, s32[28]{0:T(128)S(1)} %bitcast.49, f32[2688,1024]{1,0:T(8,128)} %bitcast.54, f32[512,512]{1,0:T(8,128)S(1)} %slice.4.held_ref, f32[32,48,128]{2,1,0:T(8,128)S(1)} %all-to-all-done.1.incoming_ref, ...), custom_call_target="tpu_custom_call" | custom-call | flops 2818572288 | bytes 11010048 | tf_op jit(solution)/shard_map/turn/pallas_call | solution.py:290
  83.8 3.7 %all-to-all-start.2 = ((f32[32,48,128]{2,1,0:T(8,128)}), f32[32,48,128]{2,1,0:T(8,128)S(1)}, u32[]{:S(2)}, u32[]{:S(2)}) async-start(f32[32,48,128]{2,1,0:T(8,128)} %copy-done.1), calls=%async_computation.2 | async-start | bytes 1572864 | tf_op jit(solution)/shard_map/all_to_all | solution.py:303
  87.5 4.4 %fusion = f32[64,1024]{1,0:T(8,128)S(1)} fusion(f32[64,1024]{1,0:T(8,128)S(1)} %get-tuple-element.11.previous_ref, f32[1,1024,1024]{2,1,0:T(8,128)} %param.9), kind=kOutput, calls=%fused_computation | convolution fusion | flops 402653184 | bytes 4718592 | tf_op jit(solution)/shard_map/dot_general | solution.py:311
  92.0 2.3 %collective-permute-start.7 = (f32[64,512]{1,0:T(8,128)S(1)}, f32[64,512]{1,0:T(8,128)S(1)}, u32[]{:S(2)}, u32[]{:S(2)}) collective-permute-start(f32[64,512]{1,0:T(8,128)S(1)} %get-tuple-element.14), channel_id=1, source_target_pairs={{1,0},{2,1},{3,2},{4,3},{5,4},{6,5},{7,6},{8,7},{9,8},{10,9},{11,1... | collective-permute-start | bytes 393224 | tf_op jit(solution)/shard_map/ppermute | solution.py:25
  94.3 2.2 %collective-permute-start.6 = (f32[64,512]{1,0:T(8,128)S(1)}, f32[64,512]{1,0:T(8,128)S(1)}, u32[]{:S(2)}, u32[]{:S(2)}) collective-permute-start(f32[64,512]{1,0:T(8,128)S(1)} %get-tuple-element.15), channel_id=1, source_target_pairs={{1,0},{2,1},{3,2},{4,3},{5,4},{6,5},{7,6},{8,7},{9,8},{10,9},{11,1... | collective-permute-start | bytes 393224 | tf_op jit(solution)/shard_map/ppermute | solution.py:25
  96.5 1.6 %fusion.24 = f32[64,1024]{1,0:T(8,128)S(1)} fusion(f32[64,1024]{1,0:T(8,128)S(1)} %get-tuple-element.11.previous_ref, f32[1,1024,1024]{2,1,0:T(8,128)S(1)} %copy-done.6), kind=kOutput, calls=%fused_computation.21 | convolution fusion | flops 402653184 | bytes 4718592 | tf_op jit(solution)/shard_map/dot_general | solution.py:309
  98.1 5.2 %collective-permute-start.8 = (f32[64,1024]{1,0:T(8,128)S(1)}, f32[64,1024]{1,0:T(8,128)S(1)}, u32[]{:S(2)}, u32[]{:S(2)}) collective-permute-start(f32[64,1024]{1,0:T(8,128)S(1)} %fusion.24), channel_id=1, source_target_pairs={{0,1},{1,2},{2,3},{3,4},{4,5},{5,6},{6,7},{7,8},{8,9},{9,10},{10,1... | collective-permute-start | bytes 786440 | tf_op jit(solution)/shard_map/ppermute | solution.py:25
  104.0 5.4 %collective-permute-done.6 = f32[64,512]{1,0:T(8,128)S(1)} collective-permute-done((f32[64,512]{1,0:T(8,128)S(1)}, f32[64,512]{1,0:T(8,128)S(1)}, u32[]{:S(2)}, u32[]{:S(2)}) %collective-permute-start.6) | collective-permute-done | bytes 131104 | tf_op jit(solution)/shard_map/ppermute | solution.py:25
  109.4 1.1 fusion.12
  110.6 1.1 fusion.6
  111.8 5.7 %far.1 = f32[64,1024]{1,0:T(8,128)} custom-call(s32[28]{0:T(128)S(1)} %bitcast.46, s32[28]{0:T(128)S(1)} %bitcast.50, f32[2688,1024]{1,0:T(8,128)} %bitcast.55, f32[512,512]{1,0:T(8,128)S(1)} %slice.4.held_ref, f32[32,48,128]{2,1,0:T(8,128)S(1)} %all-to-all-done.2.incoming_ref, f32[64,1024]{1,0:T(8,128)S(1)} %sub.35.base_ref, ...), custom_call_target="tpu_custom_call" | custom-call | flops 1409286144 | bytes 11010048 | tf_op jit(solution)/shard_map/far/pallas_call | solution.py:290
  (40 shorter events, 2.2 us)
Async XLA Ops:
  0.6 13.7 %copy-start = (f32[1,64,1024]{2,1,0:T(8,128)S(1)}, f32[1,64,1024]{2,1,0:T(8,128)}, u32[]{:S(2)}) copy-start(f32[1,64,1024]{2,1,0:T(8,128)} %param.8) | copy-start | bytes 786436
  8.1 20.2 %copy-start.9 = (f32[1,64,1024]{2,1,0:T(8,128)S(1)}, f32[1,64,1024]{2,1,0:T(8,128)}, u32[]{:S(2)}) copy-start(f32[1,64,1024]{2,1,0:T(8,128)} %param.7) | copy-start | bytes 786436
  8.1 30.5 %all-to-all-start = ((f32[32,48,128]{2,1,0:T(8,128)}), f32[32,48,128]{2,1,0:T(8,128)S(1)}, u32[]{:S(2)}, u32[]{:S(2)}) async-start(f32[32,48,128]{2,1,0:T(8,128)} %project.1), calls=%async_computation | async-start | bytes 1572864 | tf_op jit(solution)/shard_map/all_to_all | solution.py:303
  14.3 13.9 %copy-start.7 = (f32[1,1024,1024]{2,1,0:T(8,128)S(1)}, f32[1,1024,1024]{2,1,0:T(8,128)}, u32[]{:S(2)}) copy-start(f32[1,1024,1024]{2,1,0:T(8,128)} %param.9) | copy-start | bytes 12582916
  14.4 23.0 %collective-permute-start.1 = (f32[64,512]{1,0:T(8,128)S(1)}, f32[64,512]{1,0:T(8,128)S(1)}, u32[]{:S(2)}, u32[]{:S(2)}) collective-permute-start(f32[64,512]{1,0:T(8,128)S(1)} %get-tuple-element.18), channel_id=1, source_target_pairs={{1,0},{2,1},{3,2},{4,3},{5,4},{6,5},{7,6},{8,7},{9,8},{10,9},{11,1... | collective-permute-start | bytes 393224 | tf_op jit(solution)/shard_map/ppermute | solution.py:25
  17.0 19.3 %collective-permute-start = (f32[64,512]{1,0:T(8,128)S(1)}, f32[64,512]{1,0:T(8,128)S(1)}, u32[]{:S(2)}, u32[]{:S(2)}) collective-permute-start(f32[64,512]{1,0:T(8,128)S(1)} %get-tuple-element.19), channel_id=1, source_target_pairs={{1,0},{2,1},{3,2},{4,3},{5,4},{6,5},{7,6},{8,7},{9,8},{10,9},{11,1... | collective-permute-start | bytes 393224 | tf_op jit(solution)/shard_map/ppermute | solution.py:25
  22.8 13.5 %copy-start.4 = (f32[1,1024,1024]{2,1,0:T(8,128)S(1)}, f32[1,1024,1024]{2,1,0:T(8,128)}, u32[]{:S(2)}) copy-start(f32[1,1024,1024]{2,1,0:T(8,128)} %param.10) | copy-start | bytes 12582916
  22.8 15.8 %collective-permute-start.2 = (f32[64,1024]{1,0:T(8,128)S(1)}, f32[64,1024]{1,0:T(8,128)S(1)}, u32[]{:S(2)}, u32[]{:S(2)}) collective-permute-start(f32[64,1024]{1,0:T(8,128)S(1)} %fusion.28), channel_id=1, source_target_pairs={{0,1},{1,2},{2,3},{3,4},{4,5},{5,6},{6,7},{7,8},{8,9},{9,10},{10,1... | collective-permute-start | bytes 786440 | tf_op jit(solution)/shard_map/ppermute | solution.py:25
  30.4 8.2 %copy-start.2 = (s32[1,28]{1,0:T(1,128)S(1)}, s32[1,28]{1,0:T(1,128)}, u32[]{:S(2)}) copy-start(s32[1,28]{1,0:T(1,128)} %param.12) | copy-start | bytes 340
  30.4 8.2 %copy-start.3 = (s32[1,28]{1,0:T(1,128)S(1)}, s32[1,28]{1,0:T(1,128)}, u32[]{:S(2)}) copy-start(s32[1,28]{1,0:T(1,128)} %param.13) | copy-start | bytes 340
  47.8 26.7 %all-to-all-start.1 = ((f32[32,48,128]{2,1,0:T(8,128)}), f32[32,48,128]{2,1,0:T(8,128)S(1)}, u32[]{:S(2)}, u32[]{:S(2)}) async-start(f32[32,48,128]{2,1,0:T(8,128)} %get-tuple-element.9), calls=%async_computation.1 | async-start | bytes 1572864 | tf_op jit(solution)/shard_map/all_to_all | solution.py:303
  51.5 6.4 %copy-start.8 = (f32[1,1024,1024]{2,1,0:T(8,128)S(1)}, f32[1,1024,1024]{2,1,0:T(8,128)}, u32[]{:S(2)}) copy-start(f32[1,1024,1024]{2,1,0:T(8,128)} %param.9) | copy-start | bytes 12582916
  51.5 20.4 %copy-start.5 = (f32[1,1024,1024]{2,1,0:T(8,128)S(1)}, f32[1,1024,1024]{2,1,0:T(8,128)}, u32[]{:S(2)}) copy-start(f32[1,1024,1024]{2,1,0:T(8,128)} %param.10) | copy-start | bytes 12582916
  51.5 20.4 %collective-permute-start.3 = (f32[64,512]{1,0:T(8,128)S(1)}, f32[64,512]{1,0:T(8,128)S(1)}, u32[]{:S(2)}, u32[]{:S(2)}) collective-permute-start(f32[64,512]{1,0:T(8,128)S(1)} %get-tuple-element.17), channel_id=1, source_target_pairs={{1,0},{2,1},{3,2},{4,3},{5,4},{6,5},{7,6},{8,7},{9,8},{10,9},{11,1... | collective-permute-start | bytes 393224 | tf_op jit(solution)/shard_map/ppermute | solution.py:25
  60.1 13.3 %collective-permute-start.4 = (f32[64,512]{1,0:T(8,128)S(1)}, f32[64,512]{1,0:T(8,128)S(1)}, u32[]{:S(2)}, u32[]{:S(2)}) collective-permute-start(f32[64,512]{1,0:T(8,128)S(1)} %get-tuple-element.16), channel_id=1, source_target_pairs={{1,0},{2,1},{3,2},{4,3},{5,4},{6,5},{7,6},{8,7},{9,8},{10,9},{11,1... | collective-permute-start | bytes 393224 | tf_op jit(solution)/shard_map/ppermute | solution.py:25
  62.3 12.3 %collective-permute-start.5 = (f32[64,1024]{1,0:T(8,128)S(1)}, f32[64,1024]{1,0:T(8,128)S(1)}, u32[]{:S(2)}, u32[]{:S(2)}) collective-permute-start(f32[64,1024]{1,0:T(8,128)S(1)} %fusion.26), channel_id=1, source_target_pairs={{0,1},{1,2},{2,3},{3,4},{4,5},{5,6},{6,7},{7,8},{8,9},{9,10},{10,1... | collective-permute-start | bytes 786440 | tf_op jit(solution)/shard_map/ppermute | solution.py:25
  83.0 0.9 copy-start.1
  83.8 27.9 %all-to-all-start.2 = ((f32[32,48,128]{2,1,0:T(8,128)}), f32[32,48,128]{2,1,0:T(8,128)S(1)}, u32[]{:S(2)}, u32[]{:S(2)}) async-start(f32[32,48,128]{2,1,0:T(8,128)} %copy-done.1), calls=%async_computation.2 | async-start | bytes 1572864 | tf_op jit(solution)/shard_map/all_to_all | solution.py:303
  87.5 9.0 %copy-start.6 = (f32[1,1024,1024]{2,1,0:T(8,128)S(1)}, f32[1,1024,1024]{2,1,0:T(8,128)}, u32[]{:S(2)}) copy-start(f32[1,1024,1024]{2,1,0:T(8,128)} %param.10) | copy-start | bytes 12582916
  92.0 18.6 %collective-permute-start.7 = (f32[64,512]{1,0:T(8,128)S(1)}, f32[64,512]{1,0:T(8,128)S(1)}, u32[]{:S(2)}, u32[]{:S(2)}) collective-permute-start(f32[64,512]{1,0:T(8,128)S(1)} %get-tuple-element.14), channel_id=1, source_target_pairs={{1,0},{2,1},{3,2},{4,3},{5,4},{6,5},{7,6},{8,7},{9,8},{10,9},{11,1... | collective-permute-start | bytes 393224 | tf_op jit(solution)/shard_map/ppermute | solution.py:25
  94.3 15.1 %collective-permute-start.6 = (f32[64,512]{1,0:T(8,128)S(1)}, f32[64,512]{1,0:T(8,128)S(1)}, u32[]{:S(2)}, u32[]{:S(2)}) collective-permute-start(f32[64,512]{1,0:T(8,128)S(1)} %get-tuple-element.15), channel_id=1, source_target_pairs={{1,0},{2,1},{3,2},{4,3},{5,4},{6,5},{7,6},{8,7},{9,8},{10,9},{11,1... | collective-permute-start | bytes 393224 | tf_op jit(solution)/shard_map/ppermute | solution.py:25
  98.1 13.7 %collective-permute-start.8 = (f32[64,1024]{1,0:T(8,128)S(1)}, f32[64,1024]{1,0:T(8,128)S(1)}, u32[]{:S(2)}, u32[]{:S(2)}) collective-permute-start(f32[64,1024]{1,0:T(8,128)S(1)} %fusion.24), channel_id=1, source_target_pairs={{0,1},{1,2},{2,3},{3,4},{4,5},{5,6},{6,7},{7,8},{8,9},{9,10},{10,1... | collective-permute-start | bytes 786440 | tf_op jit(solution)/shard_map/ppermute | solution.py:25

commit v6 on v5

--- a/solution.py
+++ b/solution.py
@@ -90,26 +90,30 @@
     sums_ref[...] = total if first else sums_ref[...] + total
 
 
-def project_last(split_ref, vectors, sums_ref, width, partner_ref, ranks_ref, outgoing_ref):
-    operand = operand_of(vectors)
-    rows, lanes = sums_ref.shape
+def store_chunks(slots, total, width, partner_ref, ranks_ref, outgoing_ref):
+    lanes = total.shape[1]
     half = width // 2
     own = lax.axis_index(AXES)
     left = lax.broadcasted_iota(jnp.int32, (half, lanes), 1) < lanes // 2
     rank_index = lax.broadcasted_iota(jnp.int32, (half, lanes), 0) + jnp.where(left, 0, half)
-    slots = rows // width
+    total = total + pltpu.roll(total, lanes // 2, 1)
+    for inner, slot in enumerate(slots):
+        base = inner * width
+        chunk = jnp.where(left, total[base:base + half], total[base + half:base + width])
+        chunk = jnp.where(rank_index < ranks_ref[slot], chunk, 0.0)
+        place = partner_ref[slot]
+        outgoing_ref[jnp.where(place >= 0, place, own)] = chunk
+
+
+def project_last(split_ref, vectors, sums_ref, width, partner_ref, ranks_ref, outgoing_ref):
+    operand = operand_of(vectors)
+    slots = sums_ref.shape[0] // width
     together = -(-slots // 4)
     for at in range(0, slots, together):
         end = min(at + together, slots)
         some = slice(at * width, end * width)
         total = sums_ref[some, :] + product(split_ref[some, :operand.shape[0]], operand, NN)
-        total = total + pltpu.roll(total, lanes // 2, 1)
-        for slot in range(at, end):
-            base = (slot - at) * width
-            chunk = jnp.where(left, total[base:base + half], total[base + half:base + width])
-            chunk = jnp.where(rank_index < ranks_ref[slot], chunk, 0.0)
-            place = partner_ref[slot]
-            outgoing_ref[jnp.where(place >= 0, place, own)] = chunk
+        store_chunks(range(at, end), total, width, partner_ref, ranks_ref, outgoing_ref)
 
 
 def apart(partner_ref):
@@ -144,9 +148,9 @@
     each_slot(slots, visit)
 
 
-def project_kernel(rectangles, width, partner_hbm, ranks_hbm, vectors_hbm, factors_ref,
-                   outgoing_ref, buffer, semaphore, split_ref, sums_ref, partner_ref, ranks_ref,
-                   vectors_ref, small_semaphore):
+def project_kernel(groups, width, partner_hbm, ranks_hbm, vectors_hbm, factors_ref,
+                   outgoing_ref, buffer, semaphore, split_ref, partner_ref, ranks_ref,
+                   vectors_ref, operand_ref, small_semaphore):
     small = [
         pltpu.make_async_copy(source, target, small_semaphore.at[index])
         for index, (source, target) in enumerate((
@@ -155,21 +159,25 @@
     ]
     for copy in small:
         copy.start()
-    pieces = Pieces(rectangles, factors_ref, buffer, semaphore, split_ref)
+    points = factors_ref.shape[1]
+    rectangles = [((first * width, last * width), (0, points)) for first, last in groups]
+    pieces = Pieces(rectangles, factors_ref, buffer, semaphore, None)
     pieces.start()
     for copy in small:
         copy.wait()
-    for index, (_, columns) in enumerate(rectangles):
+    operand_ref[...] = operand_of(vectors_ref[...])
+    for index, (first, last) in enumerate(groups):
+        rows = (last - first) * width
+
         @apart(partner_ref)
         def _():
-            pieces.load(index)
-            vectors = vectors_ref[:, slice(*columns)]
-            if index + 1 < len(rectangles):
-                project(split_ref, vectors, sums_ref, index == 0)
-            else:
-                project_last(
-                    split_ref, vectors, sums_ref, width, partner_ref, ranks_ref, outgoing_ref
-                )
+            pieces.copy(index).wait()
+            high, low = halves(buffer[first * width:last * width])
+            split_ref[:rows, :points], split_ref[:rows, points:] = high, low
+            total = product(split_ref[:rows, :], operand_ref[...], NN)
+            store_chunks(
+                range(first, last), total, width, partner_ref, ranks_ref, outgoing_ref
+            )
 
 
 def turn_kernel(weights, rectangles, width, partner_ref, ranks_ref, factors_ref, held_ref,
@@ -228,7 +236,8 @@
     chunks = jax.ShapeDtypeStruct((device_count, rank_width // 2, 2 * n), jnp.float32)
     factor_block = factor_block.reshape(rows, points)
     middle, quarter = points // 2, points // 4
-    by_columns = [((0, rows), (at, at + quarter)) for at in range(0, points, quarter)]
+    together = -(-slots // 2)
+    groups = [(at, min(at + together, slots)) for at in range(0, slots, together)]
     held_rows = 512
     held = factor_block[:held_rows, :middle]
     factor_block = pltpu.with_memory_space_constraint(factor_block, pltpu.HBM)
@@ -267,15 +276,18 @@
 
     def projected(vectors):
         return pl.pallas_call(
-            functools.partial(project_kernel, by_columns, rank_width),
+            functools.partial(project_kernel, groups, rank_width),
             out_shape=chunks,
             in_specs=[ANY_SPEC] * 4,
             out_specs=VMEM_SPEC,
-            scratch_shapes=loading(by_columns) + [
-                sums,
+            scratch_shapes=[
+                pltpu.VMEM((rows, points), jnp.float32),
+                pltpu.SemaphoreType.DMA((len(groups),)),
+                pltpu.VMEM((together * rank_width, 2 * points), jnp.bfloat16),
                 pltpu.SMEM((slots,), jnp.int32),
                 pltpu.SMEM((slots,), jnp.int32),
                 pltpu.VMEM((n, points), jnp.float32),
+                pltpu.VMEM((2 * points, 2 * n), jnp.bfloat16),
                 pltpu.SemaphoreType.DMA((3,)),
             ],
             compiler_params=params,

time: 118 us -> 118 us (level)
  no operation moved by 1% of the time
where the time goes in v6:
time: 118 us; the launch traced here: 117 us
  starting transfers between devices  43.5 us (37%)
  Pallas kernels  30.3 us (26%)
  matrix products  24.3 us (21%)
  waiting for transfers between devices  14.7 us (12%)
  local copies, waits for them, and re-layouts  2.3 us (2%)
  between operations  1.23 us (1%)
    ppermute x9, starting transfers between devices, from_behind(): return lax.ppermute(block, AXES, route)  29.9 us
    pallas_call x3, Pallas kernels, turn(): pl.pallas_call(functools.partial(turn_kernel, weights, rectangles, rank_w...  23.3 us
    ppermute x9, waiting for transfers between devices, from_behind(): return lax.ppermute(block, AXES, route)  14.7 us
    all_to_all x3, starting transfers between devices, finish(): lax.all_to_all(outgoing, AXES, split_axis=0, concat_axis=0, tiled=True)  13.6 us
    dot_general x3, matrix products, finish(): carried = lax.dot_general(vectors, neighbour_block, NN, precision=exact)  8.8 us
    dot_general x3, matrix products, finish(): partial = before - lax.dot_general(vectors, diag_block, NT, precision=exact)  8.68 us
    pallas_call x1, Pallas kernels, projected(): pl.pallas_call(functools.partial(project_kernel, groups, rank_width), out...  6.99 us
    dot_general x6, matrix products, finish(): lax.dot_general(part, tile, NT, precision=exact)  6.79 us
  transfers between devices with their start and end apart: 12, of which 4 were waited for; matrix products, arithmetic and copies ran while one was open for 23% of the time, Pallas kernels for 0%

profile of v6, /device:TPU:15, one launch (start us, length us, event | category | flops | bytes accessed | tf_op | source)
XLA Modules:
  0.0 117.3 jit_solution(631812606085654332)
XLA Ops:
  0.6 7.0 %project.1 = f32[32,48,128]{2,1,0:T(8,128)} custom-call(s32[28]{0:T(128)} %bitcast.43, s32[28]{0:T(128)} %bitcast.47, f32[64,1024]{1,0:T(8,128)} %bitcast.40, f32[2688,1024]{1,0:T(8,128)} %bitcast.51), custom_call_target="tpu_custom_call" | custom-call | flops 1409286144 | bytes 11010048 | tf_op jit(solution)/shard_map/project/pallas_call | solution.py:278
  7.6 6.2 %all-to-all-start = ((f32[32,48,128]{2,1,0:T(8,128)}), f32[32,48,128]{2,1,0:T(8,128)S(1)}, u32[]{:S(2)}, u32[]{:S(2)}) async-start(f32[32,48,128]{2,1,0:T(8,128)} %project.1), calls=%async_computation | async-start | bytes 1572864 | tf_op jit(solution)/shard_map/all_to_all | solution.py:315
  13.9 2.6 %collective-permute-start.1 = (f32[64,512]{1,0:T(8,128)S(1)}, f32[64,512]{1,0:T(8,128)S(1)}, u32[]{:S(2)}, u32[]{:S(2)}) collective-permute-start(f32[64,512]{1,0:T(8,128)S(1)} %get-tuple-element.18), channel_id=1, source_target_pairs={{1,0},{2,1},{3,2},{4,3},{5,4},{6,5},{7,6},{8,7},{9,8},{10,9},{11,1... | collective-permute-start | bytes 393224 | tf_op jit(solution)/shard_map/ppermute | solution.py:25
  16.5 2.2 %collective-permute-start = (f32[64,512]{1,0:T(8,128)S(1)}, f32[64,512]{1,0:T(8,128)S(1)}, u32[]{:S(2)}, u32[]{:S(2)}) collective-permute-start(f32[64,512]{1,0:T(8,128)S(1)} %get-tuple-element.19), channel_id=1, source_target_pairs={{1,0},{2,1},{3,2},{4,3},{5,4},{6,5},{7,6},{8,7},{9,8},{10,9},{11,1... | collective-permute-start | bytes 393224 | tf_op jit(solution)/shard_map/ppermute | solution.py:25
  18.7 3.6 %fusion.28 = f32[64,1024]{1,0:T(8,128)S(1)} fusion(f32[1,1024,1024]{2,1,0:T(8,128)} %param.10, f32[1,64,1024]{2,1,0:T(8,128)S(1)} %copy-done), kind=kOutput, calls=%fused_computation.25 | convolution fusion | flops 402653184 | bytes 4718592 | tf_op jit(solution)/shard_map/dot_general | solution.py:321
  22.3 5.4 %collective-permute-start.2 = (f32[64,1024]{1,0:T(8,128)S(1)}, f32[64,1024]{1,0:T(8,128)S(1)}, u32[]{:S(2)}, u32[]{:S(2)}) collective-permute-start(f32[64,1024]{1,0:T(8,128)S(1)} %fusion.28), channel_id=1, source_target_pairs={{0,1},{1,2},{2,3},{3,4},{4,5},{5,6},{6,7},{7,8},{8,9},{9,10},{10,1... | collective-permute-start | bytes 786440 | tf_op jit(solution)/shard_map/ppermute | solution.py:25
  27.8 2.2 %fusion.21 = f32[64,1024]{1,0:T(8,128)S(1)} fusion(f32[1,1024,1024]{2,1,0:T(8,128)S(1)} %copy-done.7, f32[1,64,1024]{2,1,0:T(8,128)S(1)} %copy-done.9, f32[1,64,1024]{2,1,0:T(8,128)S(1)} %copy-done), kind=kOutput, calls=%fused_computation.19 | convolution fusion | flops 402718720 | bytes 4980736 | tf_op jit(solution)/shard_map/dot_general | solution.py:323
  30.0 1.3 %slice.4.held_ref = f32[512,512]{1,0:T(8,128)S(1)} slice(f32[2688,1024]{1,0:T(8,128)} %bitcast.52), slice={[0:512], [0:512]} | slice | bytes 2097152 | tf_op jit(solution)/shard_map/slice | solution.py:242
  31.3 4.5 %collective-permute-done = f32[64,512]{1,0:T(8,128)S(1)} collective-permute-done((f32[64,512]{1,0:T(8,128)S(1)}, f32[64,512]{1,0:T(8,128)S(1)}, u32[]{:S(2)}, u32[]{:S(2)}) %collective-permute-start) | collective-permute-done | bytes 131104 | tf_op jit(solution)/shard_map/ppermute | solution.py:25
  35.8 1.1 fusion.18
  36.9 1.1 fusion.10
  38.1 9.2 %turn.2 = (f32[64,1024]{1,0:T(8,128)S(1)}, f32[64,1024]{1,0:T(8,128)S(1)}, f32[32,48,128]{2,1,0:T(8,128)}) custom-call(s32[28]{0:T(128)S(1)} %bitcast.44, s32[28]{0:T(128)S(1)} %bitcast.48, f32[2688,1024]{1,0:T(8,128)} %bitcast.53, f32[512,512]{1,0:T(8,128)S(1)} %slice.4.held_ref, f32[32,48,128]{2,1,0:T(8,128)S(1)} %all-to-all-done.incoming_ref, ...), custom_call_target="tpu_custom_call" | custom-call | flops 2818572288 | bytes 11010048 | tf_op jit(solution)/shard_map/turn/pallas_call | solution.py:302
  47.4 3.7 %all-to-all-start.1 = ((f32[32,48,128]{2,1,0:T(8,128)}), f32[32,48,128]{2,1,0:T(8,128)S(1)}, u32[]{:S(2)}, u32[]{:S(2)}) async-start(f32[32,48,128]{2,1,0:T(8,128)} %get-tuple-element.9), calls=%async_computation.1 | async-start | bytes 1572864 | tf_op jit(solution)/shard_map/all_to_all | solution.py:315
  51.1 2.7 %collective-permute-start.3 = (f32[64,512]{1,0:T(8,128)S(1)}, f32[64,512]{1,0:T(8,128)S(1)}, u32[]{:S(2)}, u32[]{:S(2)}) collective-permute-start(f32[64,512]{1,0:T(8,128)S(1)} %get-tuple-element.17), channel_id=1, source_target_pairs={{1,0},{2,1},{3,2},{4,3},{5,4},{6,5},{7,6},{8,7},{9,8},{10,9},{11,1... | collective-permute-start | bytes 393224 | tf_op jit(solution)/shard_map/ppermute | solution.py:25
  53.8 3.6 %fusion.26 = f32[64,1024]{1,0:T(8,128)S(1)} fusion(f32[64,1024]{1,0:T(8,128)S(1)} %get-tuple-element.8.previous_ref, f32[1,1024,1024]{2,1,0:T(8,128)} %param.10), kind=kOutput, calls=%fused_computation.23 | convolution fusion | flops 402653184 | bytes 4718592 | tf_op jit(solution)/shard_map/dot_general | solution.py:321
  57.4 2.2 %fusion.2 = f32[64,1024]{1,0:T(8,128)S(1)} fusion(f32[64,1024]{1,0:T(8,128)S(1)} %get-tuple-element.8.previous_ref, f32[1,1024,1024]{2,1,0:T(8,128)S(1)} %copy-done.8), kind=kOutput, calls=%fused_computation.2 | convolution fusion | flops 402653184 | bytes 4718592 | tf_op jit(solution)/shard_map/dot_general | solution.py:323
  59.6 2.2 %collective-permute-start.4 = (f32[64,512]{1,0:T(8,128)S(1)}, f32[64,512]{1,0:T(8,128)S(1)}, u32[]{:S(2)}, u32[]{:S(2)}) collective-permute-start(f32[64,512]{1,0:T(8,128)S(1)} %get-tuple-element.16), channel_id=1, source_target_pairs={{1,0},{2,1},{3,2},{4,3},{5,4},{6,5},{7,6},{8,7},{9,8},{10,9},{11,1... | collective-permute-start | bytes 393224 | tf_op jit(solution)/shard_map/ppermute | solution.py:25
  61.8 5.2 %collective-permute-start.5 = (f32[64,1024]{1,0:T(8,128)S(1)}, f32[64,1024]{1,0:T(8,128)S(1)}, u32[]{:S(2)}, u32[]{:S(2)}) collective-permute-start(f32[64,1024]{1,0:T(8,128)S(1)} %fusion.26), channel_id=1, source_target_pairs={{0,1},{1,2},{2,3},{3,4},{4,5},{5,6},{6,7},{7,8},{8,9},{9,10},{10,1... | collective-permute-start | bytes 786440 | tf_op jit(solution)/shard_map/ppermute | solution.py:25
  67.0 4.5 %collective-permute-done.3 = f32[64,512]{1,0:T(8,128)S(1)} collective-permute-done((f32[64,512]{1,0:T(8,128)S(1)}, f32[64,512]{1,0:T(8,128)S(1)}, u32[]{:S(2)}, u32[]{:S(2)}) %collective-permute-start.3) | collective-permute-done | bytes 131104 | tf_op jit(solution)/shard_map/ppermute | solution.py:25
  71.5 1.1 fusion.14
  72.9 1.1 fusion.8
  74.1 8.4 %turn.3 = (f32[64,1024]{1,0:T(8,128)S(1)}, f32[64,1024]{1,0:T(8,128)S(1)}, f32[32,48,128]{2,1,0:T(8,128)S(1)}) custom-call(s32[28]{0:T(128)S(1)} %bitcast.45, s32[28]{0:T(128)S(1)} %bitcast.49, f32[2688,1024]{1,0:T(8,128)} %bitcast.54, f32[512,512]{1,0:T(8,128)S(1)} %slice.4.held_ref, f32[32,48,128]{2,1,0:T(8,128)S(1)} %all-to-all-done.1.incoming_ref, ...), custom_call_target="tpu_custom_call" | custom-call | flops 2818572288 | bytes 11010048 | tf_op jit(solution)/shard_map/turn/pallas_call | solution.py:302
  83.4 3.7 %all-to-all-start.2 = ((f32[32,48,128]{2,1,0:T(8,128)}), f32[32,48,128]{2,1,0:T(8,128)S(1)}, u32[]{:S(2)}, u32[]{:S(2)}) async-start(f32[32,48,128]{2,1,0:T(8,128)} %copy-done.1), calls=%async_computation.2 | async-start | bytes 1572864 | tf_op jit(solution)/shard_map/all_to_all | solution.py:315
  87.1 4.4 %fusion = f32[64,1024]{1,0:T(8,128)S(1)} fusion(f32[64,1024]{1,0:T(8,128)S(1)} %get-tuple-element.11.previous_ref, f32[1,1024,1024]{2,1,0:T(8,128)} %param.9), kind=kOutput, calls=%fused_computation | convolution fusion | flops 402653184 | bytes 4718592 | tf_op jit(solution)/shard_map/dot_general | solution.py:323
  91.5 2.3 %collective-permute-start.7 = (f32[64,512]{1,0:T(8,128)S(1)}, f32[64,512]{1,0:T(8,128)S(1)}, u32[]{:S(2)}, u32[]{:S(2)}) collective-permute-start(f32[64,512]{1,0:T(8,128)S(1)} %get-tuple-element.14), channel_id=1, source_target_pairs={{1,0},{2,1},{3,2},{4,3},{5,4},{6,5},{7,6},{8,7},{9,8},{10,9},{11,1... | collective-permute-start | bytes 393224 | tf_op jit(solution)/shard_map/ppermute | solution.py:25
  93.8 2.2 %collective-permute-start.6 = (f32[64,512]{1,0:T(8,128)S(1)}, f32[64,512]{1,0:T(8,128)S(1)}, u32[]{:S(2)}, u32[]{:S(2)}) collective-permute-start(f32[64,512]{1,0:T(8,128)S(1)} %get-tuple-element.15), channel_id=1, source_target_pairs={{1,0},{2,1},{3,2},{4,3},{5,4},{6,5},{7,6},{8,7},{9,8},{10,9},{11,1... | collective-permute-start | bytes 393224 | tf_op jit(solution)/shard_map/ppermute | solution.py:25
  96.0 1.6 %fusion.24 = f32[64,1024]{1,0:T(8,128)S(1)} fusion(f32[64,1024]{1,0:T(8,128)S(1)} %get-tuple-element.11.previous_ref, f32[1,1024,1024]{2,1,0:T(8,128)S(1)} %copy-done.6), kind=kOutput, calls=%fused_computation.21 | convolution fusion | flops 402653184 | bytes 4718592 | tf_op jit(solution)/shard_map/dot_general | solution.py:321
  97.6 5.2 %collective-permute-start.8 = (f32[64,1024]{1,0:T(8,128)S(1)}, f32[64,1024]{1,0:T(8,128)S(1)}, u32[]{:S(2)}, u32[]{:S(2)}) collective-permute-start(f32[64,1024]{1,0:T(8,128)S(1)} %fusion.24), channel_id=1, source_target_pairs={{0,1},{1,2},{2,3},{3,4},{4,5},{5,6},{6,7},{7,8},{8,9},{9,10},{10,1... | collective-permute-start | bytes 786440 | tf_op jit(solution)/shard_map/ppermute | solution.py:25
  103.6 5.4 %collective-permute-done.6 = f32[64,512]{1,0:T(8,128)S(1)} collective-permute-done((f32[64,512]{1,0:T(8,128)S(1)}, f32[64,512]{1,0:T(8,128)S(1)}, u32[]{:S(2)}, u32[]{:S(2)}) %collective-permute-start.6) | collective-permute-done | bytes 131104 | tf_op jit(solution)/shard_map/ppermute | solution.py:25
  109.0 1.1 fusion.12
  110.1 1.1 fusion.6
  111.3 5.7 %far.1 = f32[64,1024]{1,0:T(8,128)} custom-call(s32[28]{0:T(128)S(1)} %bitcast.46, s32[28]{0:T(128)S(1)} %bitcast.50, f32[2688,1024]{1,0:T(8,128)} %bitcast.55, f32[512,512]{1,0:T(8,128)S(1)} %slice.4.held_ref, f32[32,48,128]{2,1,0:T(8,128)S(1)} %all-to-all-done.2.incoming_ref, f32[64,1024]{1,0:T(8,128)S(1)} %sub.35.base_ref, ...), custom_call_target="tpu_custom_call" | custom-call | flops 1409286144 | bytes 11010048 | tf_op jit(solution)/shard_map/far/pallas_call | solution.py:302
  (40 shorter events, 2.2 us)
Async XLA Ops:
  0.6 13.3 %copy-start = (f32[1,64,1024]{2,1,0:T(8,128)S(1)}, f32[1,64,1024]{2,1,0:T(8,128)}, u32[]{:S(2)}) copy-start(f32[1,64,1024]{2,1,0:T(8,128)} %param.8) | copy-start | bytes 786436
  7.6 20.2 %copy-start.9 = (f32[1,64,1024]{2,1,0:T(8,128)S(1)}, f32[1,64,1024]{2,1,0:T(8,128)}, u32[]{:S(2)}) copy-start(f32[1,64,1024]{2,1,0:T(8,128)} %param.7) | copy-start | bytes 786436
  7.6 30.5 %all-to-all-start = ((f32[32,48,128]{2,1,0:T(8,128)}), f32[32,48,128]{2,1,0:T(8,128)S(1)}, u32[]{:S(2)}, u32[]{:S(2)}) async-start(f32[32,48,128]{2,1,0:T(8,128)} %project.1), calls=%async_computation | async-start | bytes 1572864 | tf_op jit(solution)/shard_map/all_to_all | solution.py:315
  13.9 13.9 %copy-start.7 = (f32[1,1024,1024]{2,1,0:T(8,128)S(1)}, f32[1,1024,1024]{2,1,0:T(8,128)}, u32[]{:S(2)}) copy-start(f32[1,1024,1024]{2,1,0:T(8,128)} %param.9) | copy-start | bytes 12582916
  13.9 23.0 %collective-permute-start.1 = (f32[64,512]{1,0:T(8,128)S(1)}, f32[64,512]{1,0:T(8,128)S(1)}, u32[]{:S(2)}, u32[]{:S(2)}) collective-permute-start(f32[64,512]{1,0:T(8,128)S(1)} %get-tuple-element.18), channel_id=1, source_target_pairs={{1,0},{2,1},{3,2},{4,3},{5,4},{6,5},{7,6},{8,7},{9,8},{10,9},{11,1... | collective-permute-start | bytes 393224 | tf_op jit(solution)/shard_map/ppermute | solution.py:25
  16.5 19.3 %collective-permute-start = (f32[64,512]{1,0:T(8,128)S(1)}, f32[64,512]{1,0:T(8,128)S(1)}, u32[]{:S(2)}, u32[]{:S(2)}) collective-permute-start(f32[64,512]{1,0:T(8,128)S(1)} %get-tuple-element.19), channel_id=1, source_target_pairs={{1,0},{2,1},{3,2},{4,3},{5,4},{6,5},{7,6},{8,7},{9,8},{10,9},{11,1... | collective-permute-start | bytes 393224 | tf_op jit(solution)/shard_map/ppermute | solution.py:25
  22.3 13.5 %copy-start.4 = (f32[1,1024,1024]{2,1,0:T(8,128)S(1)}, f32[1,1024,1024]{2,1,0:T(8,128)}, u32[]{:S(2)}) copy-start(f32[1,1024,1024]{2,1,0:T(8,128)} %param.10) | copy-start | bytes 12582916
  22.3 15.8 %collective-permute-start.2 = (f32[64,1024]{1,0:T(8,128)S(1)}, f32[64,1024]{1,0:T(8,128)S(1)}, u32[]{:S(2)}, u32[]{:S(2)}) collective-permute-start(f32[64,1024]{1,0:T(8,128)S(1)} %fusion.28), channel_id=1, source_target_pairs={{0,1},{1,2},{2,3},{3,4},{4,5},{5,6},{6,7},{7,8},{8,9},{9,10},{10,1... | collective-permute-start | bytes 786440 | tf_op jit(solution)/shard_map/ppermute | solution.py:25
  30.0 8.2 %copy-start.2 = (s32[1,28]{1,0:T(1,128)S(1)}, s32[1,28]{1,0:T(1,128)}, u32[]{:S(2)}) copy-start(s32[1,28]{1,0:T(1,128)} %param.12) | copy-start | bytes 340
  30.0 8.2 %copy-start.3 = (s32[1,28]{1,0:T(1,128)S(1)}, s32[1,28]{1,0:T(1,128)}, u32[]{:S(2)}) copy-start(s32[1,28]{1,0:T(1,128)} %param.13) | copy-start | bytes 340
  47.4 26.7 %all-to-all-start.1 = ((f32[32,48,128]{2,1,0:T(8,128)}), f32[32,48,128]{2,1,0:T(8,128)S(1)}, u32[]{:S(2)}, u32[]{:S(2)}) async-start(f32[32,48,128]{2,1,0:T(8,128)} %get-tuple-element.9), calls=%async_computation.1 | async-start | bytes 1572864 | tf_op jit(solution)/shard_map/all_to_all | solution.py:315
  51.0 6.4 %copy-start.8 = (f32[1,1024,1024]{2,1,0:T(8,128)S(1)}, f32[1,1024,1024]{2,1,0:T(8,128)}, u32[]{:S(2)}) copy-start(f32[1,1024,1024]{2,1,0:T(8,128)} %param.9) | copy-start | bytes 12582916
  51.1 20.4 %copy-start.5 = (f32[1,1024,1024]{2,1,0:T(8,128)S(1)}, f32[1,1024,1024]{2,1,0:T(8,128)}, u32[]{:S(2)}) copy-start(f32[1,1024,1024]{2,1,0:T(8,128)} %param.10) | copy-start | bytes 12582916
  51.1 20.4 %collective-permute-start.3 = (f32[64,512]{1,0:T(8,128)S(1)}, f32[64,512]{1,0:T(8,128)S(1)}, u32[]{:S(2)}, u32[]{:S(2)}) collective-permute-start(f32[64,512]{1,0:T(8,128)S(1)} %get-tuple-element.17), channel_id=1, source_target_pairs={{1,0},{2,1},{3,2},{4,3},{5,4},{6,5},{7,6},{8,7},{9,8},{10,9},{11,1... | collective-permute-start | bytes 393224 | tf_op jit(solution)/shard_map/ppermute | solution.py:25
  59.6 13.3 %collective-permute-start.4 = (f32[64,512]{1,0:T(8,128)S(1)}, f32[64,512]{1,0:T(8,128)S(1)}, u32[]{:S(2)}, u32[]{:S(2)}) collective-permute-start(f32[64,512]{1,0:T(8,128)S(1)} %get-tuple-element.16), channel_id=1, source_target_pairs={{1,0},{2,1},{3,2},{4,3},{5,4},{6,5},{7,6},{8,7},{9,8},{10,9},{11,1... | collective-permute-start | bytes 393224 | tf_op jit(solution)/shard_map/ppermute | solution.py:25
  61.8 12.3 %collective-permute-start.5 = (f32[64,1024]{1,0:T(8,128)S(1)}, f32[64,1024]{1,0:T(8,128)S(1)}, u32[]{:S(2)}, u32[]{:S(2)}) collective-permute-start(f32[64,1024]{1,0:T(8,128)S(1)} %fusion.26), channel_id=1, source_target_pairs={{0,1},{1,2},{2,3},{3,4},{4,5},{5,6},{6,7},{7,8},{8,9},{9,10},{10,1... | collective-permute-start | bytes 786440 | tf_op jit(solution)/shard_map/ppermute | solution.py:25
  82.5 0.9 copy-start.1
  83.4 27.9 %all-to-all-start.2 = ((f32[32,48,128]{2,1,0:T(8,128)}), f32[32,48,128]{2,1,0:T(8,128)S(1)}, u32[]{:S(2)}, u32[]{:S(2)}) async-start(f32[32,48,128]{2,1,0:T(8,128)} %copy-done.1), calls=%async_computation.2 | async-start | bytes 1572864 | tf_op jit(solution)/shard_map/all_to_all | solution.py:315
  87.1 9.0 %copy-start.6 = (f32[1,1024,1024]{2,1,0:T(8,128)S(1)}, f32[1,1024,1024]{2,1,0:T(8,128)}, u32[]{:S(2)}) copy-start(f32[1,1024,1024]{2,1,0:T(8,128)} %param.10) | copy-start | bytes 12582916
  91.5 18.6 %collective-permute-start.7 = (f32[64,512]{1,0:T(8,128)S(1)}, f32[64,512]{1,0:T(8,128)S(1)}, u32[]{:S(2)}, u32[]{:S(2)}) collective-permute-start(f32[64,512]{1,0:T(8,128)S(1)} %get-tuple-element.14), channel_id=1, source_target_pairs={{1,0},{2,1},{3,2},{4,3},{5,4},{6,5},{7,6},{8,7},{9,8},{10,9},{11,1... | collective-permute-start | bytes 393224 | tf_op jit(solution)/shard_map/ppermute | solution.py:25
  93.8 15.1 %collective-permute-start.6 = (f32[64,512]{1,0:T(8,128)S(1)}, f32[64,512]{1,0:T(8,128)S(1)}, u32[]{:S(2)}, u32[]{:S(2)}) collective-permute-start(f32[64,512]{1,0:T(8,128)S(1)} %get-tuple-element.15), channel_id=1, source_target_pairs={{1,0},{2,1},{3,2},{4,3},{5,4},{6,5},{7,6},{8,7},{9,8},{10,9},{11,1... | collective-permute-start | bytes 393224 | tf_op jit(solution)/shard_map/ppermute | solution.py:25
  97.6 13.7 %collective-permute-start.8 = (f32[64,1024]{1,0:T(8,128)S(1)}, f32[64,1024]{1,0:T(8,128)S(1)}, u32[]{:S(2)}, u32[]{:S(2)}) collective-permute-start(f32[64,1024]{1,0:T(8,128)S(1)} %fusion.24), channel_id=1, source_target_pairs={{0,1},{1,2},{2,3},{3,4},{4,5},{5,6},{6,7},{7,8},{8,9},{9,10},{10,1... | collective-permute-start | bytes 786440 | tf_op jit(solution)/shard_map/ppermute | solution.py:25

commit v7 on v6

--- a/solution.py
+++ b/solution.py
@@ -108,7 +108,7 @@
 def project_last(split_ref, vectors, sums_ref, width, partner_ref, ranks_ref, outgoing_ref):
     operand = operand_of(vectors)
     slots = sums_ref.shape[0] // width
-    together = -(-slots // 4)
+    together = -(-slots // 2)
     for at in range(0, slots, together):
         end = min(at + together, slots)
         some = slice(at * width, end * width)
@@ -121,7 +121,7 @@
 
 
 def each_slot(slots, visit):
-    together = next(size for size in (7, 4, 2, 1) if slots % size == 0)
+    together = next(size for size in (14, 11, 7, 4, 2, 1) if slots % size == 0)
 
     @pl.loop(0, slots // together)
     def _(group):
@@ -180,16 +180,27 @@
             )
 
 
-def turn_kernel(weights, rectangles, width, partner_ref, ranks_ref, factors_ref, held_ref,
+def turn_kernel(weights, rectangles, width, partner_hbm, ranks_hbm, factors_ref, held_ref,
                 incoming_ref, base_ref, lower_ref, previous_ref, *rest):
+    *rest, partner_ref, ranks_ref, small_semaphore = rest
     if weights is None:
         residual_ref, *rest = rest
         buffer, semaphore, split_ref, received_ref, turned_ref = rest
     else:
         residual_ref, direction_ref, outgoing_ref, *rest = rest
         buffer, semaphore, split_ref, received_ref, turned_ref, sums_ref = rest
+    small = [
+        pltpu.make_async_copy(source, target, small_semaphore.at[index])
+        for index, (source, target) in enumerate((
+            (partner_hbm, partner_ref), (ranks_hbm, ranks_ref)
+        ))
+    ]
+    for copy in small:
+        copy.start()
     pieces = Pieces(rectangles, factors_ref, buffer, semaphore, split_ref, held_ref)
     pieces.start()
+    for copy in small:
+        copy.wait()
     unpack(width, factors_ref.shape[0] // width, partner_ref, incoming_ref, received_ref)
     turned_ref[...] = received_ref[...].T
     rows = factors_ref.shape[0]
@@ -219,7 +230,6 @@
                 )
 
 
-SMEM_SPEC = pl.BlockSpec(memory_space=pltpu.SMEM)
 VMEM_SPEC = pl.BlockSpec(memory_space=pltpu.VMEM)
 ANY_SPEC = pl.BlockSpec(memory_space=pltpu.HBM)
 
@@ -302,9 +312,13 @@
         return pl.pallas_call(
             functools.partial(turn_kernel, weights, rectangles, rank_width),
             out_shape=outs,
-            in_specs=[SMEM_SPEC, SMEM_SPEC, ANY_SPEC] + [VMEM_SPEC] * 5,
+            in_specs=[pl.BlockSpec(memory_space=pl.ANY)] * 2 + [ANY_SPEC] + [VMEM_SPEC] * 5,
             out_specs=(VMEM_SPEC,) * len(outs),
-            scratch_shapes=loading(rectangles) + received + ([] if last else [sums]),
+            scratch_shapes=loading(rectangles) + received + ([] if last else [sums]) + [
+                pltpu.SMEM((slots,), jnp.int32),
+                pltpu.SMEM((slots,), jnp.int32),
+                pltpu.SemaphoreType.DMA((2,)),
+            ],
             compiler_params=params,
             cost_estimate=cost(1 if last else 2),
             name="far" if last else "turn",

time: 118 us -> 116 us (0.983)
  Pallas kernels: 30.3 us -> 29 us
    pallas_call x3, Pallas kernels: 23.3 us -> 22 us  [turn(): pl.pallas_call(functools.partial(turn_kernel, weights, rectangles, rank_w...]
where the time goes in v7:
time: 116 us
  starting transfers between devices  43.5 us (38%)
  Pallas kernels  29 us (25%)
  matrix products  24.3 us (21%)
  waiting for transfers between devices  14.7 us (13%)
  local copies, waits for them, and re-layouts  2.3 us (2%)
  between operations  1.23 us (1%)
    ppermute x9, starting transfers between devices, from_behind(): return lax.ppermute(block, AXES, route)  29.9 us
    pallas_call x3, Pallas kernels, turn(): pl.pallas_call(functools.partial(turn_kernel, weights, rectangles, rank_w...  22 us
    ppermute x9, waiting for transfers between devices, from_behind(): return lax.ppermute(block, AXES, route)  14.7 us
    all_to_all x3, starting transfers between devices, finish(): lax.all_to_all(outgoing, AXES, split_axis=0, concat_axis=0, tiled=True)  13.6 us
    dot_general x3, matrix products, finish(): carried = lax.dot_general(vectors, neighbour_block, NN, precision=exact)  8.81 us
    dot_general x3, matrix products, finish(): partial = before - lax.dot_general(vectors, diag_block, NT, precision=exact)  8.68 us
    pallas_call x1, Pallas kernels, projected(): pl.pallas_call(functools.partial(project_kernel, groups, rank_width), out...  6.99 us
    dot_general x6, matrix products, finish(): lax.dot_general(part, tile, NT, precision=exact)  6.79 us
  transfers between devices with their start and end apart: 12, of which 4 were waited for; matrix products, arithmetic and copies ran while one was open for 23% of the time, Pallas kernels for 0%

profile of v7, /device:TPU:15, one launch (start us, length us, event | category | flops | bytes accessed | tf_op | source)
XLA Modules:
  0.0 115.9 jit_solution(14338953967449118355)
XLA Ops:
  0.6 7.0 %project.1 = f32[32,48,128]{2,1,0:T(8,128)} custom-call(s32[28]{0:T(128)} %bitcast.43, s32[28]{0:T(128)} %bitcast.47, f32[64,1024]{1,0:T(8,128)} %bitcast.40, f32[2688,1024]{1,0:T(8,128)} %bitcast.51), custom_call_target="tpu_custom_call" | custom-call | flops 1409286144 | bytes 11010048 | tf_op jit(solution)/shard_map/project/pallas_call | solution.py:288
  7.6 6.2 %all-to-all-start = ((f32[32,48,128]{2,1,0:T(8,128)}), f32[32,48,128]{2,1,0:T(8,128)S(1)}, u32[]{:S(2)}, u32[]{:S(2)}) async-start(f32[32,48,128]{2,1,0:T(8,128)} %project.1), calls=%async_computation | async-start | bytes 1572864 | tf_op jit(solution)/shard_map/all_to_all | solution.py:329
  13.9 2.6 %collective-permute-start.1 = (f32[64,512]{1,0:T(8,128)S(1)}, f32[64,512]{1,0:T(8,128)S(1)}, u32[]{:S(2)}, u32[]{:S(2)}) collective-permute-start(f32[64,512]{1,0:T(8,128)S(1)} %get-tuple-element.18), channel_id=1, source_target_pairs={{1,0},{2,1},{3,2},{4,3},{5,4},{6,5},{7,6},{8,7},{9,8},{10,9},{11,1... | collective-permute-start | bytes 393224 | tf_op jit(solution)/shard_map/ppermute | solution.py:25
  16.5 2.2 %collective-permute-start = (f32[64,512]{1,0:T(8,128)S(1)}, f32[64,512]{1,0:T(8,128)S(1)}, u32[]{:S(2)}, u32[]{:S(2)}) collective-permute-start(f32[64,512]{1,0:T(8,128)S(1)} %get-tuple-element.19), channel_id=1, source_target_pairs={{1,0},{2,1},{3,2},{4,3},{5,4},{6,5},{7,6},{8,7},{9,8},{10,9},{11,1... | collective-permute-start | bytes 393224 | tf_op jit(solution)/shard_map/ppermute | solution.py:25
  18.7 3.6 %fusion.28 = f32[64,1024]{1,0:T(8,128)S(1)} fusion(f32[1,1024,1024]{2,1,0:T(8,128)} %param.10, f32[1,64,1024]{2,1,0:T(8,128)S(1)} %copy-done), kind=kOutput, calls=%fused_computation.25 | convolution fusion | flops 402653184 | bytes 4718592 | tf_op jit(solution)/shard_map/dot_general | solution.py:335
  22.3 5.4 %collective-permute-start.2 = (f32[64,1024]{1,0:T(8,128)S(1)}, f32[64,1024]{1,0:T(8,128)S(1)}, u32[]{:S(2)}, u32[]{:S(2)}) collective-permute-start(f32[64,1024]{1,0:T(8,128)S(1)} %fusion.28), channel_id=1, source_target_pairs={{0,1},{1,2},{2,3},{3,4},{4,5},{5,6},{6,7},{7,8},{8,9},{9,10},{10,1... | collective-permute-start | bytes 786440 | tf_op jit(solution)/shard_map/ppermute | solution.py:25
  27.8 2.2 %fusion.21 = f32[64,1024]{1,0:T(8,128)S(1)} fusion(f32[1,1024,1024]{2,1,0:T(8,128)S(1)} %copy-done.7, f32[1,64,1024]{2,1,0:T(8,128)S(1)} %copy-done.9, f32[1,64,1024]{2,1,0:T(8,128)S(1)} %copy-done), kind=kOutput, calls=%fused_computation.19 | convolution fusion | flops 402718720 | bytes 4980736 | tf_op jit(solution)/shard_map/dot_general | solution.py:337
  30.0 1.3 %slice.4.held_ref = f32[512,512]{1,0:T(8,128)S(1)} slice(f32[2688,1024]{1,0:T(8,128)} %bitcast.52), slice={[0:512], [0:512]} | slice | bytes 2097152 | tf_op jit(solution)/shard_map/slice | solution.py:252
  31.3 4.5 %collective-permute-done = f32[64,512]{1,0:T(8,128)S(1)} collective-permute-done((f32[64,512]{1,0:T(8,128)S(1)}, f32[64,512]{1,0:T(8,128)S(1)}, u32[]{:S(2)}, u32[]{:S(2)}) %collective-permute-start) | collective-permute-done | bytes 131104 | tf_op jit(solution)/shard_map/ppermute | solution.py:25
  35.8 1.1 fusion.18
  36.9 1.1 fusion.10
  38.1 8.8 %turn.2 = (f32[64,1024]{1,0:T(8,128)S(1)}, f32[64,1024]{1,0:T(8,128)S(1)}, f32[32,48,128]{2,1,0:T(8,128)}) custom-call(s32[28]{0:T(128)S(1)} %bitcast.44, s32[28]{0:T(128)S(1)} %bitcast.48, f32[2688,1024]{1,0:T(8,128)} %bitcast.53, f32[512,512]{1,0:T(8,128)S(1)} %slice.4.held_ref, f32[32,48,128]{2,1,0:T(8,128)S(1)} %all-to-all-done.incoming_ref, ...), custom_call_target="tpu_custom_call" | custom-call | flops 2818572288 | bytes 11010048 | tf_op jit(solution)/shard_map/turn/pallas_call | solution.py:312
  46.9 3.7 %all-to-all-start.1 = ((f32[32,48,128]{2,1,0:T(8,128)}), f32[32,48,128]{2,1,0:T(8,128)S(1)}, u32[]{:S(2)}, u32[]{:S(2)}) async-start(f32[32,48,128]{2,1,0:T(8,128)} %get-tuple-element.9), calls=%async_computation.1 | async-start | bytes 1572864 | tf_op jit(solution)/shard_map/all_to_all | solution.py:329
  50.7 2.7 %collective-permute-start.3 = (f32[64,512]{1,0:T(8,128)S(1)}, f32[64,512]{1,0:T(8,128)S(1)}, u32[]{:S(2)}, u32[]{:S(2)}) collective-permute-start(f32[64,512]{1,0:T(8,128)S(1)} %get-tuple-element.17), channel_id=1, source_target_pairs={{1,0},{2,1},{3,2},{4,3},{5,4},{6,5},{7,6},{8,7},{9,8},{10,9},{11,1... | collective-permute-start | bytes 393224 | tf_op jit(solution)/shard_map/ppermute | solution.py:25
  53.4 3.6 %fusion.26 = f32[64,1024]{1,0:T(8,128)S(1)} fusion(f32[64,1024]{1,0:T(8,128)S(1)} %get-tuple-element.8.previous_ref, f32[1,1024,1024]{2,1,0:T(8,128)} %param.10), kind=kOutput, calls=%fused_computation.23 | convolution fusion | flops 402653184 | bytes 4718592 | tf_op jit(solution)/shard_map/dot_general | solution.py:335
  57.0 2.2 %fusion.2 = f32[64,1024]{1,0:T(8,128)S(1)} fusion(f32[64,1024]{1,0:T(8,128)S(1)} %get-tuple-element.8.previous_ref, f32[1,1024,1024]{2,1,0:T(8,128)S(1)} %copy-done.8), kind=kOutput, calls=%fused_computation.2 | convolution fusion | flops 402653184 | bytes 4718592 | tf_op jit(solution)/shard_map/dot_general | solution.py:337
  59.2 2.2 %collective-permute-start.4 = (f32[64,512]{1,0:T(8,128)S(1)}, f32[64,512]{1,0:T(8,128)S(1)}, u32[]{:S(2)}, u32[]{:S(2)}) collective-permute-start(f32[64,512]{1,0:T(8,128)S(1)} %get-tuple-element.16), channel_id=1, source_target_pairs={{1,0},{2,1},{3,2},{4,3},{5,4},{6,5},{7,6},{8,7},{9,8},{10,9},{11,1... | collective-permute-start | bytes 393224 | tf_op jit(solution)/shard_map/ppermute | solution.py:25
  61.4 5.2 %collective-permute-start.5 = (f32[64,1024]{1,0:T(8,128)S(1)}, f32[64,1024]{1,0:T(8,128)S(1)}, u32[]{:S(2)}, u32[]{:S(2)}) collective-permute-start(f32[64,1024]{1,0:T(8,128)S(1)} %fusion.26), channel_id=1, source_target_pairs={{0,1},{1,2},{2,3},{3,4},{4,5},{5,6},{6,7},{7,8},{8,9},{9,10},{10,1... | collective-permute-start | bytes 786440 | tf_op jit(solution)/shard_map/ppermute | solution.py:25
  66.6 4.5 %collective-permute-done.3 = f32[64,512]{1,0:T(8,128)S(1)} collective-permute-done((f32[64,512]{1,0:T(8,128)S(1)}, f32[64,512]{1,0:T(8,128)S(1)}, u32[]{:S(2)}, u32[]{:S(2)}) %collective-permute-start.3) | collective-permute-done | bytes 131104 | tf_op jit(solution)/shard_map/ppermute | solution.py:25
  71.1 1.1 fusion.14
  72.5 1.1 fusion.8
  73.7 7.9 %turn.3 = (f32[64,1024]{1,0:T(8,128)S(1)}, f32[64,1024]{1,0:T(8,128)S(1)}, f32[32,48,128]{2,1,0:T(8,128)S(1)}) custom-call(s32[28]{0:T(128)S(1)} %bitcast.45, s32[28]{0:T(128)S(1)} %bitcast.49, f32[2688,1024]{1,0:T(8,128)} %bitcast.54, f32[512,512]{1,0:T(8,128)S(1)} %slice.4.held_ref, f32[32,48,128]{2,1,0:T(8,128)S(1)} %all-to-all-done.1.incoming_ref, ...), custom_call_target="tpu_custom_call" | custom-call | flops 2818572288 | bytes 11010048 | tf_op jit(solution)/shard_map/turn/pallas_call | solution.py:312
  82.5 3.7 %all-to-all-start.2 = ((f32[32,48,128]{2,1,0:T(8,128)}), f32[32,48,128]{2,1,0:T(8,128)S(1)}, u32[]{:S(2)}, u32[]{:S(2)}) async-start(f32[32,48,128]{2,1,0:T(8,128)} %copy-done.1), calls=%async_computation.2 | async-start | bytes 1572864 | tf_op jit(solution)/shard_map/all_to_all | solution.py:329
  86.2 4.4 %fusion = f32[64,1024]{1,0:T(8,128)S(1)} fusion(f32[64,1024]{1,0:T(8,128)S(1)} %get-tuple-element.11.previous_ref, f32[1,1024,1024]{2,1,0:T(8,128)} %param.9), kind=kOutput, calls=%fused_computation | convolution fusion | flops 402653184 | bytes 4718592 | tf_op jit(solution)/shard_map/dot_general | solution.py:337
  90.7 2.3 %collective-permute-start.7 = (f32[64,512]{1,0:T(8,128)S(1)}, f32[64,512]{1,0:T(8,128)S(1)}, u32[]{:S(2)}, u32[]{:S(2)}) collective-permute-start(f32[64,512]{1,0:T(8,128)S(1)} %get-tuple-element.14), channel_id=1, source_target_pairs={{1,0},{2,1},{3,2},{4,3},{5,4},{6,5},{7,6},{8,7},{9,8},{10,9},{11,1... | collective-permute-start | bytes 393224 | tf_op jit(solution)/shard_map/ppermute | solution.py:25
  93.0 2.2 %collective-permute-start.6 = (f32[64,512]{1,0:T(8,128)S(1)}, f32[64,512]{1,0:T(8,128)S(1)}, u32[]{:S(2)}, u32[]{:S(2)}) collective-permute-start(f32[64,512]{1,0:T(8,128)S(1)} %get-tuple-element.15), channel_id=1, source_target_pairs={{1,0},{2,1},{3,2},{4,3},{5,4},{6,5},{7,6},{8,7},{9,8},{10,9},{11,1... | collective-permute-start | bytes 393224 | tf_op jit(solution)/shard_map/ppermute | solution.py:25
  95.2 1.6 %fusion.24 = f32[64,1024]{1,0:T(8,128)S(1)} fusion(f32[64,1024]{1,0:T(8,128)S(1)} %get-tuple-element.11.previous_ref, f32[1,1024,1024]{2,1,0:T(8,128)S(1)} %copy-done.6), kind=kOutput, calls=%fused_computation.21 | convolution fusion | flops 402653184 | bytes 4718592 | tf_op jit(solution)/shard_map/dot_general | solution.py:335
  96.8 5.2 %collective-permute-start.8 = (f32[64,1024]{1,0:T(8,128)S(1)}, f32[64,1024]{1,0:T(8,128)S(1)}, u32[]{:S(2)}, u32[]{:S(2)}) collective-permute-start(f32[64,1024]{1,0:T(8,128)S(1)} %fusion.24), channel_id=1, source_target_pairs={{0,1},{1,2},{2,3},{3,4},{4,5},{5,6},{6,7},{7,8},{8,9},{9,10},{10,1... | collective-permute-start | bytes 786440 | tf_op jit(solution)/shard_map/ppermute | solution.py:25
  102.7 5.4 %collective-permute-done.6 = f32[64,512]{1,0:T(8,128)S(1)} collective-permute-done((f32[64,512]{1,0:T(8,128)S(1)}, f32[64,512]{1,0:T(8,128)S(1)}, u32[]{:S(2)}, u32[]{:S(2)}) %collective-permute-start.6) | collective-permute-done | bytes 131104 | tf_op jit(solution)/shard_map/ppermute | solution.py:25
  108.1 1.1 fusion.12
  109.3 1.1 fusion.6
  110.5 5.2 %far.1 = f32[64,1024]{1,0:T(8,128)} custom-call(s32[28]{0:T(128)S(1)} %bitcast.46, s32[28]{0:T(128)S(1)} %bitcast.50, f32[2688,1024]{1,0:T(8,128)} %bitcast.55, f32[512,512]{1,0:T(8,128)S(1)} %slice.4.held_ref, f32[32,48,128]{2,1,0:T(8,128)S(1)} %all-to-all-done.2.incoming_ref, f32[64,1024]{1,0:T(8,128)S(1)} %sub.35.base_ref, ...), custom_call_target="tpu_custom_call" | custom-call | flops 1409286144 | bytes 11010048 | tf_op jit(solution)/shard_map/far/pallas_call | solution.py:312
  (40 shorter events, 2.2 us)
Async XLA Ops:
  0.6 13.3 %copy-start = (f32[1,64,1024]{2,1,0:T(8,128)S(1)}, f32[1,64,1024]{2,1,0:T(8,128)}, u32[]{:S(2)}) copy-start(f32[1,64,1024]{2,1,0:T(8,128)} %param.8) | copy-start | bytes 786436
  7.6 20.2 %copy-start.9 = (f32[1,64,1024]{2,1,0:T(8,128)S(1)}, f32[1,64,1024]{2,1,0:T(8,128)}, u32[]{:S(2)}) copy-start(f32[1,64,1024]{2,1,0:T(8,128)} %param.7) | copy-start | bytes 786436
  7.6 30.5 %all-to-all-start = ((f32[32,48,128]{2,1,0:T(8,128)}), f32[32,48,128]{2,1,0:T(8,128)S(1)}, u32[]{:S(2)}, u32[]{:S(2)}) async-start(f32[32,48,128]{2,1,0:T(8,128)} %project.1), calls=%async_computation | async-start | bytes 1572864 | tf_op jit(solution)/shard_map/all_to_all | solution.py:329
  13.9 13.9 %copy-start.7 = (f32[1,1024,1024]{2,1,0:T(8,128)S(1)}, f32[1,1024,1024]{2,1,0:T(8,128)}, u32[]{:S(2)}) copy-start(f32[1,1024,1024]{2,1,0:T(8,128)} %param.9) | copy-start | bytes 12582916
  13.9 23.0 %collective-permute-start.1 = (f32[64,512]{1,0:T(8,128)S(1)}, f32[64,512]{1,0:T(8,128)S(1)}, u32[]{:S(2)}, u32[]{:S(2)}) collective-permute-start(f32[64,512]{1,0:T(8,128)S(1)} %get-tuple-element.18), channel_id=1, source_target_pairs={{1,0},{2,1},{3,2},{4,3},{5,4},{6,5},{7,6},{8,7},{9,8},{10,9},{11,1... | collective-permute-start | bytes 393224 | tf_op jit(solution)/shard_map/ppermute | solution.py:25
  16.5 19.3 %collective-permute-start = (f32[64,512]{1,0:T(8,128)S(1)}, f32[64,512]{1,0:T(8,128)S(1)}, u32[]{:S(2)}, u32[]{:S(2)}) collective-permute-start(f32[64,512]{1,0:T(8,128)S(1)} %get-tuple-element.19), channel_id=1, source_target_pairs={{1,0},{2,1},{3,2},{4,3},{5,4},{6,5},{7,6},{8,7},{9,8},{10,9},{11,1... | collective-permute-start | bytes 393224 | tf_op jit(solution)/shard_map/ppermute | solution.py:25
  22.3 13.5 %copy-start.4 = (f32[1,1024,1024]{2,1,0:T(8,128)S(1)}, f32[1,1024,1024]{2,1,0:T(8,128)}, u32[]{:S(2)}) copy-start(f32[1,1024,1024]{2,1,0:T(8,128)} %param.10) | copy-start | bytes 12582916
  22.3 15.8 %collective-permute-start.2 = (f32[64,1024]{1,0:T(8,128)S(1)}, f32[64,1024]{1,0:T(8,128)S(1)}, u32[]{:S(2)}, u32[]{:S(2)}) collective-permute-start(f32[64,1024]{1,0:T(8,128)S(1)} %fusion.28), channel_id=1, source_target_pairs={{0,1},{1,2},{2,3},{3,4},{4,5},{5,6},{6,7},{7,8},{8,9},{9,10},{10,1... | collective-permute-start | bytes 786440 | tf_op jit(solution)/shard_map/ppermute | solution.py:25
  30.0 8.2 %copy-start.2 = (s32[1,28]{1,0:T(1,128)S(1)}, s32[1,28]{1,0:T(1,128)}, u32[]{:S(2)}) copy-start(s32[1,28]{1,0:T(1,128)} %param.12) | copy-start | bytes 340
  30.0 8.2 %copy-start.3 = (s32[1,28]{1,0:T(1,128)S(1)}, s32[1,28]{1,0:T(1,128)}, u32[]{:S(2)}) copy-start(s32[1,28]{1,0:T(1,128)} %param.13) | copy-start | bytes 340
  46.9 26.7 %all-to-all-start.1 = ((f32[32,48,128]{2,1,0:T(8,128)}), f32[32,48,128]{2,1,0:T(8,128)S(1)}, u32[]{:S(2)}, u32[]{:S(2)}) async-start(f32[32,48,128]{2,1,0:T(8,128)} %get-tuple-element.9), calls=%async_computation.1 | async-start | bytes 1572864 | tf_op jit(solution)/shard_map/all_to_all | solution.py:329
  50.6 6.4 %copy-start.8 = (f32[1,1024,1024]{2,1,0:T(8,128)S(1)}, f32[1,1024,1024]{2,1,0:T(8,128)}, u32[]{:S(2)}) copy-start(f32[1,1024,1024]{2,1,0:T(8,128)} %param.9) | copy-start | bytes 12582916
  50.7 20.4 %copy-start.5 = (f32[1,1024,1024]{2,1,0:T(8,128)S(1)}, f32[1,1024,1024]{2,1,0:T(8,128)}, u32[]{:S(2)}) copy-start(f32[1,1024,1024]{2,1,0:T(8,128)} %param.10) | copy-start | bytes 12582916
  50.7 20.4 %collective-permute-start.3 = (f32[64,512]{1,0:T(8,128)S(1)}, f32[64,512]{1,0:T(8,128)S(1)}, u32[]{:S(2)}, u32[]{:S(2)}) collective-permute-start(f32[64,512]{1,0:T(8,128)S(1)} %get-tuple-element.17), channel_id=1, source_target_pairs={{1,0},{2,1},{3,2},{4,3},{5,4},{6,5},{7,6},{8,7},{9,8},{10,9},{11,1... | collective-permute-start | bytes 393224 | tf_op jit(solution)/shard_map/ppermute | solution.py:25
  59.2 13.3 %collective-permute-start.4 = (f32[64,512]{1,0:T(8,128)S(1)}, f32[64,512]{1,0:T(8,128)S(1)}, u32[]{:S(2)}, u32[]{:S(2)}) collective-permute-start(f32[64,512]{1,0:T(8,128)S(1)} %get-tuple-element.16), channel_id=1, source_target_pairs={{1,0},{2,1},{3,2},{4,3},{5,4},{6,5},{7,6},{8,7},{9,8},{10,9},{11,1... | collective-permute-start | bytes 393224 | tf_op jit(solution)/shard_map/ppermute | solution.py:25
  61.4 12.3 %collective-permute-start.5 = (f32[64,1024]{1,0:T(8,128)S(1)}, f32[64,1024]{1,0:T(8,128)S(1)}, u32[]{:S(2)}, u32[]{:S(2)}) collective-permute-start(f32[64,1024]{1,0:T(8,128)S(1)} %fusion.26), channel_id=1, source_target_pairs={{0,1},{1,2},{2,3},{3,4},{4,5},{5,6},{6,7},{7,8},{8,9},{9,10},{10,1... | collective-permute-start | bytes 786440 | tf_op jit(solution)/shard_map/ppermute | solution.py:25
  81.7 0.9 copy-start.1
  82.5 27.9 %all-to-all-start.2 = ((f32[32,48,128]{2,1,0:T(8,128)}), f32[32,48,128]{2,1,0:T(8,128)S(1)}, u32[]{:S(2)}, u32[]{:S(2)}) async-start(f32[32,48,128]{2,1,0:T(8,128)} %copy-done.1), calls=%async_computation.2 | async-start | bytes 1572864 | tf_op jit(solution)/shard_map/all_to_all | solution.py:329
  86.2 9.0 %copy-start.6 = (f32[1,1024,1024]{2,1,0:T(8,128)S(1)}, f32[1,1024,1024]{2,1,0:T(8,128)}, u32[]{:S(2)}) copy-start(f32[1,1024,1024]{2,1,0:T(8,128)} %param.10) | copy-start | bytes 12582916
  90.7 18.6 %collective-permute-start.7 = (f32[64,512]{1,0:T(8,128)S(1)}, f32[64,512]{1,0:T(8,128)S(1)}, u32[]{:S(2)}, u32[]{:S(2)}) collective-permute-start(f32[64,512]{1,0:T(8,128)S(1)} %get-tuple-element.14), channel_id=1, source_target_pairs={{1,0},{2,1},{3,2},{4,3},{5,4},{6,5},{7,6},{8,7},{9,8},{10,9},{11,1... | collective-permute-start | bytes 393224 | tf_op jit(solution)/shard_map/ppermute | solution.py:25
  93.0 15.1 %collective-permute-start.6 = (f32[64,512]{1,0:T(8,128)S(1)}, f32[64,512]{1,0:T(8,128)S(1)}, u32[]{:S(2)}, u32[]{:S(2)}) collective-permute-start(f32[64,512]{1,0:T(8,128)S(1)} %get-tuple-element.15), channel_id=1, source_target_pairs={{1,0},{2,1},{3,2},{4,3},{5,4},{6,5},{7,6},{8,7},{9,8},{10,9},{11,1... | collective-permute-start | bytes 393224 | tf_op jit(solution)/shard_map/ppermute | solution.py:25
  96.8 13.7 %collective-permute-start.8 = (f32[64,1024]{1,0:T(8,128)S(1)}, f32[64,1024]{1,0:T(8,128)S(1)}, u32[]{:S(2)}, u32[]{:S(2)}) collective-permute-start(f32[64,1024]{1,0:T(8,128)S(1)} %fusion.24), channel_id=1, source_target_pairs={{0,1},{1,2},{2,3},{3,4},{4,5},{5,6},{6,7},{7,8},{8,9},{9,10},{10,1... | collective-permute-start | bytes 786440 | tf_op jit(solution)/shard_map/ppermute | solution.py:25
